TPU v7x, 32 devices: a whole 2x2x4 slice. The times are simulated.
32 devices in a mesh: fsdp: 4 (over y, core), ctx: 4 (over z), tp: 2 (over x).
Axes of the slice: x: 2, y: 2, z: 4, core: 2. Of those that a mesh axis runs over, the one named last changes fastest.
Arguments:
- layer_input: bfloat16 [4, 1024, 1536], P('fsdp', 'ctx'), may hold values from -6 to 6
- segments: int32 [4, 1024], P('fsdp', 'ctx'), may hold values from 0 to 5, as said below
- positions: int32 [4, 1024], P('fsdp', 'ctx'), may hold values from 0 to 1023, as said below
- attn_gain: bfloat16 [1536], P(('fsdp', 'ctx')), may hold values from 0.099609375 to 1.8984375
- query_proj: bfloat16 [1536, 1536], P(('fsdp', 'ctx'), 'tp'), may hold values from -0.21875 to 0.21875
- key_proj: bfloat16 [1536, 768], P(('fsdp', 'ctx'), 'tp'), may hold values from -0.21875 to 0.21875
- value_proj: bfloat16 [1536, 768], P(('fsdp', 'ctx'), 'tp'), may hold values from -0.15625 to 0.15625
- out_proj: bfloat16 [1536, 1536], P('tp', ('fsdp', 'ctx')), may hold values from -1.25 to 1.25
- mlp_gain: bfloat16 [1536], P(('fsdp', 'ctx')), may hold values from 0.099609375 to 1.8984375
- gate_proj: bfloat16 [1536, 4096], P(('fsdp', 'ctx'), 'tp'), may hold values from -0.15625 to 0.15625
- up_proj: bfloat16 [1536, 4096], P(('fsdp', 'ctx'), 'tp'), may hold values from -0.15625 to 0.15625
- down_proj: bfloat16 [4096, 1536], P('tp', ('fsdp', 'ctx')), may hold values from -0.09375 to 0.09375
- out_grad: bfloat16 [4, 1024, 1536], P('fsdp', 'ctx'), may hold values from -6 to 6
Outputs:
- layer_output: bfloat16 [4, 1024, 1536], P('fsdp', 'ctx')
- input_grad: bfloat16 [4, 1024, 1536], P('fsdp', 'ctx')
- attn_gain_grad: float32 [1536], P(('fsdp', 'ctx'))
- query_proj_grad: float32 [1536, 1536], P(('fsdp', 'ctx'), 'tp')
- key_proj_grad: float32 [1536, 768], P(('fsdp', 'ctx'), 'tp')
- value_proj_grad: float32 [1536, 768], P(('fsdp', 'ctx'), 'tp')
- out_proj_grad: float32 [1536, 1536], P('tp', ('fsdp', 'ctx'))
- mlp_gain_grad: float32 [1536], P(('fsdp', 'ctx'))
- gate_proj_grad: float32 [1536, 4096], P(('fsdp', 'ctx'), 'tp')
- up_proj_grad: float32 [1536, 4096], P(('fsdp', 'ctx'), 'tp')
- down_proj_grad: float32 [4096, 1536], P('tp', ('fsdp', 'ctx'))
Inputs may be any that keep to these rules, and one draw needn't show every extreme that they name: `segments`: numbers the documents of each sequence 0, 1, 2 and so on, never falling; every document has 200 to 2000 tokens except that the last of a sequence may be cut short. `positions`: each token's offset from the first token of its document.
All inputs are finite; a program needn't handle non-finite values.
Results may differ from a plain program's by a relative error of at most 0.018.
Values may be sent and summed in bfloat16 or wider, within the bound.
A program may use at most 192 MiB of HBM per device.

v0:
```python
import jax
import jax.numpy as jnp
from jax import lax
from jax.sharding import PartitionSpec as P

HQ = 16
HK = 8
DH = 96


EPS = 1e-05
THETA = 100000.0
NEGATIVE = -1e30


def rotary_tables(positions):
    half_dim = DH // 2
    freq_index = jnp.arange(half_dim, dtype=jnp.float32)
    inverse = THETA ** (-2.0 * freq_index / DH)
    angles = positions.astype(jnp.float32)[..., None] * inverse
    return (jnp.cos(angles), jnp.sin(angles))


def rotate(field_in, cos_table, sin_table):
    half_dim = field_in.shape[-1] // 2
    front_half = field_in[..., :half_dim]
    back_half = field_in[..., half_dim:]
    return jnp.concatenate(
        [
            front_half * cos_table - back_half * sin_table,
            back_half * cos_table + front_half * sin_table,
        ],
        axis=-1,
    )


def unrotate(field_in, cos_table, sin_table):
    half_dim = field_in.shape[-1] // 2
    front_half = field_in[..., :half_dim]
    back_half = field_in[..., half_dim:]
    return jnp.concatenate(
        [
            front_half * cos_table + back_half * sin_table,
            back_half * cos_table - front_half * sin_table,
        ],
        axis=-1,
    )


def inverse_rms(values):
    return lax.rsqrt(jnp.mean(values * values, axis=-1, keepdims=True) + EPS)


def contract(left, right, left_dim, right_dim):
    return lax.dot_general(
        left, right, (((left_dim,), (right_dim,)), ((), ())), preferred_element_type=jnp.float32
    )


def norm_back(upstream, inner, values, scale_rows):
    cubed = scale_rows * scale_rows * scale_rows
    return (
        upstream
        + scale_rows * inner
        - values * cubed * jnp.mean(inner * values, axis=-1, keepdims=True)
    )


def to_blocks(matrix, seq_count, local_kv, groups):
    span = matrix.shape[0] // seq_count
    shaped = matrix.reshape(seq_count, span, local_kv, groups, DH).transpose(0, 2, 1, 3, 4)
    return shaped.reshape(seq_count * local_kv, span * groups, DH)


def from_blocks(blocks, seq_count, local_kv, groups):
    span = blocks.shape[1] // groups
    shaped = blocks.reshape(seq_count, local_kv, span, groups, DH).transpose(0, 2, 1, 3, 4)
    return shaped.reshape(seq_count * span, local_kv * groups * DH)


def seq_items(matrix, local_kv):
    seq_count = matrix.shape[0]
    length = matrix.shape[1]
    return (
        matrix.reshape(seq_count, length, local_kv, DH)
        .transpose(0, 2, 1, 3)
        .reshape(seq_count * local_kv, length, DH)
    )


def from_items(items, seq_count, local_kv):
    length = items.shape[1]
    return (
        items.reshape(seq_count, local_kv, length, DH)
        .transpose(0, 2, 1, 3)
        .reshape(seq_count, length, local_kv * DH)
    )


def on_device(
    layer_input,
    segments,
    positions,
    attn_gain,
    query_proj,
    key_proj,
    value_proj,
    out_proj,
    mlp_gain,
    gate_proj,
    up_proj,
    down_proj,
    out_grad,
):
    attn_full = (
        lax.all_gather(attn_gain, ("fsdp", "ctx"), axis=0, tiled=True),
        lax.all_gather(query_proj, ("fsdp", "ctx"), axis=0, tiled=True),
        lax.all_gather(key_proj, ("fsdp", "ctx"), axis=0, tiled=True),
        lax.all_gather(value_proj, ("fsdp", "ctx"), axis=0, tiled=True),
        lax.all_gather(out_proj, ("fsdp", "ctx"), axis=1, tiled=True),
    )
    mlp_full = (
        lax.all_gather(mlp_gain, ("fsdp", "ctx"), axis=0, tiled=True),
        lax.all_gather(gate_proj, ("fsdp", "ctx"), axis=0, tiled=True),
        lax.all_gather(up_proj, ("fsdp", "ctx"), axis=0, tiled=True),
        lax.all_gather(down_proj, ("fsdp", "ctx"), axis=1, tiled=True),
    )
    seq_count, span, width = layer_input.shape
    total_rows = seq_count * span
    groups = HQ // HK
    local_kv = key_proj.shape[1] // DH
    score_scale = DH ** (-0.5)
    inputs = layer_input.reshape(total_rows, width).astype(jnp.float32)
    scale_attn = inverse_rms(inputs)
    normed_attn = (inputs * scale_attn * attn_full[0].astype(jnp.float32)).astype(jnp.bfloat16)
    query_pre = jnp.dot(normed_attn, attn_full[1], preferred_element_type=jnp.float32)
    key_pre = jnp.dot(normed_attn, attn_full[2], preferred_element_type=jnp.float32)
    value_pre = jnp.dot(normed_attn, attn_full[3], preferred_element_type=jnp.float32)
    cos_table, sin_table = rotary_tables(positions.reshape(total_rows))
    cos_table = cos_table[:, None, :]
    sin_table = sin_table[:, None, :]
    query_rot = (
        rotate(query_pre.reshape(total_rows, -1, DH), cos_table, sin_table)
        .astype(jnp.bfloat16)
        .reshape(total_rows, -1)
    )
    key_rot = (
        rotate(key_pre.reshape(total_rows, local_kv, DH), cos_table, sin_table)
        .astype(jnp.bfloat16)
        .reshape(seq_count, span, local_kv * DH)
    )
    value_low = value_pre.astype(jnp.bfloat16).reshape(seq_count, span, local_kv * DH)
    key_all, value_all, segment_all = (
        lax.all_gather(key_rot, "ctx", axis=1, tiled=True),
        lax.all_gather(value_low, "ctx", axis=1, tiled=True),
        lax.all_gather(segments.astype(jnp.bfloat16), "ctx", axis=1, tiled=True),
    )
    key_items = seq_items(key_all, local_kv)
    value_items = seq_items(value_all, local_kv)
    key_segments = jnp.repeat(segment_all.astype(jnp.int32), local_kv, axis=0)
    query_segments = jnp.repeat(jnp.repeat(segments, groups, axis=1), local_kv, axis=0)
    query_index = jnp.repeat(
        lax.axis_index("ctx") * span + jnp.arange(span, dtype=jnp.int32), groups
    )
    key_index = jnp.arange(key_all.shape[1], dtype=jnp.int32)
    query_blocks = to_blocks(query_rot, seq_count, local_kv, groups)

    def block_scores(block_query, block_keys, key_segment, query_segment):
        scores = (
            jnp.einsum("qd,kd->qk", block_query, block_keys, preferred_element_type=jnp.float32)
            * score_scale
        )
        allowed = (query_segment[:, None] == key_segment[None, :]) & (
            query_index[:, None] >= key_index[None, :]
        )
        return (scores, allowed)

    def forward_block(block_item):
        block_query, block_keys, block_values, key_segment, query_segment = block_item
        scores, allowed = block_scores(block_query, block_keys, key_segment, query_segment)
        scores = jnp.where(allowed, scores, NEGATIVE)
        row_max = jnp.max(scores, axis=1, keepdims=True)
        exp_scores = jnp.exp(scores - row_max)
        row_total = jnp.sum(exp_scores, axis=1, keepdims=True)
        attn_probs = (exp_scores / row_total).astype(jnp.bfloat16)
        mixed_block = jnp.dot(attn_probs, block_values, preferred_element_type=jnp.float32)
        return (mixed_block.astype(jnp.bfloat16), (row_max + jnp.log(row_total))[:, 0])

    mixed_blocks, row_lse = lax.map(
        forward_block, (query_blocks, key_items, value_items, key_segments, query_segments)
    )
    mixed_rows = from_blocks(mixed_blocks, seq_count, local_kv, groups)
    attended = lax.psum(jnp.dot(mixed_rows, attn_full[4], preferred_element_type=jnp.float32), "tp")
    residual = inputs + attended
    scale_mlp = inverse_rms(residual)
    normed_mlp = (residual * scale_mlp * mlp_full[0].astype(jnp.float32)).astype(jnp.bfloat16)
    gate_pre = jnp.dot(normed_mlp, mlp_full[1], preferred_element_type=jnp.float32)
    up_pre = jnp.dot(normed_mlp, mlp_full[2], preferred_element_type=jnp.float32)
    activated = jax.nn.silu(gate_pre)
    hidden = (activated * up_pre).astype(jnp.bfloat16)
    mlp_out = lax.psum(
        jnp.dot(hidden, mlp_full[3], preferred_element_type=jnp.float32).astype(jnp.bfloat16), "tp"
    ).astype(jnp.float32)
    layer_output = (residual + mlp_out).astype(jnp.bfloat16).reshape(seq_count, span, width)
    mlp_back = (
        lax.all_gather(mlp_gain, ("fsdp", "ctx"), axis=0, tiled=True),
        lax.all_gather(gate_proj, ("fsdp", "ctx"), axis=0, tiled=True),
        lax.all_gather(up_proj, ("fsdp", "ctx"), axis=0, tiled=True),
        lax.all_gather(down_proj, ("fsdp", "ctx"), axis=1, tiled=True),
    )
    upstream = out_grad.reshape(total_rows, width).astype(jnp.float32)
    upstream_low = upstream.astype(jnp.bfloat16)
    hidden_grad = contract(upstream_low, mlp_back[3], 1, 1)
    down_weight_grad = contract(hidden, upstream_low, 0, 0)
    sigmoid_gate = jax.nn.sigmoid(gate_pre)
    gate_grad = (
        hidden_grad * up_pre * sigmoid_gate * (1.0 + gate_pre * (1.0 - sigmoid_gate))
    ).astype(jnp.bfloat16)
    up_grad = (hidden_grad * activated).astype(jnp.bfloat16)
    normed_mlp_grad = lax.psum(
        contract(gate_grad, mlp_back[1], 1, 1) + contract(up_grad, mlp_back[2], 1, 1), "tp"
    )
    mlp_gain_term = jnp.sum(normed_mlp_grad * residual * scale_mlp, axis=0)
    residual_grad = norm_back(
        upstream, normed_mlp_grad * mlp_back[0].astype(jnp.float32), residual, scale_mlp
    )
    gate_weight_grad = contract(normed_mlp, gate_grad, 0, 0)
    up_weight_grad = contract(normed_mlp, up_grad, 0, 0)
    mlp_grads = (
        lax.psum_scatter(mlp_gain_term, ("fsdp", "ctx"), scatter_dimension=0, tiled=True),
        lax.psum_scatter(gate_weight_grad, ("fsdp", "ctx"), scatter_dimension=0, tiled=True),
        lax.psum_scatter(up_weight_grad, ("fsdp", "ctx"), scatter_dimension=0, tiled=True),
        lax.psum_scatter(down_weight_grad, ("fsdp", "ctx"), scatter_dimension=1, tiled=True),
    )
    attn_back = (
        lax.all_gather(attn_gain, ("fsdp", "ctx"), axis=0, tiled=True),
        lax.all_gather(query_proj, ("fsdp", "ctx"), axis=0, tiled=True),
        lax.all_gather(key_proj, ("fsdp", "ctx"), axis=0, tiled=True),
        lax.all_gather(value_proj, ("fsdp", "ctx"), axis=0, tiled=True),
        lax.all_gather(out_proj, ("fsdp", "ctx"), axis=1, tiled=True),
    )
    residual_low = residual_grad.astype(jnp.bfloat16)
    out_weight_grad = contract(mixed_rows, residual_low, 0, 0)
    mixed_grad = contract(residual_low, attn_back[4], 1, 1).astype(jnp.bfloat16)
    grad_blocks = to_blocks(mixed_grad, seq_count, local_kv, groups)

    def backward_block(block_item):
        block_query, block_keys, block_values, key_segment, query_segment, block_lse, block_grad = (
            block_item
        )
        scores, allowed = block_scores(block_query, block_keys, key_segment, query_segment)
        attn_probs = jnp.where(allowed, jnp.exp(scores - block_lse[:, None]), 0.0)
        prob_grad = jnp.einsum(
            "qd,kd->qk", block_grad, block_values, preferred_element_type=jnp.float32
        )
        row_delta = jnp.sum(prob_grad * attn_probs, axis=1, keepdims=True)
        score_grad = (attn_probs * (prob_grad - row_delta)).astype(jnp.bfloat16)
        value_grad = jnp.einsum(
            "qk,qd->kd",
            attn_probs.astype(jnp.bfloat16),
            block_grad,
            preferred_element_type=jnp.float32,
        )
        key_grad = (
            jnp.einsum("qk,qd->kd", score_grad, block_query, preferred_element_type=jnp.float32)
            * score_scale
        )
        query_grad = (
            jnp.dot(score_grad, block_keys, preferred_element_type=jnp.float32) * score_scale
        )
        return (query_grad, key_grad, value_grad)

    query_grads, key_grads, value_grads = lax.map(
        backward_block,
        (query_blocks, key_items, value_items, key_segments, query_segments, row_lse, grad_blocks),
    )
    key_back, value_back = (
        lax.psum_scatter(
            from_items(key_grads, seq_count, local_kv).astype(jnp.bfloat16),
            "ctx",
            scatter_dimension=1,
            tiled=True,
        ).astype(jnp.float32),
        lax.psum_scatter(
            from_items(value_grads, seq_count, local_kv).astype(jnp.bfloat16),
            "ctx",
            scatter_dimension=1,
            tiled=True,
        ).astype(jnp.float32),
    )
    query_grad_rows = (
        unrotate(
            from_blocks(query_grads, seq_count, local_kv, groups).reshape(total_rows, -1, DH),
            cos_table,
            sin_table,
        )
        .astype(jnp.bfloat16)
        .reshape(total_rows, -1)
    )
    key_grad_rows = (
        unrotate(key_back.reshape(total_rows, local_kv, DH), cos_table, sin_table)
        .astype(jnp.bfloat16)
        .reshape(total_rows, -1)
    )
    value_grad_rows = value_back.reshape(total_rows, -1).astype(jnp.bfloat16)
    query_weight_grad = contract(normed_attn, query_grad_rows, 0, 0)
    key_weight_grad = contract(normed_attn, key_grad_rows, 0, 0)
    value_weight_grad = contract(normed_attn, value_grad_rows, 0, 0)
    normed_partial = (
        contract(query_grad_rows, attn_back[1], 1, 1)
        + contract(key_grad_rows, attn_back[2], 1, 1)
        + contract(value_grad_rows, attn_back[3], 1, 1)
    )
    normed_attn_grad = lax.psum(normed_partial.astype(jnp.bfloat16), "tp").astype(jnp.float32)
    attn_gain_term = jnp.sum(normed_attn_grad * inputs * scale_attn, axis=0)
    input_grad = norm_back(
        residual_grad, normed_attn_grad * attn_back[0].astype(jnp.float32), inputs, scale_attn
    )
    attn_grads = (
        lax.psum_scatter(attn_gain_term, ("fsdp", "ctx"), scatter_dimension=0, tiled=True),
        lax.psum_scatter(query_weight_grad, ("fsdp", "ctx"), scatter_dimension=0, tiled=True),
        lax.psum_scatter(key_weight_grad, ("fsdp", "ctx"), scatter_dimension=0, tiled=True),
        lax.psum_scatter(value_weight_grad, ("fsdp", "ctx"), scatter_dimension=0, tiled=True),
        lax.psum_scatter(out_weight_grad, ("fsdp", "ctx"), scatter_dimension=1, tiled=True),
    )
    return (
        layer_output,
        input_grad.astype(jnp.bfloat16).reshape(seq_count, span, width),
        attn_grads[0],
        attn_grads[1],
        attn_grads[2],
        attn_grads[3],
        attn_grads[4],
        mlp_grads[0],
        mlp_grads[1],
        mlp_grads[2],
        mlp_grads[3],
    )


def solution(mesh):
    return jax.shard_map(
        on_device,
        mesh=mesh,
        in_specs=(
            P("fsdp", "ctx", None),
            P("fsdp", "ctx"),
            P("fsdp", "ctx"),
            P(("fsdp", "ctx")),
            P(("fsdp", "ctx"), "tp"),
            P(("fsdp", "ctx"), "tp"),
            P(("fsdp", "ctx"), "tp"),
            P("tp", ("fsdp", "ctx")),
            P(("fsdp", "ctx")),
            P(("fsdp", "ctx"), "tp"),
            P(("fsdp", "ctx"), "tp"),
            P("tp", ("fsdp", "ctx")),
            P("fsdp", "ctx", None),
        ),
        out_specs=(
            P("fsdp", "ctx", None),
            P("fsdp", "ctx", None),
            P(("fsdp", "ctx")),
            P(("fsdp", "ctx"), "tp"),
            P(("fsdp", "ctx"), "tp"),
            P(("fsdp", "ctx"), "tp"),
            P("tp", ("fsdp", "ctx")),
            P(("fsdp", "ctx")),
            P(("fsdp", "ctx"), "tp"),
            P(("fsdp", "ctx"), "tp"),
            P("tp", ("fsdp", "ctx")),
        ),
        check_vma=False,
    )
```

profile of v0, /device:TPU:11, one launch (start us, length us, event | category | flops | bytes accessed | tf_op | source)
XLA Modules:
  0.0 1360.6 jit_solution(13727046639164746978)
XLA Ops:
  12.3 6.2 all_gather.45
  22.2 33.2 %all-reduce.5 = (bf16[1536]{0:T(1024)(128)(2,1)S(1)}, bf16[1536]{0:T(1024)(128)(2,1)}) all-reduce(bf16[1536]{0:T(1024)(128)(2,1)S(1)} %dynamic-update-slice, bf16[1536]{0:T(1024)(128)(2,1)S(1)} %dynamic-update-slice.1), channel_id=1, replica_groups=mesh['fsdp'=4,'ctx'=4,'tp'=2] {'fsdp','ctx'}, use_global_device_ids=true, to_apply=%add | all-reduce | flops 3072 | bytes 12288
  59.9 18.1 %all_gather.49 = bf16[1,1024,384]{1,2,0:T(8,128)(2,1)S(1)} all-gather(bf16[1,256,384]{1,2,0:T(8,128)(2,1)S(1)} %bitcast.263), channel_id=1, replica_groups=mesh['fsdp'=4,'ctx'=4,'tp'=2] {'ctx'}, dimensions={1}, use_global_device_ids=true | all-gather | bytes 983040 | tf_op jit(solution)/shard_map/all_gather | solution.py:154
  78.7 11.9 all-gather.13.cloned.1.call-done
  92.5 20.8 %all-gather = bf16[1024,384]{1,0:T(8,128)(2,1)S(1)} all-gather(bf16[256,384]{1,0:T(8,128)(2,1)S(1)} %convolution_convert_fusion.3), channel_id=2, replica_groups=mesh['fsdp'=4,'ctx'=4,'tp'=2] {'ctx'}, dimensions={0}, use_global_device_ids=true | all-gather | bytes 983040 | tf_op jit(solution)/shard_map/all_gather | solution.py:155
  113.8 22.6 %all-gather.9.cloned.1.call-done = bf16[1536,768]{1,0:T(8,128)(2,1)} async-done(((bf16[96,768]{1,0:T(8,128)(2,1)}), bf16[1536,768]{1,0:T(8,128)(2,1)}) %all-gather.9.cloned.1.call-update) | async-done | bytes 2359312 | tf_op jit(solution)/shard_map/all_gather | solution.py:117
  136.4 4.3 copy.49
  140.7 2.5 fusion.77
  146.7 22.3 %while.28 = (s32[]{:T(128)}, bf16[4,512,96]{1,2,0:T(8,128)(2,1)}, f32[4,512]{1,0:T(4,128)}, s32[4,512]{1,0:T(4,128)}, s32[4,1024]{1,0:T(4,128)}, /*index=5*/bf16...) while((s32[]{:T(128)}, bf16[4,512,96]{1,2,0:T(8,128)(2,1)}, ...), condition=%wide.region_4.5_spmd.clone, body=%wide.region_1.4_spmd.clone.sunk | while | flops 207142400 | bytes 7095425 | solution.py:189
  168.9 2.3 copy.53
  172.4 7.3 all-gather.15.cloned.1.call-done
  179.7 3.7 fusion.102
  185.8 47.3 %all-reduce.11.cloned.1.call-done = f32[256,1536]{1,0:T(8,128)} async-done(((f32[256,1536]{1,0:T(8,128)}), f32[256,1536]{1,0:T(8,128)}) %all-reduce.11.cloned.1.call-update) | async-done | bytes 1572880 | tf_op jit(solution)/shard_map/psum | solution.py:193
  235.0 63.7 %all-gather.17.cloned.1.call-done = bf16[1536,2048]{1,0:T(8,128)(2,1)} async-done(((bf16[96,2048]{1,0:T(8,128)(2,1)}), bf16[1536,2048]{1,0:T(8,128)(2,1)}) %all-gather.17.cloned.1.call-update) | async-done | bytes 6291472 | tf_op jit(solution)/shard_map/all_gather | solution.py:124
  298.7 6.0 fusion.103
  304.7 57.1 %all-gather.19.cloned.1.call-done = bf16[1536,2048]{1,0:T(8,128)(2,1)} async-done(((bf16[96,2048]{1,0:T(8,128)(2,1)}), bf16[1536,2048]{1,0:T(8,128)(2,1)}) %all-gather.19.cloned.1.call-update) | async-done | bytes 6291472 | tf_op jit(solution)/shard_map/all_gather | solution.py:125
  361.8 5.9 fusion.104
  367.6 57.2 %all-gather.21.cloned.1.call-done = bf16[2048,1536]{0,1:T(8,128)(2,1)} async-done(((bf16[2048,96]{0,1:T(8,128)(2,1)}), bf16[2048,1536]{0,1:T(8,128)(2,1)}) %all-gather.21.cloned.1.call-update) | async-done | bytes 6291472 | tf_op jit(solution)/shard_map/all_gather | solution.py:126
  424.8 7.6 multiply_convert_fusion.1
  432.4 5.4 fusion.105
  437.9 3.0 convolution_add_fusion.2
  441.2 48.6 %all-reduce.13.cloned.1.call-done = f32[256,1536]{1,0:T(8,128)} async-done(((f32[256,1536]{1,0:T(8,128)}), f32[256,1536]{1,0:T(8,128)}) %all-reduce.13.cloned.1.call-update) | async-done | bytes 1572880 | tf_op jit(solution)/shard_map/psum | solution.py:220
  489.9 2.5 multiply_reduce_fusion.1
  498.4 42.8 %while.29 = (s32[]{:T(128)}, f32[4,512,96]{1,2,0:T(8,128)}, bf16[4,1024,96]{1,2,0:T(8,128)(2,1)}, bf16[4,1024,96]{1,2,0:T(8,128)(2,1)}, s32[4,512]{1,0:T(4,128)}...) while((s32[]{:T(128)}, f32[4,512,96]{1,2,0:T(8,128)}, ...), condition=%wide.region_12.13_spmd.clone, body=%wide.region_10.12_spmd.clone.sunk | while | flops 509754880 | bytes 32221468 | solution.py:273
  541.9 5.8 convolution_convert_fusion.1
  547.8 2.5 copy.57
  553.7 3.7 fusion.106
  557.4 6.0 reduce-scatter.10.cloned.1.call-done
  566.0 3.1 convolution_add_fusion.1
  569.1 19.7 %reduce-scatter.12.cloned.1.call-done = bf16[1,256,384]{1,2,0:T(8,128)(2,1)} async-done(((bf16[1,1024,384]{1,2,0:T(8,128)(2,1)}), bf16[1,256,384]{1,2,0:T(8,128)(2,1)}) %reduce-scatter.12.cloned.1.call-update) | async-done | bytes 196624 | tf_op jit(solution)/shard_map/reduce_scatter | solution.py:284
  588.8 3.3 fusion.47
  592.8 3.0 fusion.83
  595.9 3.0 fusion.81
  599.0 3.1 fusion.79
  603.0 4.5 fusion.87
  607.8 7.6 fusion.107
  615.5 7.6 fusion.108
  624.2 7.7 fusion.71
  632.6 11.9 all-reduce.15.cloned.1.call-done
  646.2 55.0 %all-reduce.4 = (f32[1536]{0:T(1024)S(1)}, f32[1536]{0:T(1024)S(1)}) all-reduce(f32[1536]{0:T(1024)S(1)} %get-tuple-element.190, f32[1536]{0:T(1024)S(1)} %copy-done.27), channel_id=5, replica_groups=mesh['fsdp'=4,'ctx'=4,'tp'=2] {'fsdp','ctx'}, use_global_device_ids=true, to_apply=%region_18.19.clone | all-reduce | flops 3072 | bytes 24576
  702.4 3.3 fusion.68
  705.7 5.7 reduce-scatter.16.cloned.1.call-done
  711.3 66.2 %reduce-scatter.18.cloned.1.call-done = f32[96,384]{1,0:T(8,128)} async-done(((f32[1536,384]{1,0:T(8,128)}), f32[96,384]{1,0:T(8,128)}) %reduce-scatter.18.cloned.1.call-update) | async-done | bytes 147472 | tf_op jit(solution)/shard_map/reduce_scatter | solution.py:323
  777.6 79.7 %reduce-scatter.14.cloned.1.call-done = f32[96,768]{1,0:T(8,128)} async-done(((f32[1536,768]{1,0:T(8,128)}), f32[96,768]{1,0:T(8,128)}) %reduce-scatter.14.cloned.1.call-update) | async-done | bytes 294928 | tf_op jit(solution)/shard_map/reduce_scatter | solution.py:321
  857.3 78.9 %reduce-scatter.20.cloned.1.call-done = f32[768,96]{0,1:T(8,128)} async-done(((f32[768,1536]{0,1:T(8,128)}), f32[768,96]{0,1:T(8,128)}) %reduce-scatter.20.cloned.1.call-update) | async-done | bytes 294928 | tf_op jit(solution)/shard_map/reduce_scatter | solution.py:324
  936.2 139.8 %reduce-scatter.22.cloned.1.call-done = f32[96,2048]{1,0:T(8,128)} async-done(((f32[1536,2048]{1,0:T(8,128)}), f32[96,2048]{1,0:T(8,128)}) %reduce-scatter.22.cloned.1.call-update) | async-done | bytes 786448 | tf_op jit(solution)/shard_map/reduce_scatter | solution.py:231
  1075.9 139.0 %reduce-scatter.24.cloned.1.call-done = f32[96,2048]{1,0:T(8,128)} async-done(((f32[1536,2048]{1,0:T(8,128)}), f32[96,2048]{1,0:T(8,128)}) %reduce-scatter.24.cloned.1.call-update) | async-done | bytes 786448 | tf_op jit(solution)/shard_map/reduce_scatter | solution.py:232
  1214.9 139.1 %reduce-scatter.26.cloned.1.call-done = f32[2048,96]{0,1:T(8,128)} async-done(((f32[2048,1536]{0,1:T(8,128)}), f32[2048,96]{0,1:T(8,128)}) %reduce-scatter.26.cloned.1.call-update) | async-done | bytes 786448 | tf_op jit(solution)/shard_map/reduce_scatter | solution.py:233
  (271 shorter events, 108.3 us)
Async XLA Ops:
  7.2 50.1 %copy-start.31 = (s32[1,256]{1,0:T(1,128)S(1)}, s32[1,256]{1,0:T(1,128)}, u32[]{:S(2)}) copy-start(s32[1,256]{1,0:T(1,128)} %param.19) | copy-start | bytes 3076
  7.2 50.4 %all-gather.11.cloned.1.call-start = ((), (), s32[]{:S(2)}) async-start(), calls=%async_computation.10 | async-start | bytes 1253376 | tf_op jit(solution)/shard_map/all_gather | solution.py:118
  7.9 82.7 %all-gather.13.cloned.1.call-start = ((), (), s32[]{:S(2)}) async-start(), calls=%async_computation.11 | async-start | bytes 1253376 | tf_op jit(solution)/shard_map/all_gather | solution.py:119
  8.7 127.7 %all-gather.9.cloned.1.call-start = ((), (), s32[]{:S(2)}) async-start(), calls=%async_computation.9 | async-start | bytes 2506752 | tf_op jit(solution)/shard_map/all_gather | solution.py:117
  9.4 170.3 %all-gather.15.cloned.1.call-start = ((), (), s32[]{:S(2)}) async-start(), calls=%async_computation.12 | async-start | bytes 2506752 | tf_op jit(solution)/shard_map/all_gather | solution.py:120
  10.0 223.1 %all-reduce.11.cloned.1.call-start = ((), (), s32[]{:S(2)}) async-start(), calls=%async_computation.13 | async-start | bytes 3145728 | tf_op jit(solution)/shard_map/psum | solution.py:193
  55.3 3.9 copy-start
  57.3 83.3 %copy-start.25 = (f32[256]{0:T(256)}, f32[256]{0:T(256)S(1)}, u32[]{:S(2)}) copy-start(f32[256]{0:T(256)S(1)} %get-tuple-element.268) | copy-start | bytes 3076
  57.6 85.6 %copy-start.15 = (f32[256,48]{0,1:T(8,128)}, f32[256,48]{0,1:T(8,128)S(1)}, u32[]{:S(2)}) copy-start(f32[256,48]{0,1:T(8,128)S(1)} %get-tuple-element.265) | copy-start | bytes 147460
  57.6 85.6 %copy-start.17 = (f32[256,48]{0,1:T(8,128)}, f32[256,48]{0,1:T(8,128)S(1)}, u32[]{:S(2)}) copy-start(f32[256,48]{0,1:T(8,128)S(1)} %get-tuple-element.266) | copy-start | bytes 147460
  168.9 2.3 copy-start.13
  168.9 14.5 %copy-start.6 = (bf16[4,1024,96]{2,1,0:T(8,128)(2,1)}, bf16[4,1024,96]{2,1,0:T(8,128)(2,1)S(1)}, u32[]{:S(2)}) copy-start(bf16[4,1024,96]{2,1,0:T(8,128)(2,1)S(1)} %get-tuple-element.524) | copy-start | bytes 2359300
  168.9 14.5 %copy-start.7 = (bf16[4,1024,96]{2,1,0:T(8,128)(2,1)}, bf16[4,1024,96]{2,1,0:T(8,128)(2,1)S(1)}, u32[]{:S(2)}) copy-start(bf16[4,1024,96]{2,1,0:T(8,128)(2,1)S(1)} %get-tuple-element.525) | copy-start | bytes 2359300
  172.4 11.0 copy-start.8
  183.4 2.3 copy-start.30
  183.4 115.3 %all-gather.17.cloned.1.call-start = ((), (), s32[]{:S(2)}) async-start(), calls=%async_computation.14 | async-start | bytes 6684672 | tf_op jit(solution)/shard_map/all_gather | solution.py:124
  184.0 177.7 %all-gather.19.cloned.1.call-start = ((), (), s32[]{:S(2)}) async-start(), calls=%async_computation.15 | async-start | bytes 6684672 | tf_op jit(solution)/shard_map/all_gather | solution.py:125
  184.8 240.0 %all-gather.21.cloned.1.call-start = ((), (), s32[]{:S(2)}) async-start(), calls=%async_computation.16 | async-start | bytes 6684672 | tf_op jit(solution)/shard_map/all_gather | solution.py:126
  185.5 304.4 %all-reduce.13.cloned.1.call-start = ((), (), s32[]{:S(2)}) async-start(), calls=%async_computation.17 | async-start | bytes 3145728 | tf_op jit(solution)/shard_map/psum | solution.py:220
  432.4 5.4 copy-start.20
  432.4 5.4 copy-start.19
  432.4 5.4 copy-start.32
  440.9 122.4 %reduce-scatter.10.cloned.1.call-start = ((), (), s32[]{:S(2)}) async-start(), calls=%async_computation.18 | async-start | bytes 983040 | tf_op jit(solution)/shard_map/reduce_scatter | solution.py:278
  489.9 2.6 copy-start.5
  489.9 2.6 copy-start.10
  504.1 2.4 copy-start.21
  504.3 3.5 copy-start.23
  514.8 2.4 copy-start.21
  515.0 3.5 copy-start.23
  525.5 2.4 copy-start.21
  525.7 3.5 copy-start.23
  536.2 2.4 copy-start.21
  536.4 3.5 copy-start.23
  541.1 47.6 %reduce-scatter.12.cloned.1.call-start = ((), (), s32[]{:S(2)}) async-start(), calls=%async_computation.19 | async-start | bytes 983040 | tf_op jit(solution)/shard_map/reduce_scatter | solution.py:284
  541.9 102.6 %all-reduce.15.cloned.1.call-start = ((), (), s32[]{:S(2)}) async-start(), calls=%async_computation.27 | async-start | bytes 3145728 | tf_op jit(solution)/shard_map/psum | solution.py:201
  547.8 4.7 copy-start.16
  547.8 4.7 copy-start.18
  563.4 2.7 copy-start.4
  592.1 119.2 %reduce-scatter.16.cloned.1.call-start = ((), (), s32[]{:S(2)}) async-start(), calls=%async_computation.21 | async-start | bytes 2506752 | tf_op jit(solution)/shard_map/reduce_scatter | solution.py:322
  595.8 181.7 %reduce-scatter.18.cloned.1.call-start = ((), (), s32[]{:S(2)}) async-start(), calls=%async_computation.22 | async-start | bytes 2506752 | tf_op jit(solution)/shard_map/reduce_scatter | solution.py:323
  598.9 258.3 %reduce-scatter.14.cloned.1.call-start = ((), (), s32[]{:S(2)}) async-start(), calls=%async_computation.20 | async-start | bytes 5013504 | tf_op jit(solution)/shard_map/reduce_scatter | solution.py:321
  602.1 334.1 %reduce-scatter.20.cloned.1.call-start = ((), (), s32[]{:S(2)}) async-start(), calls=%async_computation.23 | async-start | bytes 5013504 | tf_op jit(solution)/shard_map/reduce_scatter | solution.py:324
  607.5 468.4 %reduce-scatter.22.cloned.1.call-start = ((), (), s32[]{:S(2)}) async-start(), calls=%async_computation.24 | async-start | bytes 13369344 | tf_op jit(solution)/shard_map/reduce_scatter | solution.py:231
  615.4 599.5 %reduce-scatter.24.cloned.1.call-start = ((), (), s32[]{:S(2)}) async-start(), calls=%async_computation.25 | async-start | bytes 13369344 | tf_op jit(solution)/shard_map/reduce_scatter | solution.py:232
  623.1 731.0 %reduce-scatter.26.cloned.1.call-start = ((), (), s32[]{:S(2)}) async-start(), calls=%async_computation.26 | async-start | bytes 13369344 | tf_op jit(solution)/shard_map/reduce_scatter | solution.py:233
  631.9 14.3 %copy-start.27 = (f32[1536]{0:T(1024)S(1)}, f32[1536]{0:T(1024)}, u32[]{:S(2)}) copy-start(f32[1536]{0:T(1024)} %get-tuple-element.188) | copy-start | bytes 18436
  631.9 70.5 %copy-start.29 = (f32[256]{0:T(256)S(1)}, f32[256]{0:T(256)}, u32[]{:S(2)}) copy-start(f32[256]{0:T(256)} %get-tuple-element.267) | copy-start | bytes 3076
  644.5 57.9 %copy-start.12 = (bf16[256,1536]{1,0:T(8,128)(2,1)S(1)}, bf16[256,1536]{1,0:T(8,128)(2,1)}, u32[]{:S(2)}) copy-start(bf16[256,1536]{1,0:T(8,128)(2,1)} %get-tuple-element.239) | copy-start | bytes 2359300
  (19 other events, 23.6 us)
Sparse Core Ops, SparseCore 0:
  10.3 39.2 all-gather.10
  51.9 38.6 all-gather.12
  92.9 43.4 all-gather.8
  138.5 41.1 all-gather.14
  183.6 49.4 all-reduce.10
  235.5 63.1 all-gather.16
  301.3 60.4 all-gather.18
  364.3 60.4 all-gather.20
  441.1 48.7 all-reduce.12
  541.3 22.0 reduce-scatter.9
  566.3 22.4 reduce-scatter.11
  592.3 52.1 all-reduce.14
  649.3 61.9 reduce-scatter.15
  715.5 61.9 reduce-scatter.17
  782.3 74.8 reduce-scatter.13
  861.5 74.5 reduce-scatter.19
  941.2 134.7 reduce-scatter.21
  1081.0 133.9 reduce-scatter.23
  1220.1 133.8 reduce-scatter.25
where the time goes:
time: 1370 us; the launch traced here: 1360 us
  waiting for transfers between devices  1010 us (74%)
  blocking collectives  133 us (10%)
  matrix products  126 us (9%)
  local copies, waits for them, and re-layouts  56.2 us (4%)
  other arithmetic  20.3 us (1%)
  between operations  15.7 us (1%)
    reduce_scatter x1, waiting for transfers between devices, on_device(): lax.psum_scatter(gate_weight_grad, ('fsdp', 'ctx'), scatter_dimension=0,...  140 us
    reduce_scatter x1, waiting for transfers between devices, on_device(): lax.psum_scatter(down_weight_grad, ('fsdp', 'ctx'), scatter_dimension=1,...  139 us
    reduce_scatter x1, waiting for transfers between devices, on_device(): lax.psum_scatter(up_weight_grad, ('fsdp', 'ctx'), scatter_dimension=0, ti...  139 us
    unnamed x2, blocking collectives  88.2 us
    reduce_scatter x1, waiting for transfers between devices, on_device(): lax.psum_scatter(query_weight_grad, ('fsdp', 'ctx'), scatter_dimension=0,...  79.7 us
    reduce_scatter x1, waiting for transfers between devices, on_device(): lax.psum_scatter(out_weight_grad, ('fsdp', 'ctx'), scatter_dimension=1, t...  78.9 us
    reduce_scatter x1, waiting for transfers between devices, on_device(): lax.psum_scatter(value_weight_grad, ('fsdp', 'ctx'), scatter_dimension=0,...  66.2 us
    all_gather x1, waiting for transfers between devices, on_device(): lax.all_gather(gate_proj, ('fsdp', 'ctx'), axis=0, tiled=True)  63.7 us
  transfers between devices with their start and end apart: 19, of which 18 were waited for; matrix products, arithmetic and copies ran while one was open for 9% of the time, Pallas kernels for 0%

commit v1 on v0

v1 whole, which is shorter than its diff:
```python
import functools

import jax
import jax.numpy as jnp
from jax import lax
from jax.experimental import pallas as pl
from jax.experimental.pallas import tpu as pltpu
from jax.sharding import Mesh, PartitionSpec as P

HQ = 16
HK = 8
DH = 96


EPS = 1e-05
THETA = 100000.0
NEGATIVE = -1e30


def rotary_tables(positions):
    half_dim = DH // 2
    freq_index = jnp.arange(half_dim, dtype=jnp.float32)
    inverse = THETA ** (-2.0 * freq_index / DH)
    angles = positions.astype(jnp.float32)[..., None] * inverse
    return (jnp.cos(angles), jnp.sin(angles))


def rotate(field_in, cos_table, sin_table):
    half_dim = field_in.shape[-1] // 2
    front_half = field_in[..., :half_dim]
    back_half = field_in[..., half_dim:]
    return jnp.concatenate(
        [
            front_half * cos_table - back_half * sin_table,
            back_half * cos_table + front_half * sin_table,
        ],
        axis=-1,
    )


def unrotate(field_in, cos_table, sin_table):
    half_dim = field_in.shape[-1] // 2
    front_half = field_in[..., :half_dim]
    back_half = field_in[..., half_dim:]
    return jnp.concatenate(
        [
            front_half * cos_table + back_half * sin_table,
            back_half * cos_table - front_half * sin_table,
        ],
        axis=-1,
    )


def inverse_rms(values):
    return lax.rsqrt(jnp.mean(values * values, axis=-1, keepdims=True) + EPS)


def contract(left, right, left_dim, right_dim):
    return lax.dot_general(
        left, right, (((left_dim,), (right_dim,)), ((), ())), preferred_element_type=jnp.float32
    )


def norm_back(upstream, inner, values, scale_rows):
    cubed = scale_rows * scale_rows * scale_rows
    return (
        upstream
        + scale_rows * inner
        - values * cubed * jnp.mean(inner * values, axis=-1, keepdims=True)
    )


def to_blocks(matrix, seq_count, local_kv, groups):
    span = matrix.shape[0] // seq_count
    shaped = matrix.reshape(seq_count, span, local_kv, groups, DH).transpose(0, 2, 1, 3, 4)
    return shaped.reshape(seq_count * local_kv, span * groups, DH)


def from_blocks(blocks, seq_count, local_kv, groups):
    span = blocks.shape[1] // groups
    shaped = blocks.reshape(seq_count, local_kv, span, groups, DH).transpose(0, 2, 1, 3, 4)
    return shaped.reshape(seq_count * span, local_kv * groups * DH)


def seq_items(matrix, local_kv):
    seq_count = matrix.shape[0]
    length = matrix.shape[1]
    return (
        matrix.reshape(seq_count, length, local_kv, DH)
        .transpose(0, 2, 1, 3)
        .reshape(seq_count * local_kv, length, DH)
    )


def from_items(items, seq_count, local_kv):
    length = items.shape[1]
    return (
        items.reshape(seq_count, local_kv, length, DH)
        .transpose(0, 2, 1, 3)
        .reshape(seq_count, length, local_kv * DH)
    )


MESH_ID = pl.DeviceIdType.MESH
BF16 = jnp.bfloat16
F32 = jnp.float32
GROUP = ("fy", "pr", "ctx")
VMEM_LIMIT = 60 * 1024 * 1024
LANES = 128


def remote(src, dst, send_sem, recv_sem, device):
    return pltpu.make_async_remote_copy(
        src_ref=src,
        dst_ref=dst,
        send_sem=send_sem,
        recv_sem=recv_sem,
        device_id=device,
        device_id_type=MESH_ID,
    )


def greet(devices_and_conditions, count):
    barrier = pltpu.get_barrier_semaphore()
    for device, condition in devices_and_conditions:
        if condition is None:
            pl.semaphore_signal(barrier, inc=1, device_id=device, device_id_type=MESH_ID)
        else:

            @pl.when(condition)
            def _(device=device):
                pl.semaphore_signal(barrier, inc=1, device_id=device, device_id_type=MESH_ID)

    pl.semaphore_wait(barrier, count)


def dot(left, right, left_dim=1, right_dim=0):
    return lax.dot_general(
        left, right, (((left_dim,), (right_dim,)), ((), ())), preferred_element_type=F32
    )


def pair_kernel(nz, ng, *refs):
    raws = refs[:ng]
    small, rows_in, grad_in = refs[ng : ng + 3]
    pieces = refs[ng + 3 : 2 * ng + 3]
    smalls, rows_out, grad_out = refs[2 * ng + 3 : 2 * ng + 6]
    loc, cs, cr, zs, zr, ts, tr = refs[2 * ng + 6 :]
    y = lax.axis_index("fy")
    c = lax.axis_index("pr")
    z = lax.axis_index("ctx")
    other_y = {"fy": 1 - y}
    other_c = {"pr": 1 - c}
    greet(
        [(other_y, None), (other_c, None)] + [({"ctx": t}, z != t) for t in range(nz)], nz + 1
    )

    def small_to(t):
        return remote(small, smalls.at[y, c, z], zs.at[t], zr.at[z], {"ctx": t})

    def small_from(t):
        return remote(small, smalls.at[y, c, t], zs.at[t], zr.at[t], {"ctx": t})

    mine = pltpu.make_async_copy(small, smalls.at[y, c, z], loc.at[ng + 2])
    mine.start()
    for t in range(nz):

        @pl.when(z != t)
        def _(t=t):
            small_to(t).start()

    core = [remote(raws[g].at[1 - c], pieces[g].at[c], cs.at[g], cr.at[g], other_c) for g in range(ng)]
    local = [pltpu.make_async_copy(raws[g].at[c], pieces[g].at[c], loc.at[g]) for g in range(ng)]
    core.append(remote(rows_in, rows_out.at[c], cs.at[ng], cr.at[ng], other_c))
    core.append(remote(grad_in, grad_out.at[c], cs.at[ng + 1], cr.at[ng + 1], other_c))
    local.append(pltpu.make_async_copy(rows_in, rows_out.at[c], loc.at[ng]))
    local.append(pltpu.make_async_copy(grad_in, grad_out.at[c], loc.at[ng + 1]))
    for copy in core + local:
        copy.start()
    mine.wait()
    for t in range(nz):

        @pl.when(z != t)
        def _(t=t):
            small_from(t).wait_recv()

    line = remote(smalls.at[y, c], smalls.at[y, c], ts.at[0], tr.at[0], other_y)
    line.start()
    remote(smalls.at[1 - y, c], smalls.at[1 - y, c], ts.at[0], tr.at[0], other_y).wait_recv()
    plane = remote(smalls.at[:, c], smalls.at[:, c], ts.at[1], tr.at[1], other_c)
    plane.start()
    remote(smalls.at[:, 1 - c], smalls.at[:, 1 - c], ts.at[1], tr.at[1], other_c).wait_recv()
    for copy in core:
        copy.wait()
    for copy in local:
        copy.wait()
    line.wait_send()
    plane.wait_send()
    for t in range(nz):

        @pl.when(z != t)
        def _(t=t):
            small_to(t).wait_send()


def pair_swap(raws, small, rows, grads, ny, nz):
    ng = len(raws)
    dma = pltpu.SemaphoreType.DMA
    vmem = pl.BlockSpec(memory_space=pltpu.VMEM)
    shapes = [jax.ShapeDtypeStruct(raw.shape, raw.dtype) for raw in raws]
    shapes.append(jax.ShapeDtypeStruct((ny, 2, nz) + small.shape, small.dtype))
    shapes.append(jax.ShapeDtypeStruct((2,) + rows.shape, rows.dtype))
    shapes.append(jax.ShapeDtypeStruct((2,) + grads.shape, grads.dtype))
    results = pl.pallas_call(
        functools.partial(pair_kernel, nz, ng),
        out_shape=shapes,
        in_specs=[vmem] * (ng + 3),
        out_specs=[vmem] * (ng + 3),
        scratch_shapes=[
            dma((ng + 3,)),
            dma((ng + 2,)),
            dma((ng + 2,)),
            dma((nz,)),
            dma((nz,)),
            dma((2,)),
            dma((2,)),
        ],
        name="pair_swap",
        compiler_params=pltpu.CompilerParams(collective_id=0, has_side_effects=True),
    )(*raws, small, rows, grads)
    return results[:ng], results[ng], results[ng + 1], results[ng + 2]


class Gather:
    def __init__(self, nz, outs, us, ur, ds, dr, ys, yr, es, er):
        self.nz, self.outs = nz, outs
        self.sems = (us, ur, ds, dr, ys, yr, es, er)
        self.y = lax.axis_index("fy")
        self.z = lax.axis_index("ctx")
        self.odd = lax.rem(self.z, 2)
        self.pair = self.z + 1 - 2 * self.odd

    def up(self, g, s, slot):
        piece = self.outs[g].at[self.y, :, self.z - s]
        us, ur = self.sems[0], self.sems[1]
        return remote(piece, piece, us.at[g, slot], ur.at[g, slot], {"ctx": self.z + 1})

    def down(self, g, s, slot):
        piece = self.outs[g].at[self.y, :, self.z + s]
        ds, dr = self.sems[2], self.sems[3]
        return remote(piece, piece, ds.at[g, slot], dr.at[g, slot], {"ctx": self.z - 1})

    def across(self, g, slot, origin, half, row):
        piece = self.outs[g].at[row, 0, origin] if half else self.outs[g].at[row, :, origin]
        ys, yr = self.sems[4], self.sems[5]
        return remote(piece, piece, ys.at[g, slot], yr.at[g, slot], {"fy": 1 - self.y})

    def extra(self, g, origin):
        piece = self.outs[g].at[1 - self.y, 1, origin]
        es, er = self.sems[6], self.sems[7]
        return remote(piece, piece, es.at[g], er.at[g], {"ctx": self.pair})

    def own_z(self, g):
        @pl.when(self.z < self.nz - 1)
        def _():
            self.up(g, 0, 0).start()

        @pl.when(self.z > 0)
        def _():
            self.down(g, 0, 0).start()

    def own_y(self, g):
        self.across(g, 0, self.z, False, self.y).start()

    def each_across(self, g, s, row, act):
        z, nz = self.z, self.nz
        if s == 0:
            act(self.across(g, 0, z, False, row))
            return
        if s == 1:

            @pl.when(self.odd == 1)
            def _():
                act(self.across(g, 1, z - 1, True, row))

            @pl.when((self.odd == 0) & (z > 0))
            def _():
                act(self.across(g, 1, z - 1, False, row))

            @pl.when(self.odd == 0)
            def _():
                act(self.across(g, nz, z + 1, True, row))

            @pl.when((self.odd == 1) & (z < nz - 1))
            def _():
                act(self.across(g, nz, z + 1, False, row))

            return

        @pl.when(z >= s)
        def _():
            act(self.across(g, s, z - s, False, row))

        @pl.when(z + s < nz)
        def _():
            act(self.across(g, nz - 1 + s, z + s, False, row))

    def step(self, g, s):
        z, nz = self.z, self.nz

        @pl.when(z >= s)
        def _():
            self.up(g, s - 1 + 1, s - 1).wait_recv()

            @pl.when(z < nz - 1)
            def _():
                self.up(g, s, s).start()

        @pl.when(z + s < nz)
        def _():
            self.down(g, s, s - 1).wait_recv()

            @pl.when(z > 0)
            def _():
                self.down(g, s, s).start()

        self.each_across(g, s, self.y, lambda copy: copy.start())

    def spread(self, g):
        self.across(g, 0, self.z, False, 1 - self.y).wait_recv()
        self.extra(g, self.z).start()

    def finish(self, g):
        for s in range(1, self.nz):
            self.each_across(g, s, 1 - self.y, lambda copy: copy.wait_recv())
        self.extra(g, self.pair).wait_recv()

    def drain(self, g):
        z, nz = self.z, self.nz
        for s in range(nz):

            @pl.when((z >= s) & (z < nz - 1))
            def _(s=s):
                self.up(g, s, s).wait_send()

            @pl.when((z + s < nz) & (z > 0))
            def _(s=s):
                self.down(g, s, s).wait_send()

            self.each_across(g, s, self.y, lambda copy: copy.wait_send())
        self.extra(g, self.z).wait_send()


def forward_kernel(nz, items, scale, *refs):
    (normed, rows, cos, sin, q_seg, k_seg, spread_mat, gain) = refs[5:13]
    pieces = refs[:5]
    outs = refs[13:18]
    (q_out, k_out, v_out, mixed_out, mixed_low, lse_out, residual, normed_mlp) = refs[18:26]
    (acc, kvu, top, core_send, core_land, x_send, x_land, attended) = refs[26:34]
    loc, us, ur, ds, dr, ys, yr, es, er, ks, kr, cs, cr, xs, xr, ns, nr = refs[34:]
    y = lax.axis_index("fy")
    c = lax.axis_index("pr")
    z = lax.axis_index("ctx")
    x = lax.axis_index("tp")
    span = rows.shape[0]
    other_c = {"pr": 1 - c}
    other_x = {"tp": 1 - x}
    gather = Gather(nz, outs, us, ur, ds, dr, ys, yr, es, er)
    greet(
        [
            ({"fy": 1 - y}, None),
            (other_c, None),
            (other_x, None),
            ({"ctx": z + 1}, z < nz - 1),
            ({"ctx": z - 1}, z > 0),
        ],
        3 + (z < nz - 1).astype(jnp.int32) + (z > 0).astype(jnp.int32),
    )
    local = [pltpu.make_async_copy(pieces[g], outs[g].at[y, :, z], loc.at[g]) for g in range(5)]
    for copy in local:
        copy.start()
    early, late = (0, 1), (2, 3, 4)
    for g in early:
        local[g].wait()
        gather.own_z(g)
        gather.own_y(g)
    for g in late:
        local[g].wait()
    for s in range(1, nz):
        for g in early:
            gather.step(g, s)
        if s == 1:
            for g in early:
                gather.spread(g)
        if s == min(2, nz - 1):
            for g in late:
                gather.own_z(g)
    for g in late:
        gather.own_y(g)
    for g in early:
        gather.finish(g)

    chunk = nz * outs[0].shape[3]
    half = outs[0].shape[4] // 2
    for i in range(4):
        block = outs[0][i // 2, i % 2].reshape(chunk, 2 * half)
        wide = jnp.concatenate(
            [
                dot(block[:, :half], spread_mat[...]).astype(BF16),
                dot(block[:, half:], spread_mat[...]).astype(BF16),
            ],
            axis=1,
        )
        part = dot(normed[:, i * chunk : (i + 1) * chunk], wide)
        if i == 0:
            acc[...] = part
        else:
            acc[...] += part

    def rotated(b, lane):
        field = acc[pl.ds(b * span, span), pl.ds(lane * LANES, LANES)]
        turned = pltpu.roll(field, LANES // 2, 1)
        return (field * cos[pl.ds(b * span, span)] + turned * sin[pl.ds(b * span, span)]).astype(
            BF16
        )

    def keys_up(b, s):
        piece = kvu.at[z - s, b]
        return remote(piece, piece, ks.at[b, s], kr.at[b, s], {"ctx": z + 1})

    def keys_from(b, s):
        piece = kvu.at[z - s, b]
        return remote(piece, piece, ks.at[b, s - 1], kr.at[b, s - 1], {"ctx": z - 1})

    for b in range(2):
        fields = []
        for k in range(2):
            k_out[z, b * 2 + k] = rotated(b, 4 + k)
            fields.append(k_out[z, b * 2 + k])
        for k in range(2):
            v_out[z, b * 2 + k] = acc[
                pl.ds(b * span, span), pl.ds((6 + k) * LANES, LANES)
            ].astype(BF16)
            fields.append(v_out[z, b * 2 + k])
        kvu[z, b] = dot(jnp.concatenate(fields, axis=1), spread_mat[...], 1, 1).astype(BF16)

        @pl.when(z < nz - 1)
        def _(b=b):
            keys_up(b, 0).start()

    for b in range(2):
        for k in range(2):
            for j in range(2):
                q_out[b * 2 + k, pl.ds(j * span, span)] = rotated(b, 2 * k + j)

    def attend(block, first):
        def one(i, _):
            b = i // 2
            scores = dot(q_out[i], k_out[block, i], 1, 1) * scale
            allowed = q_seg[b] == k_seg[b, block]
            if first:
                row = lax.broadcasted_iota(jnp.int32, scores.shape, 0)
                column = lax.broadcasted_iota(jnp.int32, scores.shape, 1)
                allowed = allowed & (lax.rem(row, span) >= column)
            scores = jnp.where(allowed, scores, NEGATIVE)
            peak = jnp.max(scores, axis=1, keepdims=True)
            if first:
                probs = jnp.exp(scores - peak)
                total = jnp.sum(probs, axis=1, keepdims=True)
                mixed_out[i] = dot(probs.astype(BF16), v_out[block, i])
            else:
                old = top[i][:, :1]
                peak = jnp.maximum(old, peak)
                keep = jnp.exp(old - peak)
                probs = jnp.exp(scores - peak)
                total = keep * lse_out[i][:, :1] + jnp.sum(probs, axis=1, keepdims=True)
                mixed_out[i] = keep * mixed_out[i] + dot(probs.astype(BF16), v_out[block, i])
            top[i] = jnp.broadcast_to(peak, top.shape[1:])
            lse_out[i] = jnp.broadcast_to(total, lse_out.shape[1:])
            return 0

        lax.fori_loop(0, items, one, 0)

    attend(z, True)
    for g in late:
        gather.step(g, 1)
    for s in range(1, nz):

        @pl.when(z >= s)
        def _(s=s):
            for b in range(2):
                keys_from(b, s).wait_recv()

                @pl.when(z < nz - 1)
                def _(b=b):
                    keys_up(b, s).start()

                wide = dot(kvu[z - s, b], spread_mat[...]).astype(BF16)
                for k in range(2):
                    k_out[z - s, b * 2 + k] = wide[:, k * LANES : (k + 1) * LANES]
                    v_out[z - s, b * 2 + k] = wide[:, (2 + k) * LANES : (3 + k) * LANES]
            attend(z - s, False)

        if s == 1:
            for g in late:
                gather.spread(g)

    for i in range(items):
        total = lse_out[i]
        mixed_out[i] = mixed_out[i] / total
        lse_out[i] = top[i] + jnp.log(total)
    for b in range(2):
        heads = [
            mixed_out[b * 2 + k, pl.ds(j * span, span)].astype(BF16)
            for k in range(2)
            for j in range(2)
        ]
        mixed_low[pl.ds(b * span, span)] = dot(
            jnp.concatenate(heads, axis=1), spread_mat[...], 1, 1
        ).astype(BF16)
    for g in late:
        if nz > 2:
            gather.step(g, 2)

    def core(i):
        return remote(core_send.at[i], core_land.at[i], cs.at[i], cr.at[i], other_c)

    def sideways(i):
        return remote(x_send.at[i], x_land.at[i], xs.at[i], xr.at[i], other_x)

    def projected(who, i):
        weights = outs[1][i // 2, i % 2].reshape(chunk, half)
        return dot(mixed_low[pl.ds(pl.multiple_of(who * span, span), span)], weights, 1, 1)

    for i in range(4):
        core_send[i] = projected(1 - c, i).astype(BF16)
        core(i).start()
    for i in range(4):
        part = projected(c, i)
        core(i).wait_recv()
        x_send[i] = (part + core_land[i].astype(F32)).astype(BF16)
        sideways(i).start()
    for s in range(3, nz):
        for g in late:
            gather.step(g, s)
    squares = jnp.zeros((span, 1), F32)
    for i in range(4):
        sideways(i).wait_recv()
        column = pl.ds(i * chunk, chunk)
        total = rows[:, column].astype(F32) + (x_send[i].astype(F32) + x_land[i].astype(F32))
        residual[:, column] = total
        squares = squares + jnp.sum(total * total, axis=1, keepdims=True)
    factor = lax.rsqrt(squares / (4 * chunk) + EPS)
    normed_mlp[c] = (residual[...] * factor * gain[...]).astype(BF16)
    swap = remote(normed_mlp.at[c], normed_mlp.at[c], ns.at[0], nr.at[0], other_c)
    swap.start()
    remote(normed_mlp.at[1 - c], normed_mlp.at[1 - c], ns.at[0], nr.at[0], other_c).wait_recv()
    for g in late:
        gather.finish(g)
    for g in range(5):
        gather.drain(g)
    for b in range(2):
        for s in range(nz):

            @pl.when((z >= s) & (z < nz - 1))
            def _(b=b, s=s):
                keys_up(b, s).wait_send()

    for i in range(4):
        core(i).wait_send()
        sideways(i).wait_send()
    swap.wait_send()


def forward(pieces, normed, rows, cos, sin, q_seg, k_seg, spread_mat, gain, ny, nz):
    dma = pltpu.SemaphoreType.DMA
    vmem = pl.BlockSpec(memory_space=pltpu.VMEM)
    span, width = rows.shape
    items, q_rows = 4, 2 * span
    shape = jax.ShapeDtypeStruct
    chunk = width // 4
    out_shape = [shape((ny, 2, nz) + piece.shape[1:], BF16) for piece in pieces] + [
        shape((items, q_rows, LANES), BF16),
        shape((nz, items, span, LANES), BF16),
        shape((nz, items, span, LANES), BF16),
        shape((items, q_rows, LANES), F32),
        shape((2 * span, 4 * DH), BF16),
        shape((items, q_rows, LANES), F32),
        shape((span, width), F32),
        shape((2, span, width), BF16),
    ]
    return pl.pallas_call(
        functools.partial(forward_kernel, nz, items, DH ** (-0.5)),
        out_shape=out_shape,
        in_specs=[vmem] * 13,
        out_specs=[vmem] * len(out_shape),
        scratch_shapes=[
            pltpu.VMEM((2 * span, 8 * LANES), F32),
            pltpu.VMEM((nz, 2, span, 4 * DH), BF16),
            pltpu.VMEM((items, q_rows, LANES), F32),
        ]
        + [pltpu.VMEM((4, span, chunk), BF16)] * 4
        + [pltpu.VMEM((8, LANES), F32)]
        + [dma((5,))]
        + [dma((5, nz))] * 4
        + [dma((5, 2 * nz))] * 2
        + [dma((5,))] * 2
        + [dma((2, nz))] * 2
        + [dma((4,))] * 4
        + [dma((1,))] * 2,
        name="forward",
        compiler_params=pltpu.CompilerParams(
            collective_id=1, has_side_effects=True, vmem_limit_bytes=VMEM_LIMIT
        ),
    )(*pieces, normed, rows, cos, sin, q_seg, k_seg, spread_mat, gain)


def keys_down_kernel(nz, grads, out, sends, lands, ds, dr):
    z = lax.axis_index("ctx")
    greet(
        [({"ctx": z + 1}, z < nz - 1), ({"ctx": z - 1}, z > 0)],
        (z < nz - 1).astype(jnp.int32) + (z > 0).astype(jnp.int32),
    )

    def down(b, t):
        return remote(sends.at[t, b], lands.at[t, b], ds.at[b, t], dr.at[b, t], {"ctx": z - 1})

    for t in range(nz):
        for b in range(2):

            @pl.when(z >= t)
            def _(b=b, t=t):
                @pl.when(z < nz - 1)
                def _():
                    down(b, t).wait_recv()
                    sends[t, b] = (grads[t, b].astype(F32) + lands[t, b].astype(F32)).astype(BF16)

                @pl.when(z == nz - 1)
                def _():
                    sends[t, b] = grads[t, b]

                @pl.when(z > t)
                def _():
                    down(b, t).start()

                @pl.when(z == t)
                def _():
                    out[b] = sends[t, b]

    for t in range(nz):
        for b in range(2):

            @pl.when(z > t)
            def _(b=b, t=t):
                down(b, t).wait_send()


def keys_down(grads, nz):
    dma = pltpu.SemaphoreType.DMA
    vmem = pl.BlockSpec(memory_space=pltpu.VMEM)
    return pl.pallas_call(
        functools.partial(keys_down_kernel, nz),
        out_shape=jax.ShapeDtypeStruct(grads.shape[1:], BF16),
        in_specs=[vmem],
        out_specs=vmem,
        scratch_shapes=[
            pltpu.VMEM(grads.shape, BF16),
            pltpu.VMEM(grads.shape, BF16),
            dma((2, nz)),
            dma((2, nz)),
        ],
        name="keys_down",
        compiler_params=pltpu.CompilerParams(
            collective_id=2, has_side_effects=True, vmem_limit_bytes=VMEM_LIMIT
        ),
    )(grads)


CHUNKS = 4


def sum_kernel(part, out, core_send, core_land, x_send, x_land, cs, cr, xs, xr, fs, fr):
    c = lax.axis_index("pr")
    x = lax.axis_index("tp")
    other_c = {"pr": 1 - c}
    other_x = {"tp": 1 - x}
    greet([(other_c, None), (other_x, None)], 2)
    rows = part.shape[1] // CHUNKS

    def core(i):
        return remote(core_send.at[i], core_land.at[i], cs.at[i], cr.at[i], other_c)

    def across(i):
        return remote(x_send.at[i], x_land.at[i], xs.at[i], xr.at[i], other_x)

    def final(i):
        piece = out.at[c, pl.ds(i * rows, rows)]
        return remote(piece, piece, fs.at[i], fr.at[i], other_c)

    def final_from(i):
        piece = out.at[1 - c, pl.ds(i * rows, rows)]
        return remote(piece, piece, fs.at[i], fr.at[i], other_c)

    for i in range(CHUNKS):
        core_send[i] = part[1 - c, pl.ds(i * rows, rows)].astype(BF16)
        core(i).start()
    for i in range(CHUNKS):
        core(i).wait_recv()
        x_send[i] = (
            part[c, pl.ds(i * rows, rows)].astype(F32) + core_land[i].astype(F32)
        ).astype(BF16)
        across(i).start()
    for i in range(CHUNKS):
        across(i).wait_recv()
        out[c, pl.ds(i * rows, rows)] = x_send[i].astype(F32) + x_land[i].astype(F32)
        final(i).start()
    for i in range(CHUNKS):
        final_from(i).wait_recv()
    for i in range(CHUNKS):
        core(i).wait_send()
        across(i).wait_send()
        final(i).wait_send()


def sum_parts(part):
    dma = pltpu.SemaphoreType.DMA
    vmem = pl.BlockSpec(memory_space=pltpu.VMEM)
    rows, width = part.shape[1] // CHUNKS, part.shape[2]
    return pl.pallas_call(
        sum_kernel,
        out_shape=jax.ShapeDtypeStruct(part.shape, F32),
        in_specs=[vmem],
        out_specs=vmem,
        scratch_shapes=[pltpu.VMEM((CHUNKS, rows, width), BF16)] * 4 + [dma((CHUNKS,))] * 6,
        name="sum_parts",
        compiler_params=pltpu.CompilerParams(
            collective_id=3, has_side_effects=True, vmem_limit_bytes=VMEM_LIMIT
        ),
    )(part)


def inward(nz):
    order = []
    for k in range((nz + 1) // 2):
        order.append(nz - 1 - k)
        if k != nz - 1 - k:
            order.append(k)
    return order


def scatter_kernel(nz, ng, *refs):
    parts = refs[:ng]
    small = refs[ng]
    outs = refs[ng + 1 : 2 * ng + 1]
    smalls = refs[2 * ng + 1]
    scratch = refs[2 * ng + 2 :]
    owns, lands, ins, sends, totals = (scratch[i * ng : (i + 1) * ng] for i in range(5))
    loc, ys, yr, zs, zr, cs, cr, ws, wr, ts, tr = scratch[5 * ng :]
    y = lax.axis_index("fy")
    c = lax.axis_index("pr")
    z = lax.axis_index("ctx")
    other_y = {"fy": 1 - y}
    other_c = {"pr": 1 - c}
    greet(
        [(other_y, None), (other_c, None)] + [({"ctx": t}, z != t) for t in range(nz)], nz + 1
    )

    def across(g, t):
        return remote(parts[g].at[1 - y, :, t], lands[g].at[t], ys.at[g, t], yr.at[g, t], other_y)

    def own(g, t):
        return pltpu.make_async_copy(parts[g].at[y, :, t], owns[g].at[t], loc.at[g, t])

    def up(g, t):
        return remote(
            sends[g].at[t], ins[g].at[0, t], zs.at[0, g, t], zr.at[0, g, t], {"ctx": z + 1}
        )

    def down(g, t):
        return remote(
            sends[g].at[t], ins[g].at[1, t], zs.at[1, g, t], zr.at[1, g, t], {"ctx": z - 1}
        )

    def swap(g):
        return remote(totals[g].at[1 - c], outs[g].at[c], cs.at[g], cr.at[g], other_c)

    def keep(g):
        return pltpu.make_async_copy(totals[g].at[c], outs[g].at[c], loc.at[ng, g])

    def swap_from(g):
        return remote(totals[g].at[1 - c], outs[g].at[1 - c], cs.at[g], cr.at[g], other_c)

    def small_to(t):
        return remote(smalls.at[:, c, z], smalls.at[:, c, z], ws.at[t], wr.at[z], {"ctx": t})

    def small_from(t):
        return remote(smalls.at[:, c, t], smalls.at[:, c, t], ws.at[t], wr.at[t], {"ctx": t})

    def rows_of(g):
        block = owns[g].shape[2]
        return 32 if block % 32 == 0 else block

    def each_tile(g, body):
        rows = rows_of(g)
        per = owns[g].shape[2] // rows

        def step(i, _):
            body(i // per, pl.ds(pl.multiple_of((i % per) * rows, 8), rows))
            return 0

        lax.fori_loop(0, 2 * per, step, 0)

    order = inward(nz)
    mine = pltpu.make_async_copy(small, smalls.at[y, c, z], loc.at[ng + 1, 0])
    mine.start()
    line = remote(small, smalls.at[y, c, z], ts.at[0], tr.at[0], other_y)
    line.start()
    for t in order:
        for g in range(ng):
            across(g, t).start()
            own(g, t).start()
    mine.wait()
    remote(small, smalls.at[1 - y, c, z], ts.at[0], tr.at[0], other_y).wait_recv()
    for t in range(nz):

        @pl.when(z != t)
        def _(t=t):
            small_to(t).start()

    for t in order:
        for g in range(ng):
            side = (z > t).astype(jnp.int32)
            first = ((z == 0) & (z < t)) | ((z == nz - 1) & (z > t))

            @pl.when(first)
            def _(g=g, t=t, side=side):
                def clear(k, rows):
                    ins[g][side, t, k, rows] = jnp.zeros(
                        (rows_of(g), ins[g].shape[-1]), BF16
                    )

                each_tile(g, clear)

            own(g, t).wait()
            across(g, t).wait_recv()

            @pl.when((z < t) & (z > 0))
            def _(g=g, t=t):
                up(g, t).wait_recv()

            @pl.when((z > t) & (z < nz - 1))
            def _(g=g, t=t):
                down(g, t).wait_recv()

            @pl.when(z != t)
            def _(g=g, t=t, side=side):
                def add(k, rows):
                    sends[g][t, k, rows] = (
                        owns[g][t, k, rows].astype(F32)
                        + lands[g][t, k, rows].astype(F32)
                        + ins[g][side, t, k, rows].astype(F32)
                    ).astype(BF16)

                each_tile(g, add)

            @pl.when(z < t)
            def _(g=g, t=t):
                up(g, t).start()

            @pl.when(z > t)
            def _(g=g, t=t):
                down(g, t).start()

    for g in range(ng):

        @pl.when(z > 0)
        def _(g=g):
            up(g, z).wait_recv()

        @pl.when(z < nz - 1)
        def _(g=g):
            down(g, z).wait_recv()

        @pl.when(z == 0)
        def _(g=g):
            def clear(k, rows):
                ins[g][0, z, k, rows] = jnp.zeros((rows_of(g), ins[g].shape[-1]), BF16)

            each_tile(g, clear)

        @pl.when(z == nz - 1)
        def _(g=g):
            def clear(k, rows):
                ins[g][1, z, k, rows] = jnp.zeros((rows_of(g), ins[g].shape[-1]), BF16)

            each_tile(g, clear)

        def add(k, rows, g=g):
            totals[g][k, rows] = (
                owns[g][z, k, rows].astype(F32)
                + lands[g][z, k, rows].astype(F32)
                + ins[g][0, z, k, rows].astype(F32)
                + ins[g][1, z, k, rows].astype(F32)
            )

        each_tile(g, add)
        swap(g).start()
        keep(g).start()

    for t in range(nz):

        @pl.when(z != t)
        def _(t=t):
            small_from(t).wait_recv()

    plane = remote(smalls.at[:, c], smalls.at[:, c], ts.at[1], tr.at[1], other_c)
    plane.start()
    remote(smalls.at[:, 1 - c], smalls.at[:, 1 - c], ts.at[1], tr.at[1], other_c).wait_recv()
    for g in range(ng):
        swap_from(g).wait_recv()
        keep(g).wait()
        swap(g).wait_send()
    line.wait_send()
    plane.wait_send()
    for t in range(nz):

        @pl.when(z != t)
        def _(t=t):
            small_to(t).wait_send()

        for g in range(ng):
            across(g, t).wait_send()

            @pl.when(z < t)
            def _(g=g, t=t):
                up(g, t).wait_send()

            @pl.when(z > t)
            def _(g=g, t=t):
                down(g, t).wait_send()


def scatter_all(parts, small, ny, nz):
    ng = len(parts)
    dma = pltpu.SemaphoreType.DMA
    anywhere = pl.BlockSpec(memory_space=pl.ANY)
    shapes = [jax.ShapeDtypeStruct((2,) + part.shape[3:], F32) for part in parts]
    shapes.append(jax.ShapeDtypeStruct((ny, 2, nz) + small.shape, small.dtype))
    slots = [pltpu.VMEM((nz, 2) + part.shape[3:], BF16) for part in parts]
    results = pl.pallas_call(
        functools.partial(scatter_kernel, nz, ng),
        out_shape=shapes,
        in_specs=[anywhere] * (ng + 1),
        out_specs=[anywhere] * (ng + 1),
        scratch_shapes=slots * 2
        + [pltpu.VMEM((2, nz, 2) + part.shape[3:], BF16) for part in parts]
        + slots
        + [pltpu.VMEM((2,) + part.shape[3:], F32) for part in parts]
        + [
            dma((ng + 2, max(nz, ng))),
            dma((ng, nz)),
            dma((ng, nz)),
            dma((2, ng, nz)),
            dma((2, ng, nz)),
            dma((ng,)),
            dma((ng,)),
            dma((nz,)),
            dma((nz,)),
            dma((2,)),
            dma((2,)),
        ],
        name="scatter_all",
        compiler_params=pltpu.CompilerParams(
            collective_id=4, has_side_effects=True, vmem_limit_bytes=VMEM_LIMIT
        ),
    )(*parts, small)
    return results[:ng], results[ng]


def halves(matrix):
    half = matrix.shape[1] // 2
    return jnp.stack([matrix[:, :half], matrix[:, half:]])


def join(halved):
    return jnp.concatenate([halved[0], halved[1]], axis=1)


def on_device(
    ny,
    nz,
    layer_input,
    segments,
    positions,
    attn_gain,
    query_proj,
    key_proj,
    value_proj,
    out_proj,
    mlp_gain,
    gate_proj,
    up_proj,
    down_proj,
    out_grad,
):
    _, span, width = layer_input.shape
    block = query_proj.shape[0]
    groups = HQ // HK
    score_scale = DH ** (-0.5)
    y = lax.axis_index("fy")
    c = lax.axis_index("pr")
    z = lax.axis_index("ctx")
    rows_per = span // LANES
    small = jnp.concatenate(
        [
            jnp.pad(attn_gain.astype(F32), (0, LANES - block))[None],
            jnp.pad(mlp_gain.astype(F32), (0, LANES - block))[None],
            segments.astype(F32).reshape(rows_per, LANES),
            positions.astype(F32).reshape(rows_per, LANES),
            jnp.zeros((6 - 2 * rows_per, LANES), F32),
        ]
    )
    qkv_raw = jnp.concatenate([halves(query_proj), halves(key_proj), halves(value_proj)], axis=2)
    raws = (
        qkv_raw,
        halves(out_proj.T),
        halves(gate_proj),
        halves(up_proj),
        halves(down_proj.T),
    )
    layer_rows = layer_input.reshape(span, width)
    pieces, smalls, rows_both, grads_both = pair_swap(
        raws, small, layer_rows, out_grad.reshape(span, width), ny, nz
    )
    attn_gain_full = smalls[:, :, :, 0, :block].reshape(width)
    mlp_gain_full = smalls[:, :, :, 1, :block].reshape(width)
    mine = lax.dynamic_index_in_dim(smalls, y, 0, keepdims=False)
    segment_all = mine[:, :, 2 : 2 + rows_per].reshape(2, nz, 1, span).astype(jnp.int32)
    position_all = mine[:, :, 2 + rows_per : 2 + 2 * rows_per].reshape(2, nz, span)
    here = lax.dynamic_index_in_dim(position_all, z, 1, keepdims=False)
    segments_here = lax.dynamic_index_in_dim(segment_all, z, 1, keepdims=False)
    q_seg = jnp.tile(segments_here.reshape(2, span), (1, groups))[:, :, None]

    total_rows = 2 * span
    inputs = rows_both.reshape(total_rows, width).astype(F32)
    scale_attn = inverse_rms(inputs)
    normed_attn = (inputs * scale_attn * attn_gain_full).astype(BF16)
    cos_half, sin_half = rotary_tables(here.reshape(total_rows))
    blank = jnp.zeros((total_rows, LANES // 2 - DH // 2), F32)
    cos_wide = jnp.concatenate([cos_half, blank, cos_half, blank], axis=1)
    sin_wide = jnp.concatenate([-sin_half, blank, sin_half, blank], axis=1)
    lane_from = jnp.arange(4 * DH)
    lane_to = lane_from // DH * LANES + lane_from % DH
    lane_to = jnp.where(lane_from % DH < DH // 2, lane_to, lane_to + LANES // 2 - DH // 2)
    spread_mat = (lane_to[:, None] == jnp.arange(4 * LANES)[None]).astype(BF16)
    results = forward(
        pieces,
        normed_attn,
        layer_rows,
        cos_wide,
        sin_wide,
        q_seg,
        segment_all,
        spread_mat,
        mlp_gain_full.reshape(1, width),
        ny,
        nz,
    )
    qkv_full, out_full, gate_full, up_full, down_full = (
        piece.reshape(width, piece.shape[-1]) for piece in results[:5]
    )
    q_items, k_items, v_items, mixed_wide, mixed_rows, row_lse, residual_own, normed_mlp = results[5:]
    normed_mlp = normed_mlp.reshape(total_rows, width)
    gate_pre = jnp.dot(normed_mlp, gate_full, preferred_element_type=F32)
    up_pre = jnp.dot(normed_mlp, up_full, preferred_element_type=F32)
    activated = jax.nn.silu(gate_pre)
    hidden = (activated * up_pre).astype(BF16)

    def own_rows(both):
        return lax.dynamic_slice_in_dim(both.reshape(total_rows, width), c * span, span, 0)

    mlp_out = sum_parts(contract(hidden, down_full, 1, 1).reshape(2, span, width))
    layer_output = (residual_own + own_rows(mlp_out)).astype(BF16)

    upstream_low = grads_both.reshape(total_rows, width)
    hidden_grad = jnp.dot(upstream_low, down_full, preferred_element_type=F32)
    down_part = contract(upstream_low, hidden, 0, 0).astype(BF16)
    sigmoid_gate = jax.nn.sigmoid(gate_pre)
    gate_grad = (
        hidden_grad * up_pre * sigmoid_gate * (1.0 + gate_pre * (1.0 - sigmoid_gate))
    ).astype(BF16)
    up_grad = (hidden_grad * activated).astype(BF16)
    normed_mlp_grad = own_rows(
        sum_parts(
            (contract(gate_grad, gate_full, 1, 1) + contract(up_grad, up_full, 1, 1)).reshape(
                2, span, width
            )
        )
    )
    gate_part = contract(normed_mlp, gate_grad, 0, 0).astype(BF16)
    up_part = contract(normed_mlp, up_grad, 0, 0).astype(BF16)
    scale_mlp = inverse_rms(residual_own)
    mlp_gain_term = jnp.sum(normed_mlp_grad * residual_own * scale_mlp, axis=0)
    upstream = out_grad.reshape(span, width).astype(F32)
    residual_grad = norm_back(upstream, normed_mlp_grad * mlp_gain_full, residual_own, scale_mlp)
    residual_low = core_both(residual_grad.astype(BF16)).reshape(total_rows, width)
    out_part = contract(residual_low, mixed_rows, 0, 0).astype(BF16)
    mixed_grad = jnp.dot(residual_low, out_full, preferred_element_type=F32).astype(BF16)

    def to_items(rows):
        wide = jnp.dot(rows, spread_mat, preferred_element_type=F32).astype(BF16)
        return wide.reshape(2, span, 2, groups, LANES).transpose(0, 2, 3, 1, 4).reshape(
            4, groups * span, LANES
        )

    def narrow(wide):
        return contract(wide.astype(BF16), spread_mat, 1, 1)

    grad_items = to_items(mixed_grad)
    reached = (jnp.arange(nz) <= z)[:, None, None, None]
    k_all = jnp.where(reached, k_items, jnp.zeros_like(k_items)).transpose(1, 0, 2, 3).reshape(
        4, nz * span, LANES
    )
    v_all = jnp.where(reached, v_items, jnp.zeros_like(v_items)).transpose(1, 0, 2, 3).reshape(
        4, nz * span, LANES
    )
    query_index = jnp.tile(z * span + jnp.arange(span), groups)
    key_index = jnp.arange(nz * span)
    key_segments = jnp.repeat(segment_all.reshape(2, nz * span), 2, axis=0)
    query_segments = jnp.repeat(q_seg[:, :, 0], 2, axis=0)

    def backward_block(item):
        bq, bk, bv, ks, qs, blse, bg = item
        scores = jnp.einsum("qd,kd->qk", bq, bk, preferred_element_type=F32) * score_scale
        allowed = (qs[:, None] == ks[None, :]) & (query_index[:, None] >= key_index[None, :])
        probs = jnp.where(allowed, jnp.exp(scores - blse[:, :1]), 0.0)
        prob_grad = jnp.einsum("qd,kd->qk", bg, bv, preferred_element_type=F32)
        row_delta = jnp.sum(prob_grad * probs, axis=1, keepdims=True)
        score_grad = (probs * (prob_grad - row_delta)).astype(BF16)
        value_grad = jnp.einsum("qk,qd->kd", probs.astype(BF16), bg, preferred_element_type=F32)
        key_grad = jnp.einsum("qk,qd->kd", score_grad, bq, preferred_element_type=F32) * score_scale
        query_grad = jnp.dot(score_grad, bk, preferred_element_type=F32) * score_scale
        return (query_grad, key_grad, value_grad)

    query_grads, key_grads, value_grads = lax.map(
        backward_block, (q_items, k_all, v_all, key_segments, query_segments, row_lse, grad_items)
    )
    kv_wide = jnp.concatenate(
        [
            key_grads.reshape(2, 2, nz, span, LANES).transpose(2, 0, 3, 1, 4).reshape(nz * 2 * span, 2 * LANES),
            value_grads.reshape(2, 2, nz, span, LANES).transpose(2, 0, 3, 1, 4).reshape(nz * 2 * span, 2 * LANES),
        ],
        axis=1,
    )
    kv_back = keys_down(narrow(kv_wide).astype(BF16).reshape(nz, 2, span, 4 * DH), nz).reshape(
        total_rows, 4 * DH
    )
    kv_width = 2 * DH
    cos_t = cos_half[:, None, :]
    sin_t = sin_half[:, None, :]
    swapped = jnp.concatenate([query_grads[:, :, LANES // 2 :], query_grads[:, :, : LANES // 2]], axis=2)
    cos_i = jnp.repeat(jnp.tile(cos_wide.reshape(2, span, LANES), (1, groups, 1)), 2, axis=0)
    sin_i = jnp.repeat(jnp.tile(sin_wide.reshape(2, span, LANES), (1, groups, 1)), 2, axis=0)
    q_un = (query_grads * cos_i - swapped * sin_i).astype(BF16)
    q_un = q_un.reshape(2, 2, groups, span, LANES).transpose(0, 3, 1, 2, 4).reshape(total_rows, 4 * LANES)
    query_grad_rows = narrow(q_un).astype(BF16)
    key_grad_rows = (
        unrotate(kv_back[:, :kv_width].astype(F32).reshape(total_rows, 2, DH), cos_t, sin_t)
        .astype(BF16)
        .reshape(total_rows, -1)
    )
    qkv_grad_rows = jnp.concatenate([query_grad_rows, key_grad_rows, kv_back[:, kv_width:]], axis=1)
    qkv_part = contract(normed_attn, qkv_grad_rows, 0, 0).astype(BF16)
    normed_attn_grad = own_rows(
        sum_parts(contract(qkv_grad_rows, qkv_full, 1, 1).reshape(2, span, width))
    )
    inputs_own = layer_rows.astype(F32)
    scale_own = inverse_rms(inputs_own)
    attn_gain_term = jnp.sum(normed_attn_grad * inputs_own * scale_own, axis=0)
    input_grad = norm_back(
        residual_grad, normed_attn_grad * attn_gain_full, inputs_own, scale_own
    ).astype(BF16)

    parts = tuple(
        part.reshape(ny, 2, nz, block, part.shape[1])
        for part in (down_part, gate_part, up_part, out_part, qkv_part)
    )
    gains = jnp.stack([attn_gain_term, mlp_gain_term]).reshape(2 * width // LANES, LANES)
    reduced, gains_all = scatter_all(parts, gains, ny, nz)
    down_g, gate_g, up_g, out_g, qkv_g = reduced
    gain_sum = jnp.sum(gains_all, axis=(0, 1, 2)).reshape(2, width)
    place = ((y * 2 + c) * nz + z) * block
    gain_own = lax.dynamic_slice_in_dim(gain_sum, place, block, 1)
    q_width = 4 * DH
    return (
        layer_output.reshape(1, span, width),
        input_grad.reshape(1, span, width),
        gain_own[0],
        join(qkv_g[:, :, :q_width]),
        join(qkv_g[:, :, q_width : q_width + kv_width]),
        join(qkv_g[:, :, q_width + kv_width :]),
        join(out_g).T,
        gain_own[1],
        join(gate_g),
        join(up_g),
        join(down_g).T,
    )


def core_both(rows):
    def kernel(own, both, ss, rs, ls):
        c = lax.axis_index("pr")
        greet([({"pr": 1 - c}, None)], 1)
        local = pltpu.make_async_copy(own, both.at[c], ls.at[0])
        copy = remote(own, both.at[c], ss.at[0], rs.at[0], {"pr": 1 - c})
        local.start()
        copy.start()
        copy.wait()
        local.wait()

    dma = pltpu.SemaphoreType.DMA
    vmem = pl.BlockSpec(memory_space=pltpu.VMEM)
    return pl.pallas_call(
        kernel,
        out_shape=jax.ShapeDtypeStruct((2,) + rows.shape, rows.dtype),
        in_specs=[vmem],
        out_specs=vmem,
        scratch_shapes=[dma((1,)), dma((1,)), dma((1,))],
        name="core_both",
        compiler_params=pltpu.CompilerParams(collective_id=5, has_side_effects=True),
    )(rows)


def solution(mesh):
    sizes = mesh.shape
    ny, nz = sizes["fsdp"] // 2, sizes["ctx"]
    inner = Mesh(
        mesh.devices.reshape(ny, 2, nz, sizes["tp"]), ("fy", "pr", "ctx", "tp")
    )
    seqs = ("fy", "pr")
    rows = P(seqs, "ctx", None)
    marks = P(seqs, "ctx")
    gain = P(GROUP)
    tall = P(GROUP, "tp")
    wide = P("tp", GROUP)
    return jax.shard_map(
        functools.partial(on_device, ny, nz),
        mesh=inner,
        in_specs=(
            rows, marks, marks, gain, tall, tall, tall, wide, gain, tall, tall, wide, rows,
        ),
        out_specs=(rows, rows, gain, tall, tall, tall, wide, gain, tall, tall, wide),
        check_vma=False,
    )
```

time: 1370 us -> 645 us (0.47)
  waiting for transfers between devices: 1010 us -> 0 us
  Pallas kernels: 0 us -> 491 us
  blocking collectives: 133 us -> 0 us
  matrix products: 126 us -> 73.5 us
  local copies, waits for them, and re-layouts: 56.2 us -> 30.3 us
  other arithmetic: 20.3 us -> 38 us
    reduce_scatter x9 -> x0, waiting for transfers between devices: 674 us -> none  [the longest x1 140 us: on_device(): lax.psum_scatter(gate_weight_grad, ('fsdp', 'ctx'), scatter_dimension=0,...]
    pallas_call x0 -> x8, Pallas kernels: none -> 491 us  [the longest x1 169 us: scatter_all(): pl.pallas_call(functools.partial(scatter_kernel, nz, ng), out_shape=shape...]
    all_gather x7 -> x0, waiting for transfers between devices: 220 us -> none  [the longest x1 63.7 us: on_device(): lax.all_gather(gate_proj, ('fsdp', 'ctx'), axis=0, tiled=True)]
    psum x3 -> x0, waiting for transfers between devices: 108 us -> none  [the longest x1 48.6 us: on_device(): lax.psum(contract(gate_grad, mlp_back[1], 1, 1) + contract(up_grad, mlp_b...]
    unnamed x2 -> x0, blocking collectives: 88.2 us -> none
    all_gather x3 -> x0, blocking collectives: 45 us -> none  [the longest x1 20.8 us: on_device(): lax.all_gather(value_low, 'ctx', axis=1, tiled=True)]
    dot_general x14 -> x11, matrix products: 63.3 us -> 35.5 us  [contract(): lax.dot_general(left, right, (((left_dim,), (right_dim,)), ((), ())), pre...]
    dot_general x35 -> x24, matrix products: 63 us -> 37.9 us  [the longest x4 7.24 us: backward_block(): jnp.einsum('qd,kd->qk', bq, bk, preferred_element_type=F32) * score_scale]
  transfers between devices with their start and end apart: 19 -> 0, of which waited for: 18 -> 0; matrix products, arithmetic and copies ran while one was open for 9% -> 0% of each run, Pallas kernels for 0% -> 0%
where the time goes in v1:
time: 645 us; the launch traced here: 635 us
  Pallas kernels  491 us (76%)
  matrix products  73.5 us (11%)
  other arithmetic  38 us (6%)
  local copies, waits for them, and re-layouts  30.3 us (5%)
    pallas_call x1, Pallas kernels, scatter_all(): pl.pallas_call(functools.partial(scatter_kernel, nz, ng), out_shape=shape...  169 us
    pallas_call x1, Pallas kernels, forward(): pl.pallas_call(functools.partial(forward_kernel, nz, items, DH ** (-0.5))...  136 us
    pallas_call x1, Pallas kernels, keys_down(): pl.pallas_call(functools.partial(keys_down_kernel, nz), out_shape=jax.Sha...  86 us
    pallas_call x3, Pallas kernels, sum_parts(): pl.pallas_call(sum_kernel, out_shape=jax.ShapeDtypeStruct(part.shape, F32...  80.8 us
    dot_general x11, matrix products, contract(): lax.dot_general(left, right, (((left_dim,), (right_dim,)), ((), ())), pre...  35.5 us
    pallas_call x1, Pallas kernels, pair_swap(): pl.pallas_call(functools.partial(pair_kernel, nz, ng), out_shape=shapes,...  14.7 us

profile of v1, /device:TPU:11, one launch (start us, length us, event | category | flops | bytes accessed | tf_op | source)
XLA Modules:
  0.0 635.3 jit_solution(6677685398484105319)
XLA Ops:
  7.8 14.7 %pair_swap.1 = (bf16[2,96,768]{2,1,0:T(8,128)(2,1)}, bf16[2,96,384]{2,1,0:T(8,128)(2,1)}, bf16[2,96,1024]{2,1,0:T(8,128)(2,1)}, bf16[2,96,1024]{2,1,0:T(8,128)(2...) custom-call(bf16[2,96,768]{2,1,0:T(8,128)(2,1)} %maximum_maximum_fus, ...), custom_call_target="tpu_custom_call" | custom-call | tf_op jit(solution)/shard_map/pair_swap/pallas_call | solution.py:214
  27.1 1.6 fusion.32.refs_5_
  31.4 136.2 %forward.1 = (bf16[2,2,4,96,768]{4,3,2,1,0:T(8,128)(2,1)}, bf16[2,2,4,96,384]{4,3,2,1,0:T(8,128)(2,1)}, bf16[2,2,4,96,1024]{4,3,2,1,0:T(8,128)(2,1)}, bf16[2,2,4...) custom-call(bf16[2,96,768]{2,1,0:T(8,128)(2,1)} %get-tuple-element.1, ...), custom_call_target="tpu_custom_call" | custom-call | tf_op jit(solution)/shard_map/forward/pallas_call | solution.py:592
  167.7 4.3 fusion.87
  172.1 1.8 fusion.86
  174.4 2.5 multiply_convert_fusion.1
  178.0 3.6 fusion.88.part
  181.5 26.2 %sum_parts.3 = f32[2,256,1536]{2,1,0:T(8,128)} custom-call(f32[2,256,1536]{2,1,0:T(8,128)} %fusion.88.part), custom_call_target="tpu_custom_call" | custom-call | tf_op jit(solution)/shard_map/sum_parts/pallas_call | solution.py:729
  207.8 3.9 fusion.89
  211.7 3.5 convolution_add_fusion
  215.2 26.7 %sum_parts.4 = f32[2,256,1536]{2,1,0:T(8,128)} custom-call(f32[2,256,1536]{2,1,0:T(8,128)} %bitcast.295), custom_call_target="tpu_custom_call" | custom-call | tf_op jit(solution)/shard_map/sum_parts/pallas_call | solution.py:729
  242.1 2.0 multiply_reduce_fusion.2
  244.6 12.4 %fusion.83 = (bf16[256,1536]{1,0:T(8,128)(2,1)}, f32[256,1536]{1,0:T(8,128)}, bf16[1,256,1536]{2,1,0:T(8,128)(2,1)}) fusion(f32[256]{0:T(256)S(1)} %broadcast_multiply_fusion.1, f32[256,1536]{1,0:T(8,128)S(1)} %copy-done.1, f32[256]{0:T(256)S(1)} %get-tuple-element.276, f32[1536]{0:T(1024)S(1)} %mul.323, f32[512,1536]{1,0:T(8,128)S(1)} %bitcast.287, ...), kind=kLoop, calls=%fused_computation.210 | loop fusion | flops 3932160 | bytes 8659972 | tf_op jit(solution)/shard_map/convert_element_type | solution.py:1106
  257.0 4.8 core_both.1
  261.8 2.7 convolution_convert_fusion.6
  265.7 1.4 select_bitcast_fusion
  268.5 36.4 %while.15 = (s32[]{:T(128)}, f32[4,512,128]{2,1,0:T(8,128)S(1)}, bf16[4,1024,128]{2,1,0:T(8,128)(2,1)}, bf16[4,1024,128]{2,1,0:T(8,128)(2,1)}, s32[4,512]{1,0:T(...) while((s32[]{:T(128)}, f32[4,512,128]{2,1,0:T(8,128)S(1)}, ...), condition=%wide.region_6.7_spmd.clone, body=%wide.region_4.6_spmd.clone.sunk | while | flops 677576192 | bytes 27830464 | solution.py:1145
  269.7 1.8 exponential_select_fusion.2
  273.3 1.5 fusion.137
  274.8 1.6 fusion.136
  276.4 1.2 fusion.138
  278.8 1.8 exponential_select_fusion.2
  282.4 1.5 fusion.137
  283.9 1.6 fusion.136
  285.5 1.2 fusion.138
  287.9 1.8 exponential_select_fusion.2
  291.5 1.5 fusion.137
  293.0 1.6 fusion.136
  294.6 1.2 fusion.138
  297.0 1.8 exponential_select_fusion.2
  300.6 1.5 fusion.137
  302.1 1.6 fusion.136
  303.7 1.2 fusion.138
  308.5 2.5 copy.46
  312.4 2.6 convolution_convert_fusion.5
  315.0 86.0 %keys_down.1 = bf16[2,256,384]{2,1,0:T(8,128)(2,1)} custom-call(bf16[4,2,256,384]{3,2,1,0:T(8,128)(2,1)} %bitcast.310), custom_call_target="tpu_custom_call" | custom-call | tf_op jit(solution)/shard_map/keys_down/pallas_call | solution.py:661
  401.0 1.2 fusion.85
  402.9 4.8 fusion.48.part
  407.6 27.9 %sum_parts.5 = f32[2,256,1536]{2,1,0:T(8,128)} custom-call(f32[2,256,1536]{2,1,0:T(8,128)} %fusion.48.part), custom_call_target="tpu_custom_call" | custom-call | tf_op jit(solution)/shard_map/sum_parts/pallas_call | solution.py:729
  435.9 2.0 fusion.43
  438.6 4.0 convolution_convert_fusion.3
  442.6 2.0 convolution_convert_fusion.4
  444.7 3.5 convolution_convert_fusion.1
  448.2 3.5 convolution_convert_fusion
  451.8 3.6 convolution_convert_fusion.2
  455.3 168.7 %scatter_all.1 = (f32[2,96,1024]{2,1,0:T(8,128)}, f32[2,96,1024]{2,1,0:T(8,128)}, f32[2,96,1024]{2,1,0:T(8,128)}, f32[2,96,384]{2,1,0:T(8,128)}, f32[2,96,768]{2,1,0:T(8,128)}, /*index=5*/f32[2,2,4,24,128]{4,3,2,1,0:T(8,128)}) custom-call(bf16[2,2,4,96,1024]{4,3,2,1,0:T(8,128)(2,1)} %bitcast.299, bf16[2,2,4,96,1024]{4,3,2,1,0:T(8,128)(2,1)} %bitcast.297, ...), custom_call_target="tpu_custom_call" | custom-call | tf_op jit(solution)/shard_map/scatter_all/pallas_call | solution.py:950
  624.1 1.3 slice_bitcast_fusion.1
  632.1 2.7 fusion.47
  (237 shorter events, 43.9 us)
Async XLA Ops:
  0.6 3.9 copy-start.17
  1.7 3.9 copy-start.18
  4.5 1.9 copy-start.21
  4.6 2.6 copy-start.26
  4.6 2.5 copy-start.27
  4.6 2.5 copy-start.24
  4.6 2.6 copy-start.25
  22.5 4.2 copy-start.3
  23.4 5.3 copy-start.22
  24.4 4.3 copy-start.7
  167.7 4.3 copy-start.29
  167.7 4.3 copy-start.33
  172.1 1.9 copy-start.30
  172.1 2.3 copy-start.31
  177.0 30.8 %copy-start.40 = (bf16[512,1024]{1,0:T(8,128)(2,1)}, bf16[512,1024]{1,0:T(8,128)(2,1)S(1)}, u32[]{:S(2)}) copy-start(bf16[512,1024]{1,0:T(8,128)(2,1)S(1)} %get-tuple-element.222) | copy-start | bytes 3145732
  177.0 34.7 %copy-start.42 = (bf16[512,1024]{1,0:T(8,128)(2,1)}, bf16[512,1024]{1,0:T(8,128)(2,1)S(1)}, u32[]{:S(2)}) copy-start(bf16[512,1024]{1,0:T(8,128)(2,1)S(1)} %get-tuple-element.221) | copy-start | bytes 3145732
  207.8 3.9 copy-start.28
  215.2 26.7 %copy-start.1 = (f32[256,1536]{1,0:T(8,128)S(1)}, f32[256,1536]{1,0:T(8,128)}, u32[]{:S(2)}) copy-start(f32[256,1536]{1,0:T(8,128)} %get-tuple-element.113) | copy-start | bytes 4718596
  241.9 2.3 copy-start.6
  242.1 2.4 copy-start.2
  257.0 4.8 copy-start.35
  267.1 1.3 copy-start.23
  272.0 1.2 copy-start.11
  274.8 1.6 copy-start.12
  281.1 1.2 copy-start.11
  283.9 1.6 copy-start.12
  290.2 1.2 copy-start.11
  293.0 1.6 copy-start.12
  299.3 1.2 copy-start.11
  302.1 1.6 copy-start.12
  308.5 94.4 %copy-start.39 = (bf16[512,384]{1,0:T(8,128)(2,1)}, bf16[512,384]{1,0:T(8,128)(2,1)S(1)}, u32[]{:S(2)}) copy-start(bf16[512,384]{1,0:T(8,128)(2,1)S(1)} %convolution_convert_fusion.7) | copy-start | bytes 1179652
  308.5 2.6 copy-start.13
  315.0 87.3 %copy-start.8 = (f32[512,48]{1,0:T(8,128)S(1)}, f32[512,48]{1,0:T(8,128)}, u32[]{:S(2)}) copy-start(f32[512,48]{1,0:T(8,128)} %copy-done.7) | copy-start | bytes 294916
  407.6 28.0 %copy-start = (bf16[1,256,1536]{2,1,0:T(8,128)(2,1)S(1)}, bf16[1,256,1536]{2,1,0:T(8,128)(2,1)}, u32[]{:S(2)}) copy-start(bf16[1,256,1536]{2,1,0:T(8,128)(2,1)} %param.15) | copy-start | bytes 2359300
  435.6 3.0 copy-start.5
  438.6 4.0 copy-start.9
  438.6 4.0 copy-start.36
  442.6 2.1 copy-start.34
  442.6 2.1 copy-start.41
  444.7 3.5 copy-start.43
  448.2 3.5 copy-start.32
  448.2 3.5 copy-start.38
  624.0 2.2 copy-start.16
  625.3 2.0 copy-start.15
  626.3 2.0 copy-start.19
  627.3 1.8 copy-start.14
  628.3 3.2 copy-start.20
  628.3 3.8 copy-start.4
  (2 other events, 2.2 us)

commit v2 on v1

--- a/solution.py
+++ b/solution.py
@@ -25,32 +25,6 @@
     return (jnp.cos(angles), jnp.sin(angles))
 
 
-def rotate(field_in, cos_table, sin_table):
-    half_dim = field_in.shape[-1] // 2
-    front_half = field_in[..., :half_dim]
-    back_half = field_in[..., half_dim:]
-    return jnp.concatenate(
-        [
-            front_half * cos_table - back_half * sin_table,
-            back_half * cos_table + front_half * sin_table,
-        ],
-        axis=-1,
-    )
-
-
-def unrotate(field_in, cos_table, sin_table):
-    half_dim = field_in.shape[-1] // 2
-    front_half = field_in[..., :half_dim]
-    back_half = field_in[..., half_dim:]
-    return jnp.concatenate(
-        [
-            front_half * cos_table + back_half * sin_table,
-            back_half * cos_table - front_half * sin_table,
-        ],
-        axis=-1,
-    )
-
-
 def inverse_rms(values):
     return lax.rsqrt(jnp.mean(values * values, axis=-1, keepdims=True) + EPS)
 
@@ -58,46 +32,6 @@
 def contract(left, right, left_dim, right_dim):
     return lax.dot_general(
         left, right, (((left_dim,), (right_dim,)), ((), ())), preferred_element_type=jnp.float32
-    )
-
-
-def norm_back(upstream, inner, values, scale_rows):
-    cubed = scale_rows * scale_rows * scale_rows
-    return (
-        upstream
-        + scale_rows * inner
-        - values * cubed * jnp.mean(inner * values, axis=-1, keepdims=True)
-    )
-
-
-def to_blocks(matrix, seq_count, local_kv, groups):
-    span = matrix.shape[0] // seq_count
-    shaped = matrix.reshape(seq_count, span, local_kv, groups, DH).transpose(0, 2, 1, 3, 4)
-    return shaped.reshape(seq_count * local_kv, span * groups, DH)
-
-
-def from_blocks(blocks, seq_count, local_kv, groups):
-    span = blocks.shape[1] // groups
-    shaped = blocks.reshape(seq_count, local_kv, span, groups, DH).transpose(0, 2, 1, 3, 4)
-    return shaped.reshape(seq_count * span, local_kv * groups * DH)
-
-
-def seq_items(matrix, local_kv):
-    seq_count = matrix.shape[0]
-    length = matrix.shape[1]
-    return (
-        matrix.reshape(seq_count, length, local_kv, DH)
-        .transpose(0, 2, 1, 3)
-        .reshape(seq_count * local_kv, length, DH)
-    )
-
-
-def from_items(items, seq_count, local_kv):
-    length = items.shape[1]
-    return (
-        items.reshape(seq_count, local_kv, length, DH)
-        .transpose(0, 2, 1, 3)
-        .reshape(seq_count, length, local_kv * DH)
     )
 
 
@@ -615,130 +549,6 @@
     )(*pieces, normed, rows, cos, sin, q_seg, k_seg, spread_mat, gain)
 
 
-def keys_down_kernel(nz, grads, out, sends, lands, ds, dr):
-    z = lax.axis_index("ctx")
-    greet(
-        [({"ctx": z + 1}, z < nz - 1), ({"ctx": z - 1}, z > 0)],
-        (z < nz - 1).astype(jnp.int32) + (z > 0).astype(jnp.int32),
-    )
-
-    def down(b, t):
-        return remote(sends.at[t, b], lands.at[t, b], ds.at[b, t], dr.at[b, t], {"ctx": z - 1})
-
-    for t in range(nz):
-        for b in range(2):
-
-            @pl.when(z >= t)
-            def _(b=b, t=t):
-                @pl.when(z < nz - 1)
-                def _():
-                    down(b, t).wait_recv()
-                    sends[t, b] = (grads[t, b].astype(F32) + lands[t, b].astype(F32)).astype(BF16)
-
-                @pl.when(z == nz - 1)
-                def _():
-                    sends[t, b] = grads[t, b]
-
-                @pl.when(z > t)
-                def _():
-                    down(b, t).start()
-
-                @pl.when(z == t)
-                def _():
-                    out[b] = sends[t, b]
-
-    for t in range(nz):
-        for b in range(2):
-
-            @pl.when(z > t)
-            def _(b=b, t=t):
-                down(b, t).wait_send()
-
-
-def keys_down(grads, nz):
-    dma = pltpu.SemaphoreType.DMA
-    vmem = pl.BlockSpec(memory_space=pltpu.VMEM)
-    return pl.pallas_call(
-        functools.partial(keys_down_kernel, nz),
-        out_shape=jax.ShapeDtypeStruct(grads.shape[1:], BF16),
-        in_specs=[vmem],
-        out_specs=vmem,
-        scratch_shapes=[
-            pltpu.VMEM(grads.shape, BF16),
-            pltpu.VMEM(grads.shape, BF16),
-            dma((2, nz)),
-            dma((2, nz)),
-        ],
-        name="keys_down",
-        compiler_params=pltpu.CompilerParams(
-            collective_id=2, has_side_effects=True, vmem_limit_bytes=VMEM_LIMIT
-        ),
-    )(grads)
-
-
-CHUNKS = 4
-
-
-def sum_kernel(part, out, core_send, core_land, x_send, x_land, cs, cr, xs, xr, fs, fr):
-    c = lax.axis_index("pr")
-    x = lax.axis_index("tp")
-    other_c = {"pr": 1 - c}
-    other_x = {"tp": 1 - x}
-    greet([(other_c, None), (other_x, None)], 2)
-    rows = part.shape[1] // CHUNKS
-
-    def core(i):
-        return remote(core_send.at[i], core_land.at[i], cs.at[i], cr.at[i], other_c)
-
-    def across(i):
-        return remote(x_send.at[i], x_land.at[i], xs.at[i], xr.at[i], other_x)
-
-    def final(i):
-        piece = out.at[c, pl.ds(i * rows, rows)]
-        return remote(piece, piece, fs.at[i], fr.at[i], other_c)
-
-    def final_from(i):
-        piece = out.at[1 - c, pl.ds(i * rows, rows)]
-        return remote(piece, piece, fs.at[i], fr.at[i], other_c)
-
-    for i in range(CHUNKS):
-        core_send[i] = part[1 - c, pl.ds(i * rows, rows)].astype(BF16)
-        core(i).start()
-    for i in range(CHUNKS):
-        core(i).wait_recv()
-        x_send[i] = (
-            part[c, pl.ds(i * rows, rows)].astype(F32) + core_land[i].astype(F32)
-        ).astype(BF16)
-        across(i).start()
-    for i in range(CHUNKS):
-        across(i).wait_recv()
-        out[c, pl.ds(i * rows, rows)] = x_send[i].astype(F32) + x_land[i].astype(F32)
-        final(i).start()
-    for i in range(CHUNKS):
-        final_from(i).wait_recv()
-    for i in range(CHUNKS):
-        core(i).wait_send()
-        across(i).wait_send()
-        final(i).wait_send()
-
-
-def sum_parts(part):
-    dma = pltpu.SemaphoreType.DMA
-    vmem = pl.BlockSpec(memory_space=pltpu.VMEM)
-    rows, width = part.shape[1] // CHUNKS, part.shape[2]
-    return pl.pallas_call(
-        sum_kernel,
-        out_shape=jax.ShapeDtypeStruct(part.shape, F32),
-        in_specs=[vmem],
-        out_specs=vmem,
-        scratch_shapes=[pltpu.VMEM((CHUNKS, rows, width), BF16)] * 4 + [dma((CHUNKS,))] * 6,
-        name="sum_parts",
-        compiler_params=pltpu.CompilerParams(
-            collective_id=3, has_side_effects=True, vmem_limit_bytes=VMEM_LIMIT
-        ),
-    )(part)
-
-
 def inward(nz):
     order = []
     for k in range((nz + 1) // 2):
@@ -748,233 +558,694 @@
     return order
 
 
-def scatter_kernel(nz, ng, *refs):
-    parts = refs[:ng]
-    small = refs[ng]
-    outs = refs[ng + 1 : 2 * ng + 1]
-    smalls = refs[2 * ng + 1]
-    scratch = refs[2 * ng + 2 :]
-    owns, lands, ins, sends, totals = (scratch[i * ng : (i + 1) * ng] for i in range(5))
-    loc, ys, yr, zs, zr, cs, cr, ws, wr, ts, tr = scratch[5 * ng :]
+OWN = 3
+
+
+class Scatter:
+    def __init__(self, nz, sources, owns, lands, ins, overs, mids, extras, totals, outs, sems):
+        self.nz, self.sources, self.owns, self.lands = nz, sources, owns, lands
+        self.ins, self.overs, self.mids, self.extras = ins, overs, mids, extras
+        self.totals, self.outs, self.sems = totals, outs, sems
+        self.y = lax.axis_index("fy")
+        self.c = lax.axis_index("pr")
+        self.z = lax.axis_index("ctx")
+        self.pair = self.z + 1 - 2 * lax.rem(self.z, 2)
+        self.order = inward(nz)
+
+    def own_copy(self, g, place):
+        t = self.order[place] if place < self.nz else self.z
+        return pltpu.make_async_copy(
+            self.sources[g].at[self.y, :, t],
+            self.owns[g].at[place % 2],
+            self.sems[0].at[g, 3 + place % 2],
+        )
+
+    def own(self, g, place, k, rows):
+        if self.owns[g] is None:
+            t = self.order[place] if place < self.nz else self.z
+            return self.sources[g][self.y, k, t, rows].astype(F32)
+        return self.owns[g][place % 2, k, rows].astype(F32)
+
+    def fetch(self, g, place):
+        if self.owns[g] is not None and place <= self.nz:
+            self.own_copy(g, place).start()
+
+    def fetched(self, g, place):
+        if self.owns[g] is not None:
+            self.own_copy(g, place).wait()
+
+    def middle(self, g):
+        return pltpu.make_async_copy(
+            self.sources[g].at[1 - self.y, 1, self.z], self.mids[g], self.sems[0].at[g, 1]
+        )
+
+    def across(self, g, t, part):
+        ys, yr = self.sems[1], self.sems[2]
+        src, dst = self.sources[g], self.lands[g]
+        if part == "both":
+            src, dst = src.at[1 - self.y, :, t], dst.at[t]
+        else:
+            src, dst = src.at[1 - self.y, 0, t], dst.at[t, 0]
+        return remote(src, dst, ys.at[g, t], yr.at[g, t], {"fy": 1 - self.y})
+
+    def relayed(self, g):
+        ys, yr = self.sems[1], self.sems[2]
+        return remote(
+            self.mids[g],
+            self.lands[g].at[self.z, 1],
+            ys.at[g, self.nz],
+            yr.at[g, self.nz],
+            {"fy": 1 - self.y},
+        )
+
+    def extra(self, g):
+        es, er = self.sems[3], self.sems[4]
+        src = self.sources[g].at[1 - self.y, 1, self.pair]
+        return remote(src, self.extras[g], es.at[g], er.at[g], {"ctx": self.pair})
+
+    def up(self, g, t):
+        zs, zr = self.sems[5], self.sems[6]
+        return remote(
+            self.lands[g].at[t], self.ins[g].at[t], zs.at[g, 0, t], zr.at[g, 0, t], {"ctx": self.z + 1}
+        )
+
+    def down(self, g, t):
+        zs, zr = self.sems[5], self.sems[6]
+        return remote(
+            self.lands[g].at[t], self.ins[g].at[t], zs.at[g, 1, t], zr.at[g, 1, t], {"ctx": self.z - 1}
+        )
+
+    def down_home(self, g, t):
+        zs, zr = self.sems[5], self.sems[6]
+        return remote(
+            self.lands[g].at[t], self.overs[g], zs.at[g, 1, t], zr.at[g, 1, t], {"ctx": self.z - 1}
+        )
+
+    def swap(self, g, slot):
+        cs, cr = self.sems[7], self.sems[8]
+        return remote(
+            self.totals[g].at[1 - self.c], self.outs[g].at[slot], cs.at[g], cr.at[g], {"pr": 1 - self.c}
+        )
+
+    def keep(self, g):
+        return pltpu.make_async_copy(
+            self.totals[g].at[self.c], self.outs[g].at[self.c], self.sems[0].at[g, 2]
+        )
+
+    def each_tile(self, g, body):
+        block = self.lands[g].shape[2]
+        rows = 32 if block % 32 == 0 else block
+        per = block // rows
+
+        def step(i, _):
+            body(i // per, pl.ds(pl.multiple_of(lax.rem(i, per) * rows, 8), rows))
+            return 0
+
+        lax.fori_loop(0, 2 * per, step, 0)
+
+    def start(self, g):
+        self.middle(g).start()
+        self.extra(g).start()
+        self.fetch(g, 0)
+        self.fetch(g, 1)
+        self.lands[g][self.pair, 1] = jnp.zeros(self.lands[g].shape[2:], BF16)
+        for t in self.order:
+
+            @pl.when((self.z != t) & (self.pair != t))
+            def _(t=t):
+                self.across(g, t, "both").start()
+
+            @pl.when(self.pair == t)
+            def _(t=t):
+                self.across(g, t, "half").start()
+
+        self.across(g, self.z, "half").start()
+
+    def relay(self, g):
+        self.middle(g).wait()
+        self.extra(g).wait_recv()
+        self.mids[g][...] = (
+            self.mids[g][...].astype(F32) + self.extras[g][...].astype(F32)
+        ).astype(BF16)
+        self.relayed(g).start()
+
+    def step(self, g, place):
+        z, nz, t = self.z, self.nz, self.order[place]
+        land, into = self.lands[g], self.ins[g]
+        self.fetched(g, place)
+
+        @pl.when(z != t)
+        def _():
+            @pl.when(self.pair != t)
+            def _():
+                self.across(g, t, "both").wait_recv()
+
+            @pl.when(self.pair == t)
+            def _():
+                self.across(g, t, "half").wait_recv()
+
+            inner = ((z < t) & (z > 0)) | ((z > t) & (z < nz - 1))
+
+            @pl.when(inner)
+            def _():
+                @pl.when(z < t)
+                def _():
+                    self.up(g, t).wait_recv()
+
+                @pl.when(z > t)
+                def _():
+                    self.down(g, t).wait_recv()
+
+                def add(k, rows):
+                    land[t, k, rows] = (
+                        self.own(g, place, k, rows)
+                        + land[t, k, rows].astype(F32)
+                        + into[t, k, rows].astype(F32)
+                    ).astype(BF16)
+
+                self.each_tile(g, add)
+
+            @pl.when(jnp.logical_not(inner))
+            def _():
+                def add(k, rows):
+                    land[t, k, rows] = (
+                        self.own(g, place, k, rows) + land[t, k, rows].astype(F32)
+                    ).astype(BF16)
+
+                self.each_tile(g, add)
+
+            @pl.when(z < t)
+            def _():
+                self.up(g, t).start()
+
+            @pl.when(z > t + 1)
+            def _():
+                self.down(g, t).start()
+
+            @pl.when(z == t + 1)
+            def _():
+                self.down_home(g, t).start()
+
+        self.fetch(g, place + 2)
+
+    def last(self, g):
+        z, nz = self.z, self.nz
+        land, into, over = self.lands[g], self.ins[g], self.overs[g]
+        self.fetched(g, nz)
+        total = self.totals[g]
+        self.across(g, z, "half").wait_recv()
+        self.relayed(g).wait_recv()
+
+        def base(k, rows):
+            total[k, rows] = self.own(g, nz, k, rows) + land[z, k, rows].astype(F32)
+
+        self.each_tile(g, base)
+
+        @pl.when(z > 0)
+        def _():
+            self.up(g, z).wait_recv()
+
+            def add(k, rows):
+                total[k, rows] += into[z, k, rows].astype(F32)
+
+            self.each_tile(g, add)
+
+        @pl.when(z < nz - 1)
+        def _():
+            self.down_home(g, z).wait_recv()
+
+            def add(k, rows):
+                total[k, rows] += over[k, rows].astype(F32)
+
+            self.each_tile(g, add)
+
+        self.swap(g, self.c).start()
+        self.keep(g).start()
+
+    def finish(self, g):
+        self.swap(g, 1 - self.c).wait_recv()
+        self.swap(g, self.c).wait_send()
+        self.keep(g).wait()
+        self.extra(g).wait_send()
+        self.relayed(g).wait_send()
+        self.across(g, self.z, "half").wait_send()
+        for t in self.order:
+
+            @pl.when((self.z != t) & (self.pair != t))
+            def _(t=t):
+                self.across(g, t, "both").wait_send()
+
+            @pl.when(self.pair == t)
+            def _(t=t):
+                self.across(g, t, "half").wait_send()
+
+            @pl.when(self.z < t)
+            def _(t=t):
+                self.up(g, t).wait_send()
+
+            @pl.when(self.z > t)
+            def _(t=t):
+                self.down(g, t).wait_send()
+
+
+class TokenSum:
+    def __init__(self, part, bufs, sems, n):
+        self.part, self.n = part, n
+        self.core_send, self.core_land, self.x_send, self.x_land = bufs
+        self.cs, self.cr, self.xs, self.xr = sems
+        self.c = lax.axis_index("pr")
+        self.x = lax.axis_index("tp")
+
+    def core(self, i):
+        return remote(
+            self.core_send.at[i],
+            self.core_land.at[self.n % 2, i],
+            self.cs.at[self.n, i],
+            self.cr.at[self.n, i],
+            {"pr": 1 - self.c},
+        )
+
+    def sideways(self, i):
+        return remote(
+            self.x_send.at[i],
+            self.x_land.at[self.n % 2, i],
+            self.xs.at[self.n, i],
+            self.xr.at[self.n, i],
+            {"tp": 1 - self.x},
+        )
+
+    def start(self):
+        for i in range(4):
+            self.core_send[i] = self.part(1 - self.c, i).astype(BF16)
+            self.core(i).start()
+        for i in range(4):
+            mine = self.part(self.c, i).astype(F32)
+            self.core(i).wait_recv()
+            self.x_send[i] = (mine + self.core_land[self.n % 2, i].astype(F32)).astype(BF16)
+            self.sideways(i).start()
+
+    def arrived(self, i):
+        self.sideways(i).wait_recv()
+
+    def total(self, i):
+        return self.x_send[i].astype(F32) + self.x_land[self.n % 2, i].astype(F32)
+
+    def drain(self):
+        for i in range(4):
+            self.core(i).wait_send()
+            self.sideways(i).wait_send()
+
+
+def backward_kernel(nz, scale, *refs):
+    sources = refs[:3]
+    (
+        dx_part, out_part, residual, rows, upstream, mlp_gain, attn_gain, cos, sin, q_seg, k_seg,
+        spread_mat, q_items, k_items, v_items, mixed_wide, mixed_low, lse, w_qkv, w_out, normed,
+    ) = refs[3:24]
+    layer_out, input_grad = refs[24:26]
+    outs = refs[26:31]
+    gains = refs[31]
+    scratch = refs[32:]
+    owns = (*scratch[:OWN], None, None)
+    lands, ins, overs, mids, extras, totals = (
+        scratch[OWN + 5 * i : OWN + 5 * i + 5] for i in range(6)
+    )
+    (
+        o_part, qkv_part, core_send, core_land, x_send, x_land, back_rows, low_rows, grad_items,
+        delta, dq, kv_send, kv_land, qkv_rows, gain_rows, keys, values,
+    ) = scratch[OWN + 30 : OWN + 47]
+    (
+        loc, ys, yr, es, er, zs, zr, ss, sr, cs, cr, xs, xr, ns, nr, ks, kr, gs, gr, ts, tr, bs,
+    ) = scratch[OWN + 47 :]
     y = lax.axis_index("fy")
     c = lax.axis_index("pr")
     z = lax.axis_index("ctx")
-    other_y = {"fy": 1 - y}
-    other_c = {"pr": 1 - c}
+    span, width = rows.shape
+    chunk = width // 4
+    half = 4 * DH
+    sources = (*sources, o_part, qkv_part)
+    scatter = Scatter(
+        nz, sources, owns, lands, ins, overs, mids, extras, totals, outs,
+        (loc, ys, yr, es, er, zs, zr, ss, sr),
+    )
     greet(
-        [(other_y, None), (other_c, None)] + [({"ctx": t}, z != t) for t in range(nz)], nz + 1
-    )
-
-    def across(g, t):
-        return remote(parts[g].at[1 - y, :, t], lands[g].at[t], ys.at[g, t], yr.at[g, t], other_y)
-
-    def own(g, t):
-        return pltpu.make_async_copy(parts[g].at[y, :, t], owns[g].at[t], loc.at[g, t])
-
-    def up(g, t):
+        [
+            ({"fy": 1 - y}, None),
+            ({"pr": 1 - c}, None),
+            ({"tp": 1 - lax.axis_index("tp")}, None),
+        ]
+        + [({"ctx": t}, z != t) for t in range(nz)],
+        2 + nz,
+    )
+    bufs = (core_send, core_land, x_send, x_land)
+    sems = (cs, cr, xs, xr)
+    late = (0, 1, 2)
+
+    def columns(i):
+        return pl.ds(i * chunk, chunk)
+
+    first = TokenSum(lambda who, i: dx_part[who, :, columns(i)], bufs, sems, 0)
+    first.start()
+    for g in late:
+        scatter.start(g)
+
+    squares = jnp.zeros((span, 1), F32)
+    inner_sum = jnp.zeros((span, 1), F32)
+    for i in range(4):
+        first.arrived(i)
+        grad = first.total(i)
+        back_rows[:, columns(i)] = grad
+        value = residual[:, columns(i)]
+        squares = squares + jnp.sum(value * value, axis=1, keepdims=True)
+        inner_sum = inner_sum + jnp.sum(grad * mlp_gain[:, columns(i)] * value, axis=1, keepdims=True)
+    factor = lax.rsqrt(squares / width + EPS)
+    slope = factor * factor * factor * (inner_sum / width)
+    for i in range(4):
+        grad = back_rows[:, columns(i)]
+        value = residual[:, columns(i)]
+        gain_rows[1:2, columns(i)] = jnp.sum(grad * value * factor, axis=0, keepdims=True)
+        back = (
+            upstream[:, columns(i)].astype(F32)
+            + factor * (grad * mlp_gain[:, columns(i)])
+            - value * slope
+        )
+        back_rows[:, columns(i)] = back
+        low_rows[c, :, columns(i)] = back.astype(BF16)
+    first.drain()
+    swap = remote(low_rows.at[c], low_rows.at[c], ns.at[0], nr.at[0], {"pr": 1 - c})
+    swap.start()
+    for g in late:
+        scatter.relay(g)
+    remote(low_rows.at[1 - c], low_rows.at[1 - c], ns.at[0], nr.at[0], {"pr": 1 - c}).wait_recv()
+    second = TokenSum(lambda who, i: out_part[who, :, columns(i)], bufs, sems, 1)
+    second.start()
+
+    for b in range(2):
+        grads = jnp.zeros((span, half), F32)
+        for i in range(4):
+            weights = w_out[i // 2, i % 2].reshape(chunk, half)
+            grads = grads + dot(low_rows[b, :, columns(i)], weights)
+        wide = dot(grads.astype(BF16), spread_mat[...]).astype(BF16)
+        for k in range(2):
+            for j in range(2):
+                head = 2 * k + j
+                grad_items[b * 2 + k, pl.ds(j * span, span)] = wide[
+                    :, head * LANES : (head + 1) * LANES
+                ]
+    for i in range(4):
+        part = dot(low_rows[0, :, columns(i)], mixed_low[:span], 0, 0) + dot(
+            low_rows[1, :, columns(i)], mixed_low[span:], 0, 0
+        )
+        o_part[i // 2, i % 2] = part.astype(BF16).reshape(o_part.shape[2:])
+    for g in late:
+        scatter.step(g, 0)
+    scatter.start(3)
+
+    for i in range(4):
+        delta[i] = jnp.broadcast_to(
+            jnp.sum(grad_items[i].astype(F32) * mixed_wide[i], axis=1, keepdims=True),
+            delta.shape[1:],
+        )
+
+    slots = kv_send.shape[0]
+
+    def keys_down(b, s):
+        t = z - s
         return remote(
-            sends[g].at[t], ins[g].at[0, t], zs.at[0, g, t], zr.at[0, g, t], {"ctx": z + 1}
-        )
-
-    def down(g, t):
+            kv_send.at[s % slots, b], kv_land.at[t, b], ks.at[b, t], kr.at[b, t], {"ctx": z - 1}
+        )
+
+    def keys_from(b, s):
+        t = z - s
         return remote(
-            sends[g].at[t], ins[g].at[1, t], zs.at[1, g, t], zr.at[1, g, t], {"ctx": z - 1}
-        )
-
-    def swap(g):
-        return remote(totals[g].at[1 - c], outs[g].at[c], cs.at[g], cr.at[g], other_c)
-
-    def keep(g):
-        return pltpu.make_async_copy(totals[g].at[c], outs[g].at[c], loc.at[ng, g])
-
-    def swap_from(g):
-        return remote(totals[g].at[1 - c], outs[g].at[1 - c], cs.at[g], cr.at[g], other_c)
-
-    def small_to(t):
-        return remote(smalls.at[:, c, z], smalls.at[:, c, z], ws.at[t], wr.at[z], {"ctx": t})
-
-    def small_from(t):
-        return remote(smalls.at[:, c, t], smalls.at[:, c, t], ws.at[t], wr.at[t], {"ctx": t})
-
-    def rows_of(g):
-        block = owns[g].shape[2]
-        return 32 if block % 32 == 0 else block
-
-    def each_tile(g, body):
-        rows = rows_of(g)
-        per = owns[g].shape[2] // rows
-
-        def step(i, _):
-            body(i // per, pl.ds(pl.multiple_of((i % per) * rows, 8), rows))
+            kv_send.at[s % slots, b], kv_land.at[t, b], ks.at[b, t], kr.at[b, t], {"ctx": z - 1}
+        )
+
+    def load(s):
+        return (
+            pltpu.make_async_copy(k_items.at[z - s], keys.at[s % 2], bs.at[0, s % 2]),
+            pltpu.make_async_copy(v_items.at[z - s], values.at[s % 2], bs.at[1, s % 2]),
+        )
+
+    def back_block(s, diagonal):
+        block, slot = z - s, s % 2
+        for copy in load(s):
+            copy.wait()
+
+        def one(b, _):
+            key_grads, value_grads = [], []
+            for k in range(2):
+                item = b * 2 + k
+                scores = dot(q_items[item], keys[slot, item], 1, 1) * scale
+                allowed = q_seg[b] == k_seg[b, block]
+                if diagonal:
+                    row = lax.broadcasted_iota(jnp.int32, scores.shape, 0)
+                    column = lax.broadcasted_iota(jnp.int32, scores.shape, 1)
+                    allowed = allowed & (lax.rem(row, span) >= column)
+                probs = jnp.where(allowed, jnp.exp(scores - lse[item][:, :1]), 0.0)
+                prob_grad = dot(grad_items[item], values[slot, item], 1, 1)
+                score_grad = (probs * (prob_grad - delta[item][:, :1])).astype(BF16)
+                value_grads.append(dot(probs.astype(BF16), grad_items[item], 0, 0))
+                key_grads.append(dot(score_grad, q_items[item], 0, 0) * scale)
+                dq[item] += dot(score_grad, keys[slot, item]) * scale
+            wide = jnp.concatenate(key_grads + value_grads, axis=1).astype(BF16)
+            kv_send[s % slots, b] = dot(wide, spread_mat[...], 1, 1).astype(BF16)
             return 0
 
-        lax.fori_loop(0, 2 * per, step, 0)
-
-    order = inward(nz)
-    mine = pltpu.make_async_copy(small, smalls.at[y, c, z], loc.at[ng + 1, 0])
+        lax.fori_loop(0, 2, one, 0)
+
+    dq[...] = jnp.zeros_like(dq)
+    for s in range(nz - 1, -1, -1):
+
+        @pl.when(z == s)
+        def _(s=s):
+            for copy in load(s):
+                copy.start()
+
+    for s in range(nz - 1, 0, -1):
+
+        @pl.when(z >= s)
+        def _(s=s):
+            for copy in load(s - 1):
+                copy.start()
+            if s + slots < nz:
+
+                @pl.when(z >= s + slots)
+                def _():
+                    for b in range(2):
+                        keys_down(b, s + slots).wait_send()
+
+            back_block(s, False)
+            for b in range(2):
+
+                @pl.when(z < nz - 1)
+                def _(b=b):
+                    keys_from(b, s).wait_recv()
+                    kv_send[s % slots, b] = (
+                        kv_send[s % slots, b].astype(F32) + kv_land[z - s, b].astype(F32)
+                    ).astype(BF16)
+
+                keys_down(b, s).start()
+
+        for g in late:
+            scatter.step(g, nz - s)
+    if slots < nz:
+
+        @pl.when(z >= slots)
+        def _():
+            for b in range(2):
+                keys_down(b, slots).wait_send()
+
+    back_block(0, True)
+    for i in range(4):
+        second.arrived(i)
+        layer_out[:, columns(i)] = (residual[:, columns(i)] + second.total(i)).astype(BF16)
+    second.drain()
+
+    def unrotated(field, b):
+        turned = pltpu.roll(field, LANES // 2, 1)
+        here = pl.ds(b * span, span)
+        return (field * cos[here] - turned * sin[here]).astype(BF16)
+
+    for b in range(2):
+        heads = [
+            unrotated(dq[b * 2 + k, pl.ds(j * span, span)], b) for k in range(2) for j in range(2)
+        ]
+        qkv_rows[b, :, :half] = dot(
+            jnp.concatenate(heads, axis=1), spread_mat[...], 1, 1
+        ).astype(BF16)
+    for b in range(2):
+
+        @pl.when(z < nz - 1)
+        def _(b=b):
+            keys_from(b, 0).wait_recv()
+            kv_send[0, b] = (
+                kv_send[0, b].astype(F32) + kv_land[z, b].astype(F32)
+            ).astype(BF16)
+
+        wide = dot(kv_send[0, b], spread_mat[...])
+        fields = [unrotated(wide[:, k * LANES : (k + 1) * LANES], b) for k in range(2)]
+        fields += [wide[:, (2 + k) * LANES : (3 + k) * LANES].astype(BF16) for k in range(2)]
+        qkv_rows[b, :, half:] = dot(
+            jnp.concatenate(fields, axis=1), spread_mat[...], 1, 1
+        ).astype(BF16)
+    for i in range(4):
+        part = dot(normed[:span, columns(i)], qkv_rows[0], 0, 0) + dot(
+            normed[span:, columns(i)], qkv_rows[1], 0, 0
+        )
+        qkv_part[i // 2, i % 2] = part.astype(BF16).reshape(qkv_part.shape[2:])
+    scatter.start(4)
+
+    def back_in(who, i):
+        weights = w_qkv[i // 2, i % 2].reshape(chunk, 2 * half)
+        return dot(qkv_rows[who], weights, 1, 1)
+
+    third = TokenSum(back_in, bufs, sems, 2)
+    third.start()
+    scatter.relay(3)
+    scatter.relay(4)
+    for g in late:
+        scatter.last(g)
+    squares = jnp.zeros((span, 1), F32)
+    inner_sum = jnp.zeros((span, 1), F32)
+    for i in range(4):
+        third.arrived(i)
+        grad = third.total(i)
+        value = rows[:, columns(i)].astype(F32)
+        squares = squares + jnp.sum(value * value, axis=1, keepdims=True)
+        inner_sum = inner_sum + jnp.sum(grad * attn_gain[:, columns(i)] * value, axis=1, keepdims=True)
+    factor = lax.rsqrt(squares / width + EPS)
+    slope = factor * factor * factor * (inner_sum / width)
+    for i in range(4):
+        value = rows[:, columns(i)].astype(F32)
+        gain_rows[0:1, columns(i)] = jnp.sum(third.total(i) * value * factor, axis=0, keepdims=True)
+        input_grad[:, columns(i)] = (
+            back_rows[:, columns(i)]
+            + factor * (third.total(i) * attn_gain[:, columns(i)])
+            - value * slope
+        ).astype(BF16)
+    third.drain()
+
+    mine = pltpu.make_async_copy(gain_rows, gains.at[y, c, z], ts.at[2])
     mine.start()
-    line = remote(small, smalls.at[y, c, z], ts.at[0], tr.at[0], other_y)
-    line.start()
-    for t in order:
-        for g in range(ng):
-            across(g, t).start()
-            own(g, t).start()
     mine.wait()
-    remote(small, smalls.at[1 - y, c, z], ts.at[0], tr.at[0], other_y).wait_recv()
+    core_gain = remote(gains.at[y, c, z], gains.at[y, c, z], ts.at[1], tr.at[1], {"pr": 1 - c})
+    core_gain.start()
+    remote(
+        gains.at[y, 1 - c, z], gains.at[y, 1 - c, z], ts.at[1], tr.at[1], {"pr": 1 - c}
+    ).wait_recv()
+
+    def gain_to(t):
+        return remote(gains.at[y, :, z], gains.at[y, :, z], gs.at[t], gr.at[z], {"ctx": t})
+
+    def gain_from(t):
+        return remote(gains.at[y, :, t], gains.at[y, :, t], gs.at[t], gr.at[t], {"ctx": t})
+
     for t in range(nz):
 
         @pl.when(z != t)
         def _(t=t):
-            small_to(t).start()
-
-    for t in order:
-        for g in range(ng):
-            side = (z > t).astype(jnp.int32)
-            first = ((z == 0) & (z < t)) | ((z == nz - 1) & (z > t))
-
-            @pl.when(first)
-            def _(g=g, t=t, side=side):
-                def clear(k, rows):
-                    ins[g][side, t, k, rows] = jnp.zeros(
-                        (rows_of(g), ins[g].shape[-1]), BF16
-                    )
-
-                each_tile(g, clear)
-
-            own(g, t).wait()
-            across(g, t).wait_recv()
-
-            @pl.when((z < t) & (z > 0))
-            def _(g=g, t=t):
-                up(g, t).wait_recv()
-
-            @pl.when((z > t) & (z < nz - 1))
-            def _(g=g, t=t):
-                down(g, t).wait_recv()
-
-            @pl.when(z != t)
-            def _(g=g, t=t, side=side):
-                def add(k, rows):
-                    sends[g][t, k, rows] = (
-                        owns[g][t, k, rows].astype(F32)
-                        + lands[g][t, k, rows].astype(F32)
-                        + ins[g][side, t, k, rows].astype(F32)
-                    ).astype(BF16)
-
-                each_tile(g, add)
-
-            @pl.when(z < t)
-            def _(g=g, t=t):
-                up(g, t).start()
-
-            @pl.when(z > t)
-            def _(g=g, t=t):
-                down(g, t).start()
-
-    for g in range(ng):
-
-        @pl.when(z > 0)
-        def _(g=g):
-            up(g, z).wait_recv()
-
-        @pl.when(z < nz - 1)
-        def _(g=g):
-            down(g, z).wait_recv()
-
-        @pl.when(z == 0)
-        def _(g=g):
-            def clear(k, rows):
-                ins[g][0, z, k, rows] = jnp.zeros((rows_of(g), ins[g].shape[-1]), BF16)
-
-            each_tile(g, clear)
-
-        @pl.when(z == nz - 1)
-        def _(g=g):
-            def clear(k, rows):
-                ins[g][1, z, k, rows] = jnp.zeros((rows_of(g), ins[g].shape[-1]), BF16)
-
-            each_tile(g, clear)
-
-        def add(k, rows, g=g):
-            totals[g][k, rows] = (
-                owns[g][z, k, rows].astype(F32)
-                + lands[g][z, k, rows].astype(F32)
-                + ins[g][0, z, k, rows].astype(F32)
-                + ins[g][1, z, k, rows].astype(F32)
-            )
-
-        each_tile(g, add)
-        swap(g).start()
-        keep(g).start()
-
+            gain_to(t).start()
+
+    for place in range(nz):
+        scatter.step(3, place)
+        scatter.step(4, place)
     for t in range(nz):
 
         @pl.when(z != t)
         def _(t=t):
-            small_from(t).wait_recv()
-
-    plane = remote(smalls.at[:, c], smalls.at[:, c], ts.at[1], tr.at[1], other_c)
-    plane.start()
-    remote(smalls.at[:, 1 - c], smalls.at[:, 1 - c], ts.at[1], tr.at[1], other_c).wait_recv()
-    for g in range(ng):
-        swap_from(g).wait_recv()
-        keep(g).wait()
-        swap(g).wait_send()
-    line.wait_send()
-    plane.wait_send()
+            gain_from(t).wait_recv()
+
+    gain_line = remote(gains.at[y], gains.at[y], ts.at[0], tr.at[0], {"fy": 1 - y})
+    gain_line.start()
+    scatter.last(3)
+    scatter.last(4)
+    remote(gains.at[1 - y], gains.at[1 - y], ts.at[0], tr.at[0], {"fy": 1 - y}).wait_recv()
+    for g in range(5):
+        scatter.finish(g)
+    core_gain.wait_send()
+    gain_line.wait_send()
+    swap.wait_send()
     for t in range(nz):
 
         @pl.when(z != t)
         def _(t=t):
-            small_to(t).wait_send()
-
-        for g in range(ng):
-            across(g, t).wait_send()
-
-            @pl.when(z < t)
-            def _(g=g, t=t):
-                up(g, t).wait_send()
-
-            @pl.when(z > t)
-            def _(g=g, t=t):
-                down(g, t).wait_send()
-
-
-def scatter_all(parts, small, ny, nz):
-    ng = len(parts)
+            gain_to(t).wait_send()
+
+    for s in range(1, slots):
+
+        @pl.when(z >= s)
+        def _(s=s):
+            for b in range(2):
+                keys_down(b, s).wait_send()
+
+
+def backward(parts, operands, ny, nz):
     dma = pltpu.SemaphoreType.DMA
     anywhere = pl.BlockSpec(memory_space=pl.ANY)
-    shapes = [jax.ShapeDtypeStruct((2,) + part.shape[3:], F32) for part in parts]
-    shapes.append(jax.ShapeDtypeStruct((ny, 2, nz) + small.shape, small.dtype))
-    slots = [pltpu.VMEM((nz, 2) + part.shape[3:], BF16) for part in parts]
-    results = pl.pallas_call(
-        functools.partial(scatter_kernel, nz, ng),
-        out_shape=shapes,
-        in_specs=[anywhere] * (ng + 1),
-        out_specs=[anywhere] * (ng + 1),
-        scratch_shapes=slots * 2
-        + [pltpu.VMEM((2, nz, 2) + part.shape[3:], BF16) for part in parts]
-        + slots
-        + [pltpu.VMEM((2,) + part.shape[3:], F32) for part in parts]
+    vmem = pl.BlockSpec(memory_space=pltpu.VMEM)
+    residual = operands[2]
+    span, width = residual.shape
+    chunk = width // 4
+    block = parts[0].shape[3]
+    half = 4 * DH
+    wide = [part.shape[4] for part in parts] + [half, 2 * half]
+    shape = jax.ShapeDtypeStruct
+    out_shape = (
+        [shape((span, width), BF16)] * 2
+        + [shape((2, block, w), F32) for w in wide]
+        + [shape((ny, 2, nz, 2, width), F32)]
+    )
+
+    def bufs(lead, dtype=BF16):
+        return [pltpu.VMEM(lead + (block, w), dtype) for w in wide]
+
+    return pl.pallas_call(
+        functools.partial(backward_kernel, nz, DH ** (-0.5)),
+        out_shape=out_shape,
+        in_specs=[anywhere] * 3 + [vmem] * 13 + [anywhere] * 2 + [vmem] * 6,
+        out_specs=[vmem] * 2 + [anywhere] * 6,
+        scratch_shapes=bufs((2, 2))[:OWN]
+        + bufs((nz, 2))
+        + bufs((nz, 2))
+        + bufs((2,))
+        + bufs(())
+        + bufs(())
+        + bufs((2,), F32)
         + [
-            dma((ng + 2, max(nz, ng))),
-            dma((ng, nz)),
-            dma((ng, nz)),
-            dma((2, ng, nz)),
-            dma((2, ng, nz)),
-            dma((ng,)),
-            dma((ng,)),
-            dma((nz,)),
-            dma((nz,)),
-            dma((2,)),
-            dma((2,)),
-        ],
-        name="scatter_all",
+            pltpu.VMEM((ny, 2, nz, block, half), BF16),
+            pltpu.VMEM((ny, 2, nz, block, 2 * half), BF16),
+            pltpu.VMEM((4, span, chunk), BF16),
+            pltpu.VMEM((2, 4, span, chunk), BF16),
+            pltpu.VMEM((4, span, chunk), BF16),
+            pltpu.VMEM((2, 4, span, chunk), BF16),
+            pltpu.VMEM((span, width), F32),
+            pltpu.VMEM((2, span, width), BF16),
+            pltpu.VMEM((4, 2 * span, LANES), BF16),
+            pltpu.VMEM((4, 2 * span, LANES), F32),
+            pltpu.VMEM((4, 2 * span, LANES), F32),
+            pltpu.VMEM((min(nz, 4), 2, span, half), BF16),
+            pltpu.VMEM((nz, 2, span, half), BF16),
+            pltpu.VMEM((2, span, 2 * half), BF16),
+            pltpu.VMEM((2, width), F32),
+            pltpu.VMEM((2, 4, span, LANES), BF16),
+            pltpu.VMEM((2, 4, span, LANES), BF16),
+        ]
+        + [dma((5, 5))]
+        + [dma((5, nz + 1))] * 2
+        + [dma((5,))] * 2
+        + [dma((5, 2, nz))] * 2
+        + [dma((5,))] * 2
+        + [dma((3, 4))] * 4
+        + [dma((1,))] * 2
+        + [dma((2, nz))] * 2
+        + [dma((nz,))] * 2
+        + [dma((3,)), dma((2,)), dma((2, 2))],
+        name="backward",
         compiler_params=pltpu.CompilerParams(
-            collective_id=4, has_side_effects=True, vmem_limit_bytes=VMEM_LIMIT
+            collective_id=2, has_side_effects=True, vmem_limit_bytes=VMEM_LIMIT
         ),
-    )(*parts, small)
-    return results[:ng], results[ng]
+    )(*parts, *operands)
 
 
 def halves(matrix):
@@ -1006,7 +1277,6 @@
     _, span, width = layer_input.shape
     block = query_proj.shape[0]
     groups = HQ // HK
-    score_scale = DH ** (-0.5)
     y = lax.axis_index("fy")
     c = lax.axis_index("pr")
     z = lax.axis_index("ctx")
@@ -1066,132 +1336,67 @@
         ny,
         nz,
     )
-    qkv_full, out_full, gate_full, up_full, down_full = (
-        piece.reshape(width, piece.shape[-1]) for piece in results[:5]
-    )
-    q_items, k_items, v_items, mixed_wide, mixed_rows, row_lse, residual_own, normed_mlp = results[5:]
+    gate_full, up_full, down_full = (
+        piece.reshape(width, piece.shape[-1]) for piece in results[2:5]
+    )
+    q_items, k_items, v_items, mixed_wide, mixed_low, row_lse, residual_own, normed_mlp = results[5:]
     normed_mlp = normed_mlp.reshape(total_rows, width)
     gate_pre = jnp.dot(normed_mlp, gate_full, preferred_element_type=F32)
     up_pre = jnp.dot(normed_mlp, up_full, preferred_element_type=F32)
     activated = jax.nn.silu(gate_pre)
     hidden = (activated * up_pre).astype(BF16)
 
-    def own_rows(both):
-        return lax.dynamic_slice_in_dim(both.reshape(total_rows, width), c * span, span, 0)
-
-    mlp_out = sum_parts(contract(hidden, down_full, 1, 1).reshape(2, span, width))
-    layer_output = (residual_own + own_rows(mlp_out)).astype(BF16)
-
+    out_part = contract(hidden, down_full, 1, 1).astype(BF16).reshape(2, span, width)
     upstream_low = grads_both.reshape(total_rows, width)
     hidden_grad = jnp.dot(upstream_low, down_full, preferred_element_type=F32)
-    down_part = contract(upstream_low, hidden, 0, 0).astype(BF16)
     sigmoid_gate = jax.nn.sigmoid(gate_pre)
     gate_grad = (
         hidden_grad * up_pre * sigmoid_gate * (1.0 + gate_pre * (1.0 - sigmoid_gate))
     ).astype(BF16)
     up_grad = (hidden_grad * activated).astype(BF16)
-    normed_mlp_grad = own_rows(
-        sum_parts(
-            (contract(gate_grad, gate_full, 1, 1) + contract(up_grad, up_full, 1, 1)).reshape(
-                2, span, width
-            )
-        )
-    )
-    gate_part = contract(normed_mlp, gate_grad, 0, 0).astype(BF16)
-    up_part = contract(normed_mlp, up_grad, 0, 0).astype(BF16)
-    scale_mlp = inverse_rms(residual_own)
-    mlp_gain_term = jnp.sum(normed_mlp_grad * residual_own * scale_mlp, axis=0)
-    upstream = out_grad.reshape(span, width).astype(F32)
-    residual_grad = norm_back(upstream, normed_mlp_grad * mlp_gain_full, residual_own, scale_mlp)
-    residual_low = core_both(residual_grad.astype(BF16)).reshape(total_rows, width)
-    out_part = contract(residual_low, mixed_rows, 0, 0).astype(BF16)
-    mixed_grad = jnp.dot(residual_low, out_full, preferred_element_type=F32).astype(BF16)
-
-    def to_items(rows):
-        wide = jnp.dot(rows, spread_mat, preferred_element_type=F32).astype(BF16)
-        return wide.reshape(2, span, 2, groups, LANES).transpose(0, 2, 3, 1, 4).reshape(
-            4, groups * span, LANES
-        )
-
-    def narrow(wide):
-        return contract(wide.astype(BF16), spread_mat, 1, 1)
-
-    grad_items = to_items(mixed_grad)
-    reached = (jnp.arange(nz) <= z)[:, None, None, None]
-    k_all = jnp.where(reached, k_items, jnp.zeros_like(k_items)).transpose(1, 0, 2, 3).reshape(
-        4, nz * span, LANES
-    )
-    v_all = jnp.where(reached, v_items, jnp.zeros_like(v_items)).transpose(1, 0, 2, 3).reshape(
-        4, nz * span, LANES
-    )
-    query_index = jnp.tile(z * span + jnp.arange(span), groups)
-    key_index = jnp.arange(nz * span)
-    key_segments = jnp.repeat(segment_all.reshape(2, nz * span), 2, axis=0)
-    query_segments = jnp.repeat(q_seg[:, :, 0], 2, axis=0)
-
-    def backward_block(item):
-        bq, bk, bv, ks, qs, blse, bg = item
-        scores = jnp.einsum("qd,kd->qk", bq, bk, preferred_element_type=F32) * score_scale
-        allowed = (qs[:, None] == ks[None, :]) & (query_index[:, None] >= key_index[None, :])
-        probs = jnp.where(allowed, jnp.exp(scores - blse[:, :1]), 0.0)
-        prob_grad = jnp.einsum("qd,kd->qk", bg, bv, preferred_element_type=F32)
-        row_delta = jnp.sum(prob_grad * probs, axis=1, keepdims=True)
-        score_grad = (probs * (prob_grad - row_delta)).astype(BF16)
-        value_grad = jnp.einsum("qk,qd->kd", probs.astype(BF16), bg, preferred_element_type=F32)
-        key_grad = jnp.einsum("qk,qd->kd", score_grad, bq, preferred_element_type=F32) * score_scale
-        query_grad = jnp.dot(score_grad, bk, preferred_element_type=F32) * score_scale
-        return (query_grad, key_grad, value_grad)
-
-    query_grads, key_grads, value_grads = lax.map(
-        backward_block, (q_items, k_all, v_all, key_segments, query_segments, row_lse, grad_items)
-    )
-    kv_wide = jnp.concatenate(
-        [
-            key_grads.reshape(2, 2, nz, span, LANES).transpose(2, 0, 3, 1, 4).reshape(nz * 2 * span, 2 * LANES),
-            value_grads.reshape(2, 2, nz, span, LANES).transpose(2, 0, 3, 1, 4).reshape(nz * 2 * span, 2 * LANES),
-        ],
-        axis=1,
-    )
-    kv_back = keys_down(narrow(kv_wide).astype(BF16).reshape(nz, 2, span, 4 * DH), nz).reshape(
-        total_rows, 4 * DH
-    )
-    kv_width = 2 * DH
-    cos_t = cos_half[:, None, :]
-    sin_t = sin_half[:, None, :]
-    swapped = jnp.concatenate([query_grads[:, :, LANES // 2 :], query_grads[:, :, : LANES // 2]], axis=2)
-    cos_i = jnp.repeat(jnp.tile(cos_wide.reshape(2, span, LANES), (1, groups, 1)), 2, axis=0)
-    sin_i = jnp.repeat(jnp.tile(sin_wide.reshape(2, span, LANES), (1, groups, 1)), 2, axis=0)
-    q_un = (query_grads * cos_i - swapped * sin_i).astype(BF16)
-    q_un = q_un.reshape(2, 2, groups, span, LANES).transpose(0, 3, 1, 2, 4).reshape(total_rows, 4 * LANES)
-    query_grad_rows = narrow(q_un).astype(BF16)
-    key_grad_rows = (
-        unrotate(kv_back[:, :kv_width].astype(F32).reshape(total_rows, 2, DH), cos_t, sin_t)
+    dx_part = (
+        (contract(gate_grad, gate_full, 1, 1) + contract(up_grad, up_full, 1, 1))
         .astype(BF16)
-        .reshape(total_rows, -1)
-    )
-    qkv_grad_rows = jnp.concatenate([query_grad_rows, key_grad_rows, kv_back[:, kv_width:]], axis=1)
-    qkv_part = contract(normed_attn, qkv_grad_rows, 0, 0).astype(BF16)
-    normed_attn_grad = own_rows(
-        sum_parts(contract(qkv_grad_rows, qkv_full, 1, 1).reshape(2, span, width))
-    )
-    inputs_own = layer_rows.astype(F32)
-    scale_own = inverse_rms(inputs_own)
-    attn_gain_term = jnp.sum(normed_attn_grad * inputs_own * scale_own, axis=0)
-    input_grad = norm_back(
-        residual_grad, normed_attn_grad * attn_gain_full, inputs_own, scale_own
-    ).astype(BF16)
-
-    parts = tuple(
-        part.reshape(ny, 2, nz, block, part.shape[1])
-        for part in (down_part, gate_part, up_part, out_part, qkv_part)
-    )
-    gains = jnp.stack([attn_gain_term, mlp_gain_term]).reshape(2 * width // LANES, LANES)
-    reduced, gains_all = scatter_all(parts, gains, ny, nz)
-    down_g, gate_g, up_g, out_g, qkv_g = reduced
-    gain_sum = jnp.sum(gains_all, axis=(0, 1, 2)).reshape(2, width)
+        .reshape(2, span, width)
+    )
+    parts = [
+        part.astype(BF16).reshape(ny, 2, nz, block, part.shape[1])
+        for part in (
+            contract(upstream_low, hidden, 0, 0),
+            contract(normed_mlp, gate_grad, 0, 0),
+            contract(normed_mlp, up_grad, 0, 0),
+        )
+    ]
+    operands = (
+        dx_part,
+        out_part,
+        residual_own,
+        layer_rows,
+        out_grad.reshape(span, width),
+        mlp_gain_full.reshape(1, width),
+        attn_gain_full.reshape(1, width),
+        cos_wide,
+        sin_wide,
+        q_seg,
+        segment_all,
+        spread_mat,
+        q_items,
+        k_items,
+        v_items,
+        mixed_wide,
+        mixed_low,
+        row_lse,
+        results[0],
+        results[1],
+        normed_attn,
+    )
+    layer_output, input_grad, down_g, gate_g, up_g, out_g, qkv_g, gains_all = backward(
+        parts, operands, ny, nz
+    )
+    gain_sum = jnp.sum(gains_all, axis=(0, 1, 2))
     place = ((y * 2 + c) * nz + z) * block
     gain_own = lax.dynamic_slice_in_dim(gain_sum, place, block, 1)
-    q_width = 4 * DH
+    q_width, kv_width = 4 * DH, 2 * DH
     return (
         layer_output.reshape(1, span, width),
         input_grad.reshape(1, span, width),
@@ -1205,30 +1410,6 @@
         join(up_g),
         join(down_g).T,
     )
-
-
-def core_both(rows):
-    def kernel(own, both, ss, rs, ls):
-        c = lax.axis_index("pr")
-        greet([({"pr": 1 - c}, None)], 1)
-        local = pltpu.make_async_copy(own, both.at[c], ls.at[0])
-        copy = remote(own, both.at[c], ss.at[0], rs.at[0], {"pr": 1 - c})
-        local.start()
-        copy.start()
-        copy.wait()
-        local.wait()
-
-    dma = pltpu.SemaphoreType.DMA
-    vmem = pl.BlockSpec(memory_space=pltpu.VMEM)
-    return pl.pallas_call(
-        kernel,
-        out_shape=jax.ShapeDtypeStruct((2,) + rows.shape, rows.dtype),
-        in_specs=[vmem],
-        out_specs=vmem,
-        scratch_shapes=[dma((1,)), dma((1,)), dma((1,))],
-        name="core_both",
-        compiler_params=pltpu.CompilerParams(collective_id=5, has_side_effects=True),
-    )(rows)
 
 
 def solution(mesh):

time: 645 us -> 499 us (0.77)
  Pallas kernels: 491 us -> 421 us
  matrix products: 73.5 us -> 36.3 us
  other arithmetic: 38 us -> 18.8 us
  local copies, waits for them, and re-layouts: 30.3 us -> 13.2 us
    pallas_call x6 -> x1, Pallas kernels: 340 us -> 270 us  [backward(): pl.pallas_call(functools.partial(backward_kernel, nz, DH ** (-0.5)), out_...]
    dot_general x21 -> x0, matrix products: 29.3 us -> none  [the longest x4 7.24 us: backward_block(): jnp.einsum('qd,kd->qk', bq, bk, preferred_element_type=F32) * score_scale]
    convert_element_type x7 -> x0, other arithmetic: 13.9 us -> none  [the longest x1 12.4 us: on_device(): residual_grad.astype(BF16)]
    dot_general x11 -> x6, matrix products: 35.5 us -> 27.7 us  [contract(): lax.dot_general(left, right, (((left_dim,), (right_dim,)), ((), ())), pre...]
where the time goes in v2:
time: 499 us; the launch traced here: 490 us
  Pallas kernels  421 us (84%)
  matrix products  36.3 us (7%)
  other arithmetic  18.8 us (4%)
  local copies, waits for them, and re-layouts  13.2 us (3%)
    pallas_call x1, Pallas kernels, backward(): pl.pallas_call(functools.partial(backward_kernel, nz, DH ** (-0.5)), out_...  270 us
    pallas_call x1, Pallas kernels, forward(): pl.pallas_call(functools.partial(forward_kernel, nz, items, DH ** (-0.5))...  136 us
    dot_general x6, matrix products, contract(): lax.dot_general(left, right, (((left_dim,), (right_dim,)), ((), ())), pre...  27.7 us
    pallas_call x1, Pallas kernels, pair_swap(): pl.pallas_call(functools.partial(pair_kernel, nz, ng), out_shape=shapes,...  14.7 us

profile of v2, /device:TPU:11, one launch (start us, length us, event | category | flops | bytes accessed | tf_op | source)
XLA Modules:
  0.0 490.5 jit_solution(7362449092736577128)
XLA Ops:
  0.7 0.8 convert_element_type.57
  1.4 0.7 convert_element_type.58
  2.1 0.7 bitcast_convert_fusion
  2.8 0.6 concatenate.34.refs_5_
  3.4 0.9 slice_bitcast_fusion.23
  4.4 0.9 slice_bitcast_fusion.21
  5.3 0.7 pad_maximum_fusion.10.refs_1_
  6.0 1.0 slice_bitcast_fusion.25
  7.0 0.8 maximum_maximum_fusion.refs_0_
  7.8 0.9 fusion.4.refs_11_.refs_14_
  8.8 0.9 pad_maximum_fusion.2
  9.7 0.8 pad_maximum_fusion.4.refs_4_
  10.5 14.7 %pair_swap.1 = (bf16[2,96,768]{2,1,0:T(8,128)(2,1)}, bf16[2,96,384]{2,1,0:T(8,128)(2,1)}, bf16[2,96,1024]{2,1,0:T(8,128)(2,1)}, bf16[2,96,1024]{2,1,0:T(8,128)(2...) custom-call(bf16[2,96,768]{2,1,0:T(8,128)(2,1)} %maximum_maximum_fus, ...), custom_call_target="tpu_custom_call" | custom-call | tf_op jit(solution)/shard_map/pair_swap/pallas_call | solution.py:148
  25.2 1.9 multiply_reduce_fusion
  27.1 1.0 slice_reduce_fusion
  28.1 0.8 dynamic-slice_bitcast_fusion
  28.9 0.7 reshape_reshape_squeeze.2.refs_12_.refs_8_
  29.6 0.7 broadcast_in_dim_reshape_squeeze.3.refs_9_
  30.4 1.7 fusion.1.refs_5_.refs_23_
  32.1 1.1 tile.12.refs_9_.refs_12_
  33.2 1.0 fusion.7
  34.2 1.1 pad_maximum_fusion.5
  35.4 135.9 %forward.1 = (bf16[2,2,4,96,768]{4,3,2,1,0:T(8,128)(2,1)}, bf16[2,2,4,96,384]{4,3,2,1,0:T(8,128)(2,1)}, bf16[2,2,4,96,1024]{4,3,2,1,0:T(8,128)(2,1)}, bf16[2,2,4...) custom-call(bf16[2,96,768]{2,1,0:T(8,128)(2,1)} %get-tuple-element.4, ...), custom_call_target="tpu_custom_call" | custom-call | tf_op jit(solution)/shard_map/forward/pallas_call | solution.py:526
  171.3 4.3 fusion.17
  175.7 1.8 fusion.18
  177.6 0.5 copy-done.14
  178.0 2.5 multiply_convert_fusion
  180.6 3.0 convolution_convert_fusion.3
  183.5 1.8 fusion.19
  185.4 3.0 fusion.2
  188.4 3.5 convolution_convert_fusion.2
  191.8 12.9 %convolution_convert_fusion = bf16[1536,1024]{1,0:T(8,128)(2,1)} fusion(bf16[512,1536]{1,0:T(8,128)(2,1)S(1)} %bitcast.156, bf16[512,1024]{1,0:T(8,128)(2,1)S(1)} %get-tuple-element.71), kind=kOutput, calls=%fused_computation | convolution fusion | flops 1612185600 | bytes 5767168 | tf_op jit(solution)/shard_map/dot_general | solution.py:33
  204.8 3.5 convolution_convert_fusion.1
  208.3 270.2 %backward.1 = (bf16[256,1536]{1,0:T(8,128)(2,1)}, bf16[256,1536]{1,0:T(8,128)(2,1)}, f32[2,96,1024]{2,1,0:T(8,128)}, f32[2,96,1024]{2,1,0:T(8,128)}, f32[2,96,10...) custom-call(bf16[2,2,4,96,1024]{4,3,2,1,0:T(8,128)(2,1)} %bitcast.128, ...), custom_call_target="tpu_custom_call" | custom-call | tf_op jit(solution)/shard_map/backward/pallas_call | solution.py:1203
  478.5 1.1 reduce_sum.19
  479.6 0.5 slice_bitcast_fusion.28
  480.2 1.0 slice_bitcast_fusion.13
  481.2 0.7 maximum_bitcast_fusion.1
  481.9 1.0 slice_bitcast_fusion.15
  482.9 0.1 slice_bitcast_fusion.17
  483.0 0.8 pad_maximum_fusion.12
  483.8 0.7 pad_maximum_fusion.9
  484.5 0.8 pad_maximum_fusion.11
  485.4 0.9 pad_maximum_fusion
  486.4 0.9 pad_maximum_fusion.1
  487.4 0.9 maximum_bitcast_fusion
  488.3 0.9 copy.32
  489.2 0.9 copy.33
  (51 shorter events, 0.7 us)
Async XLA Ops:
  0.6 8.1 %copy-start.8 = (bf16[96,2048]{1,0:T(8,128)(2,1)S(1)}, bf16[96,2048]{1,0:T(8,128)(2,1)}, u32[]{:S(2)}) copy-start(bf16[96,2048]{1,0:T(8,128)(2,1)} %param.23) | copy-start | bytes 1179652
  0.7 8.0 %copy-start.7 = (bf16[96,2048]{1,0:T(8,128)(2,1)S(1)}, bf16[96,2048]{1,0:T(8,128)(2,1)}, u32[]{:S(2)}) copy-start(bf16[96,2048]{1,0:T(8,128)(2,1)} %param.22) | copy-start | bytes 1179652
  7.0 2.7 copy-start.9
  25.2 5.2 %copy-start = (bf16[2,256,1536]{2,1,0:T(8,128)(2,1)S(1)}, bf16[2,256,1536]{2,1,0:T(8,128)(2,1)}, u32[]{:S(2)}) copy-start(bf16[2,256,1536]{2,1,0:T(8,128)(2,1)} %get-tuple-element.46) | copy-start | bytes 4718596
  28.9 5.3 %copy-start.10 = (s32[2,4,2,128]{3,2,1,0:T(2,128)}, s32[2,4,2,128]{3,2,1,0:T(2,128)S(1)}, u32[]{:S(2)}) copy-start(s32[2,4,2,128]{3,2,1,0:T(2,128)S(1)} %get-tuple-element.105) | copy-start | bytes 24580
  171.3 4.3 copy-start.11
  171.3 4.3 copy-start.15
  175.7 1.9 copy-start.13
  175.7 2.3 copy-start.14
  180.6 3.0 copy-start.12
  478.4 4.5 copy-start.1
  478.5 6.8 %copy-start.6 = (f32[2,96,1024]{2,1,0:T(8,128)S(1)}, f32[2,96,1024]{2,1,0:T(8,128)}, u32[]{:S(2)}) copy-start(f32[2,96,1024]{2,1,0:T(8,128)} %get-tuple-element.66) | copy-start | bytes 2359300
  483.8 2.5 copy-start.5
  485.4 2.0 copy-start.4
  486.4 2.0 copy-start.3
  487.3 1.9 copy-start.2

commit v3 on v2

--- a/solution.py
+++ b/solution.py
@@ -165,124 +165,90 @@
     return results[:ng], results[ng], results[ng + 1], results[ng + 2]
 
 
+def low_bit(number):
+    return (number & -number).bit_length() - 1
+
+
+class Line:
+    def __init__(self, nz):
+        self.nz, self.levels = nz, nz.bit_length() - 1
+        self.z = lax.axis_index("ctx")
+        self.bits = [lax.rem(self.z // (1 << level), 2) for level in range(self.levels)]
+
+    def at(self, offset):
+        place = self.z
+        for level in range(self.levels):
+            if offset >> level & 1:
+                place = place + (1 << level) - (2 << level) * self.bits[level]
+        return place
+
+    def partner(self, level):
+        return self.at(1 << level)
+
+
 class Gather:
-    def __init__(self, nz, outs, us, ur, ds, dr, ys, yr, es, er):
-        self.nz, self.outs = nz, outs
-        self.sems = (us, ur, ds, dr, ys, yr, es, er)
+    def __init__(self, line, outs, zs, zr, ys, yr, es, er):
+        self.line, self.outs = line, outs
+        self.zs, self.zr, self.ys, self.yr, self.es, self.er = zs, zr, ys, yr, es, er
         self.y = lax.axis_index("fy")
-        self.z = lax.axis_index("ctx")
-        self.odd = lax.rem(self.z, 2)
-        self.pair = self.z + 1 - 2 * self.odd
-
-    def up(self, g, s, slot):
-        piece = self.outs[g].at[self.y, :, self.z - s]
-        us, ur = self.sems[0], self.sems[1]
-        return remote(piece, piece, us.at[g, slot], ur.at[g, slot], {"ctx": self.z + 1})
-
-    def down(self, g, s, slot):
-        piece = self.outs[g].at[self.y, :, self.z + s]
-        ds, dr = self.sems[2], self.sems[3]
-        return remote(piece, piece, ds.at[g, slot], dr.at[g, slot], {"ctx": self.z - 1})
-
-    def across(self, g, slot, origin, half, row):
-        piece = self.outs[g].at[row, 0, origin] if half else self.outs[g].at[row, :, origin]
-        ys, yr = self.sems[4], self.sems[5]
-        return remote(piece, piece, ys.at[g, slot], yr.at[g, slot], {"fy": 1 - self.y})
-
-    def extra(self, g, origin):
-        piece = self.outs[g].at[1 - self.y, 1, origin]
-        es, er = self.sems[6], self.sems[7]
-        return remote(piece, piece, es.at[g], er.at[g], {"ctx": self.pair})
+        offsets = range(1, line.nz)
+        self.arrivals = sorted(offsets, key=lambda offset: (-low_bit(offset), offset))
+
+    def hop(self, g, offset, level):
+        piece = self.outs[g].at[self.y, :, self.line.at(offset)]
+        slot = offset + (1 << level)
+        return remote(
+            piece, piece, self.zs.at[g, slot], self.zr.at[g, slot], {"ctx": self.line.partner(level)}
+        )
+
+    def hop_from(self, g, offset):
+        piece = self.outs[g].at[self.y, :, self.line.at(offset)]
+        partner = self.line.partner(low_bit(offset))
+        return remote(piece, piece, self.zs.at[g, offset], self.zr.at[g, offset], {"ctx": partner})
+
+    def across(self, g, offset, row):
+        place = self.line.at(offset)
+        piece = self.outs[g].at[row, 0, place] if offset == 1 else self.outs[g].at[row, :, place]
+        return remote(
+            piece, piece, self.ys.at[g, offset], self.yr.at[g, offset], {"fy": 1 - self.y}
+        )
+
+    def extra(self, g, offset):
+        piece = self.outs[g].at[1 - self.y, 1, self.line.at(offset)]
+        return remote(piece, piece, self.es.at[g], self.er.at[g], {"ctx": self.line.partner(0)})
+
+    def hops(self, offset):
+        last = low_bit(offset) if offset else self.line.levels
+        return reversed(range(last))
 
     def own_z(self, g):
-        @pl.when(self.z < self.nz - 1)
-        def _():
-            self.up(g, 0, 0).start()
-
-        @pl.when(self.z > 0)
-        def _():
-            self.down(g, 0, 0).start()
+        for level in self.hops(0):
+            self.hop(g, 0, level).start()
 
     def own_y(self, g):
-        self.across(g, 0, self.z, False, self.y).start()
-
-    def each_across(self, g, s, row, act):
-        z, nz = self.z, self.nz
-        if s == 0:
-            act(self.across(g, 0, z, False, row))
-            return
-        if s == 1:
-
-            @pl.when(self.odd == 1)
-            def _():
-                act(self.across(g, 1, z - 1, True, row))
-
-            @pl.when((self.odd == 0) & (z > 0))
-            def _():
-                act(self.across(g, 1, z - 1, False, row))
-
-            @pl.when(self.odd == 0)
-            def _():
-                act(self.across(g, nz, z + 1, True, row))
-
-            @pl.when((self.odd == 1) & (z < nz - 1))
-            def _():
-                act(self.across(g, nz, z + 1, False, row))
-
-            return
-
-        @pl.when(z >= s)
-        def _():
-            act(self.across(g, s, z - s, False, row))
-
-        @pl.when(z + s < nz)
-        def _():
-            act(self.across(g, nz - 1 + s, z + s, False, row))
-
-    def step(self, g, s):
-        z, nz = self.z, self.nz
-
-        @pl.when(z >= s)
-        def _():
-            self.up(g, s - 1 + 1, s - 1).wait_recv()
-
-            @pl.when(z < nz - 1)
-            def _():
-                self.up(g, s, s).start()
-
-        @pl.when(z + s < nz)
-        def _():
-            self.down(g, s, s - 1).wait_recv()
-
-            @pl.when(z > 0)
-            def _():
-                self.down(g, s, s).start()
-
-        self.each_across(g, s, self.y, lambda copy: copy.start())
+        self.across(g, 0, self.y).start()
+
+    def step(self, g, offset):
+        self.hop_from(g, offset).wait_recv()
+        for level in self.hops(offset):
+            self.hop(g, offset, level).start()
+        self.across(g, offset, self.y).start()
 
     def spread(self, g):
-        self.across(g, 0, self.z, False, 1 - self.y).wait_recv()
-        self.extra(g, self.z).start()
+        self.across(g, 0, 1 - self.y).wait_recv()
+        self.extra(g, 0).start()
 
     def finish(self, g):
-        for s in range(1, self.nz):
-            self.each_across(g, s, 1 - self.y, lambda copy: copy.wait_recv())
-        self.extra(g, self.pair).wait_recv()
+        for offset in self.arrivals:
+            self.across(g, offset, 1 - self.y).wait_recv()
+        self.extra(g, 1).wait_recv()
 
     def drain(self, g):
-        z, nz = self.z, self.nz
-        for s in range(nz):
-
-            @pl.when((z >= s) & (z < nz - 1))
-            def _(s=s):
-                self.up(g, s, s).wait_send()
-
-            @pl.when((z + s < nz) & (z > 0))
-            def _(s=s):
-                self.down(g, s, s).wait_send()
-
-            self.each_across(g, s, self.y, lambda copy: copy.wait_send())
-        self.extra(g, self.z).wait_send()
+        for offset in (0, *self.arrivals):
+            for level in self.hops(offset):
+                self.hop(g, offset, level).wait_send()
+            self.across(g, offset, self.y).wait_send()
+        self.extra(g, 0).wait_send()
 
 
 def forward_kernel(nz, items, scale, *refs):
@@ -290,8 +256,8 @@
     pieces = refs[:5]
     outs = refs[13:18]
     (q_out, k_out, v_out, mixed_out, mixed_low, lse_out, residual, normed_mlp) = refs[18:26]
-    (acc, kvu, top, core_send, core_land, x_send, x_land, attended) = refs[26:34]
-    loc, us, ur, ds, dr, ys, yr, es, er, ks, kr, cs, cr, xs, xr, ns, nr = refs[34:]
+    (acc, kvu, top, core_send, core_land, x_send, x_land) = refs[26:33]
+    loc, zs, zr, ys, yr, es, er, ks, kr, cs, cr, xs, xr, ns, nr = refs[33:]
     y = lax.axis_index("fy")
     c = lax.axis_index("pr")
     z = lax.axis_index("ctx")
@@ -299,16 +265,12 @@
     span = rows.shape[0]
     other_c = {"pr": 1 - c}
     other_x = {"tp": 1 - x}
-    gather = Gather(nz, outs, us, ur, ds, dr, ys, yr, es, er)
+    line = Line(nz)
+    gather = Gather(line, outs, zs, zr, ys, yr, es, er)
     greet(
-        [
-            ({"fy": 1 - y}, None),
-            (other_c, None),
-            (other_x, None),
-            ({"ctx": z + 1}, z < nz - 1),
-            ({"ctx": z - 1}, z > 0),
-        ],
-        3 + (z < nz - 1).astype(jnp.int32) + (z > 0).astype(jnp.int32),
+        [({"fy": 1 - y}, None), (other_c, None), (other_x, None)]
+        + [({"ctx": line.partner(level)}, None) for level in range(line.levels)],
+        3 + line.levels,
     )
     local = [pltpu.make_async_copy(pieces[g], outs[g].at[y, :, z], loc.at[g]) for g in range(5)]
     for copy in local:
@@ -320,16 +282,16 @@
         gather.own_y(g)
     for g in late:
         local[g].wait()
-    for s in range(1, nz):
+    gather.own_y(2)
+    for offset in gather.arrivals:
         for g in early:
-            gather.step(g, s)
-        if s == 1:
+            gather.step(g, offset)
+        if offset == gather.arrivals[0]:
             for g in early:
                 gather.spread(g)
-        if s == min(2, nz - 1):
-            for g in late:
-                gather.own_z(g)
     for g in late:
+        gather.own_z(g)
+    for g in late[1:]:
         gather.own_y(g)
     for g in early:
         gather.finish(g)
@@ -358,13 +320,24 @@
             BF16
         )
 
-    def keys_up(b, s):
-        piece = kvu.at[z - s, b]
-        return remote(piece, piece, ks.at[b, s], kr.at[b, s], {"ctx": z + 1})
-
-    def keys_from(b, s):
-        piece = kvu.at[z - s, b]
-        return remote(piece, piece, ks.at[b, s - 1], kr.at[b, s - 1], {"ctx": z - 1})
+    def keys_hop(b, offset, level):
+        piece = kvu.at[line.at(offset), b]
+        slot = offset + (1 << level)
+        return remote(
+            piece, piece, ks.at[b, slot], kr.at[b, slot], {"ctx": line.partner(level)}
+        )
+
+    def keys_from(b, offset):
+        piece = kvu.at[line.at(offset), b]
+        partner = line.partner(low_bit(offset))
+        return remote(piece, piece, ks.at[b, offset], kr.at[b, offset], {"ctx": partner})
+
+    def each_hop(offset, act):
+        for level in gather.hops(offset):
+
+            @pl.when(line.at(offset) <= line.partner(level))
+            def _(level=level):
+                act(level)
 
     for b in range(2):
         fields = []
@@ -377,10 +350,7 @@
             ].astype(BF16)
             fields.append(v_out[z, b * 2 + k])
         kvu[z, b] = dot(jnp.concatenate(fields, axis=1), spread_mat[...], 1, 1).astype(BF16)
-
-        @pl.when(z < nz - 1)
-        def _(b=b):
-            keys_up(b, 0).start()
+        each_hop(0, lambda level, b=b: keys_hop(b, 0, level).start())
 
     for b in range(2):
         for k in range(2):
@@ -416,28 +386,23 @@
         lax.fori_loop(0, items, one, 0)
 
     attend(z, True)
-    for g in late:
-        gather.step(g, 1)
-    for s in range(1, nz):
-
-        @pl.when(z >= s)
-        def _(s=s):
+    for place, offset in enumerate(gather.arrivals):
+        from_there = line.at(offset)
+
+        @pl.when(from_there <= z)
+        def _(offset=offset, from_there=from_there):
             for b in range(2):
-                keys_from(b, s).wait_recv()
-
-                @pl.when(z < nz - 1)
-                def _(b=b):
-                    keys_up(b, s).start()
-
-                wide = dot(kvu[z - s, b], spread_mat[...]).astype(BF16)
+                keys_from(b, offset).wait_recv()
+                each_hop(offset, lambda level, b=b: keys_hop(b, offset, level).start())
+                wide = dot(kvu[from_there, b], spread_mat[...]).astype(BF16)
                 for k in range(2):
-                    k_out[z - s, b * 2 + k] = wide[:, k * LANES : (k + 1) * LANES]
-                    v_out[z - s, b * 2 + k] = wide[:, (2 + k) * LANES : (3 + k) * LANES]
-            attend(z - s, False)
-
-        if s == 1:
+                    k_out[from_there, b * 2 + k] = wide[:, k * LANES : (k + 1) * LANES]
+                    v_out[from_there, b * 2 + k] = wide[:, (2 + k) * LANES : (3 + k) * LANES]
+            attend(from_there, False)
+
+        if place == 0:
             for g in late:
-                gather.spread(g)
+                gather.step(g, offset)
 
     for i in range(items):
         total = lse_out[i]
@@ -453,8 +418,7 @@
             jnp.concatenate(heads, axis=1), spread_mat[...], 1, 1
         ).astype(BF16)
     for g in late:
-        if nz > 2:
-            gather.step(g, 2)
+        gather.spread(g)
 
     def core(i):
         return remote(core_send.at[i], core_land.at[i], cs.at[i], cr.at[i], other_c)
@@ -474,9 +438,9 @@
         core(i).wait_recv()
         x_send[i] = (part + core_land[i].astype(F32)).astype(BF16)
         sideways(i).start()
-    for s in range(3, nz):
+    for offset in gather.arrivals[1:]:
         for g in late:
-            gather.step(g, s)
+            gather.step(g, offset)
     squares = jnp.zeros((span, 1), F32)
     for i in range(4):
         sideways(i).wait_recv()
@@ -494,11 +458,12 @@
     for g in range(5):
         gather.drain(g)
     for b in range(2):
-        for s in range(nz):
-
-            @pl.when((z >= s) & (z < nz - 1))
-            def _(b=b, s=s):
-                keys_up(b, s).wait_send()
+        each_hop(0, lambda level, b=b: keys_hop(b, 0, level).wait_send())
+        for offset in gather.arrivals:
+
+            @pl.when(line.at(offset) <= z)
+            def _(b=b, offset=offset):
+                each_hop(offset, lambda level: keys_hop(b, offset, level).wait_send())
 
     for i in range(4):
         core(i).wait_send()
@@ -534,10 +499,8 @@
             pltpu.VMEM((items, q_rows, LANES), F32),
         ]
         + [pltpu.VMEM((4, span, chunk), BF16)] * 4
-        + [pltpu.VMEM((8, LANES), F32)]
         + [dma((5,))]
         + [dma((5, nz))] * 4
-        + [dma((5, 2 * nz))] * 2
         + [dma((5,))] * 2
         + [dma((2, nz))] * 2
         + [dma((4,))] * 4
@@ -549,45 +512,34 @@
     )(*pieces, normed, rows, cos, sin, q_seg, k_seg, spread_mat, gain)
 
 
-def inward(nz):
-    order = []
-    for k in range((nz + 1) // 2):
-        order.append(nz - 1 - k)
-        if k != nz - 1 - k:
-            order.append(k)
-    return order
-
-
 OWN = 3
 
 
 class Scatter:
-    def __init__(self, nz, sources, owns, lands, ins, overs, mids, extras, totals, outs, sems):
-        self.nz, self.sources, self.owns, self.lands = nz, sources, owns, lands
-        self.ins, self.overs, self.mids, self.extras = ins, overs, mids, extras
+    def __init__(self, line, sources, owns, lands, ins, mids, extras, totals, outs, sems):
+        self.line, self.sources, self.owns, self.lands = line, sources, owns, lands
+        self.ins, self.mids, self.extras = ins, mids, extras
         self.totals, self.outs, self.sems = totals, outs, sems
         self.y = lax.axis_index("fy")
         self.c = lax.axis_index("pr")
-        self.z = lax.axis_index("ctx")
-        self.pair = self.z + 1 - 2 * lax.rem(self.z, 2)
-        self.order = inward(nz)
+        nz = line.nz
+        self.order = sorted(range(1, nz), key=lambda offset: (low_bit(offset), -offset)) + [0]
 
     def own_copy(self, g, place):
-        t = self.order[place] if place < self.nz else self.z
         return pltpu.make_async_copy(
-            self.sources[g].at[self.y, :, t],
+            self.sources[g].at[self.y, :, self.line.at(self.order[place])],
             self.owns[g].at[place % 2],
             self.sems[0].at[g, 3 + place % 2],
         )
 
     def own(self, g, place, k, rows):
         if self.owns[g] is None:
-            t = self.order[place] if place < self.nz else self.z
-            return self.sources[g][self.y, k, t, rows].astype(F32)
+            place_at = self.line.at(self.order[place])
+            return self.sources[g][self.y, k, place_at, rows].astype(F32)
         return self.owns[g][place % 2, k, rows].astype(F32)
 
     def fetch(self, g, place):
-        if self.owns[g] is not None and place <= self.nz:
+        if self.owns[g] is not None and place < self.line.nz:
             self.own_copy(g, place).start()
 
     def fetched(self, g, place):
@@ -596,49 +548,38 @@
 
     def middle(self, g):
         return pltpu.make_async_copy(
-            self.sources[g].at[1 - self.y, 1, self.z], self.mids[g], self.sems[0].at[g, 1]
-        )
-
-    def across(self, g, t, part):
+            self.sources[g].at[1 - self.y, 1, self.line.z], self.mids[g], self.sems[0].at[g, 1]
+        )
+
+    def across(self, g, offset):
         ys, yr = self.sems[1], self.sems[2]
-        src, dst = self.sources[g], self.lands[g]
-        if part == "both":
-            src, dst = src.at[1 - self.y, :, t], dst.at[t]
+        src, dst, place = self.sources[g], self.lands[g], self.line.at(offset)
+        if offset > 1:
+            src, dst = src.at[1 - self.y, :, place], dst.at[offset]
         else:
-            src, dst = src.at[1 - self.y, 0, t], dst.at[t, 0]
-        return remote(src, dst, ys.at[g, t], yr.at[g, t], {"fy": 1 - self.y})
+            src, dst = src.at[1 - self.y, 0, place], dst.at[offset, 0]
+        return remote(src, dst, ys.at[g, offset], yr.at[g, offset], {"fy": 1 - self.y})
 
     def relayed(self, g):
         ys, yr = self.sems[1], self.sems[2]
+        slot = self.line.nz
         return remote(
-            self.mids[g],
-            self.lands[g].at[self.z, 1],
-            ys.at[g, self.nz],
-            yr.at[g, self.nz],
-            {"fy": 1 - self.y},
+            self.mids[g], self.lands[g].at[0, 1], ys.at[g, slot], yr.at[g, slot], {"fy": 1 - self.y}
         )
 
     def extra(self, g):
         es, er = self.sems[3], self.sems[4]
-        src = self.sources[g].at[1 - self.y, 1, self.pair]
-        return remote(src, self.extras[g], es.at[g], er.at[g], {"ctx": self.pair})
-
-    def up(self, g, t):
+        src = self.sources[g].at[1 - self.y, 1, self.line.at(1)]
+        return remote(src, self.extras[g], es.at[g], er.at[g], {"ctx": self.line.partner(0)})
+
+    def hop(self, g, offset):
         zs, zr = self.sems[5], self.sems[6]
         return remote(
-            self.lands[g].at[t], self.ins[g].at[t], zs.at[g, 0, t], zr.at[g, 0, t], {"ctx": self.z + 1}
-        )
-
-    def down(self, g, t):
-        zs, zr = self.sems[5], self.sems[6]
-        return remote(
-            self.lands[g].at[t], self.ins[g].at[t], zs.at[g, 1, t], zr.at[g, 1, t], {"ctx": self.z - 1}
-        )
-
-    def down_home(self, g, t):
-        zs, zr = self.sems[5], self.sems[6]
-        return remote(
-            self.lands[g].at[t], self.overs[g], zs.at[g, 1, t], zr.at[g, 1, t], {"ctx": self.z - 1}
+            self.lands[g].at[offset],
+            self.ins[g].at[offset - 1],
+            zs.at[g, offset],
+            zr.at[g, offset],
+            {"ctx": self.line.partner(low_bit(offset))},
         )
 
     def swap(self, g, slot):
@@ -668,18 +609,9 @@
         self.extra(g).start()
         self.fetch(g, 0)
         self.fetch(g, 1)
-        self.lands[g][self.pair, 1] = jnp.zeros(self.lands[g].shape[2:], BF16)
-        for t in self.order:
-
-            @pl.when((self.z != t) & (self.pair != t))
-            def _(t=t):
-                self.across(g, t, "both").start()
-
-            @pl.when(self.pair == t)
-            def _(t=t):
-                self.across(g, t, "half").start()
-
-        self.across(g, self.z, "half").start()
+        self.lands[g][1, 1] = jnp.zeros(self.lands[g].shape[2:], BF16)
+        for offset in self.order:
+            self.across(g, offset).start()
 
     def relay(self, g):
         self.middle(g).wait()
@@ -690,95 +622,42 @@
         self.relayed(g).start()
 
     def step(self, g, place):
-        z, nz, t = self.z, self.nz, self.order[place]
+        offset = self.order[place]
         land, into = self.lands[g], self.ins[g]
         self.fetched(g, place)
-
-        @pl.when(z != t)
-        def _():
-            @pl.when(self.pair != t)
-            def _():
-                self.across(g, t, "both").wait_recv()
-
-            @pl.when(self.pair == t)
-            def _():
-                self.across(g, t, "half").wait_recv()
-
-            inner = ((z < t) & (z > 0)) | ((z > t) & (z < nz - 1))
-
-            @pl.when(inner)
-            def _():
-                @pl.when(z < t)
-                def _():
-                    self.up(g, t).wait_recv()
-
-                @pl.when(z > t)
-                def _():
-                    self.down(g, t).wait_recv()
-
-                def add(k, rows):
-                    land[t, k, rows] = (
-                        self.own(g, place, k, rows)
-                        + land[t, k, rows].astype(F32)
-                        + into[t, k, rows].astype(F32)
-                    ).astype(BF16)
-
-                self.each_tile(g, add)
-
-            @pl.when(jnp.logical_not(inner))
-            def _():
-                def add(k, rows):
-                    land[t, k, rows] = (
-                        self.own(g, place, k, rows) + land[t, k, rows].astype(F32)
-                    ).astype(BF16)
-
-                self.each_tile(g, add)
-
-            @pl.when(z < t)
-            def _():
-                self.up(g, t).start()
-
-            @pl.when(z > t + 1)
-            def _():
-                self.down(g, t).start()
-
-            @pl.when(z == t + 1)
-            def _():
-                self.down_home(g, t).start()
-
+        self.across(g, offset).wait_recv()
+        arrived = [offset ^ (1 << level) for level in range(low_bit(offset))]
+        for other in arrived:
+            self.hop(g, other).wait_recv()
+
+        def add(k, rows):
+            total = self.own(g, place, k, rows) + land[offset, k, rows].astype(F32)
+            for other in arrived:
+                total = total + into[other - 1, k, rows].astype(F32)
+            land[offset, k, rows] = total.astype(BF16)
+
+        self.each_tile(g, add)
+        self.hop(g, offset).start()
         self.fetch(g, place + 2)
 
     def last(self, g):
-        z, nz = self.z, self.nz
-        land, into, over = self.lands[g], self.ins[g], self.overs[g]
-        self.fetched(g, nz)
+        place = self.line.nz - 1
+        land, into = self.lands[g], self.ins[g]
         total = self.totals[g]
-        self.across(g, z, "half").wait_recv()
+        self.fetched(g, place)
+        self.across(g, 0).wait_recv()
         self.relayed(g).wait_recv()
-
-        def base(k, rows):
-            total[k, rows] = self.own(g, nz, k, rows) + land[z, k, rows].astype(F32)
-
-        self.each_tile(g, base)
-
-        @pl.when(z > 0)
-        def _():
-            self.up(g, z).wait_recv()
-
-            def add(k, rows):
-                total[k, rows] += into[z, k, rows].astype(F32)
-
-            self.each_tile(g, add)
-
-        @pl.when(z < nz - 1)
-        def _():
-            self.down_home(g, z).wait_recv()
-
-            def add(k, rows):
-                total[k, rows] += over[k, rows].astype(F32)
-
-            self.each_tile(g, add)
-
+        arrived = [1 << level for level in range(self.line.levels)]
+        for other in arrived:
+            self.hop(g, other).wait_recv()
+
+        def add(k, rows):
+            value = self.own(g, place, k, rows) + land[0, k, rows].astype(F32)
+            for other in arrived:
+                value = value + into[other - 1, k, rows].astype(F32)
+            total[k, rows] = value
+
+        self.each_tile(g, add)
         self.swap(g, self.c).start()
         self.keep(g).start()
 
@@ -788,24 +667,10 @@
         self.keep(g).wait()
         self.extra(g).wait_send()
         self.relayed(g).wait_send()
-        self.across(g, self.z, "half").wait_send()
-        for t in self.order:
-
-            @pl.when((self.z != t) & (self.pair != t))
-            def _(t=t):
-                self.across(g, t, "both").wait_send()
-
-            @pl.when(self.pair == t)
-            def _(t=t):
-                self.across(g, t, "half").wait_send()
-
-            @pl.when(self.z < t)
-            def _(t=t):
-                self.up(g, t).wait_send()
-
-            @pl.when(self.z > t)
-            def _(t=t):
-                self.down(g, t).wait_send()
+        for offset in self.order:
+            self.across(g, offset).wait_send()
+            if offset:
+                self.hop(g, offset).wait_send()
 
 
 class TokenSum:
@@ -867,16 +732,16 @@
     gains = refs[31]
     scratch = refs[32:]
     owns = (*scratch[:OWN], None, None)
-    lands, ins, overs, mids, extras, totals = (
-        scratch[OWN + 5 * i : OWN + 5 * i + 5] for i in range(6)
+    lands, ins, mids, extras, totals = (
+        scratch[OWN + 5 * i : OWN + 5 * i + 5] for i in range(5)
     )
     (
         o_part, qkv_part, core_send, core_land, x_send, x_land, back_rows, low_rows, grad_items,
         delta, dq, kv_send, kv_land, qkv_rows, gain_rows, keys, values,
-    ) = scratch[OWN + 30 : OWN + 47]
+    ) = scratch[OWN + 25 : OWN + 42]
     (
         loc, ys, yr, es, er, zs, zr, ss, sr, cs, cr, xs, xr, ns, nr, ks, kr, gs, gr, ts, tr, bs,
-    ) = scratch[OWN + 47 :]
+    ) = scratch[OWN + 42 :]
     y = lax.axis_index("fy")
     c = lax.axis_index("pr")
     z = lax.axis_index("ctx")
@@ -884,8 +749,9 @@
     chunk = width // 4
     half = 4 * DH
     sources = (*sources, o_part, qkv_part)
+    line = Line(nz)
     scatter = Scatter(
-        nz, sources, owns, lands, ins, overs, mids, extras, totals, outs,
+        line, sources, owns, lands, ins, mids, extras, totals, outs,
         (loc, ys, yr, es, er, zs, zr, ss, sr),
     )
     greet(
@@ -904,10 +770,13 @@
     def columns(i):
         return pl.ds(i * chunk, chunk)
 
+    scatter.start(0)
     first = TokenSum(lambda who, i: dx_part[who, :, columns(i)], bufs, sems, 0)
     first.start()
-    for g in late:
-        scatter.start(g)
+    scatter.start(2)
+    scatter.step(0, 0)
+    scatter.step(0, 1)
+    scatter.start(1)
 
     squares = jnp.zeros((span, 1), F32)
     inner_sum = jnp.zeros((span, 1), F32)
@@ -934,12 +803,7 @@
     first.drain()
     swap = remote(low_rows.at[c], low_rows.at[c], ns.at[0], nr.at[0], {"pr": 1 - c})
     swap.start()
-    for g in late:
-        scatter.relay(g)
     remote(low_rows.at[1 - c], low_rows.at[1 - c], ns.at[0], nr.at[0], {"pr": 1 - c}).wait_recv()
-    second = TokenSum(lambda who, i: out_part[who, :, columns(i)], bufs, sems, 1)
-    second.start()
-
     for b in range(2):
         grads = jnp.zeros((span, half), F32)
         for i in range(4):
@@ -957,9 +821,8 @@
             low_rows[1, :, columns(i)], mixed_low[span:], 0, 0
         )
         o_part[i // 2, i % 2] = part.astype(BF16).reshape(o_part.shape[2:])
-    for g in late:
-        scatter.step(g, 0)
     scatter.start(3)
+    scatter.step(2, 0)
 
     for i in range(4):
         delta[i] = jnp.broadcast_to(
@@ -968,28 +831,46 @@
         )
 
     slots = kv_send.shape[0]
-
-    def keys_down(b, s):
-        t = z - s
+    order = scatter.order
+
+    def keys_hop(b, place):
+        offset = order[place]
         return remote(
-            kv_send.at[s % slots, b], kv_land.at[t, b], ks.at[b, t], kr.at[b, t], {"ctx": z - 1}
-        )
-
-    def keys_from(b, s):
-        t = z - s
-        return remote(
-            kv_send.at[s % slots, b], kv_land.at[t, b], ks.at[b, t], kr.at[b, t], {"ctx": z - 1}
-        )
-
-    def load(s):
+            kv_send.at[place % slots, b],
+            kv_land.at[offset, b],
+            ks.at[b, offset],
+            kr.at[b, offset],
+            {"ctx": line.partner(low_bit(offset))},
+        )
+
+    def keys_add(b, place, offset):
+        remote(
+            kv_send.at[place % slots, b],
+            kv_land.at[offset, b],
+            ks.at[b, offset],
+            kr.at[b, offset],
+            {"ctx": line.partner(low_bit(offset))},
+        ).wait_recv()
+        kv_send[place % slots, b] = (
+            kv_send[place % slots, b].astype(F32) + kv_land[offset, b].astype(F32)
+        ).astype(BF16)
+
+    def load(place):
+        block = line.at(order[place])
         return (
-            pltpu.make_async_copy(k_items.at[z - s], keys.at[s % 2], bs.at[0, s % 2]),
-            pltpu.make_async_copy(v_items.at[z - s], values.at[s % 2], bs.at[1, s % 2]),
-        )
-
-    def back_block(s, diagonal):
-        block, slot = z - s, s % 2
-        for copy in load(s):
+            pltpu.make_async_copy(k_items.at[block], keys.at[place % 2], bs.at[0, place % 2]),
+            pltpu.make_async_copy(v_items.at[block], values.at[place % 2], bs.at[1, place % 2]),
+        )
+
+    def load_start(place):
+        @pl.when(line.at(order[place]) <= z)
+        def _():
+            for copy in load(place):
+                copy.start()
+
+    def back_block(place, diagonal):
+        block, slot = line.at(order[place]), place % 2
+        for copy in load(place):
             copy.wait()
 
         def one(b, _):
@@ -1009,58 +890,67 @@
                 key_grads.append(dot(score_grad, q_items[item], 0, 0) * scale)
                 dq[item] += dot(score_grad, keys[slot, item]) * scale
             wide = jnp.concatenate(key_grads + value_grads, axis=1).astype(BF16)
-            kv_send[s % slots, b] = dot(wide, spread_mat[...], 1, 1).astype(BF16)
+            kv_send[place % slots, b] = dot(wide, spread_mat[...], 1, 1).astype(BF16)
             return 0
 
         lax.fori_loop(0, 2, one, 0)
 
-    dq[...] = jnp.zeros_like(dq)
-    for s in range(nz - 1, -1, -1):
-
-        @pl.when(z == s)
-        def _(s=s):
-            for copy in load(s):
-                copy.start()
-
-    for s in range(nz - 1, 0, -1):
-
-        @pl.when(z >= s)
-        def _(s=s):
-            for copy in load(s - 1):
-                copy.start()
-            if s + slots < nz:
-
-                @pl.when(z >= s + slots)
-                def _():
-                    for b in range(2):
-                        keys_down(b, s + slots).wait_send()
-
-            back_block(s, False)
-            for b in range(2):
-
-                @pl.when(z < nz - 1)
-                def _(b=b):
-                    keys_from(b, s).wait_recv()
-                    kv_send[s % slots, b] = (
-                        kv_send[s % slots, b].astype(F32) + kv_land[z - s, b].astype(F32)
-                    ).astype(BF16)
-
-                keys_down(b, s).start()
-
-        for g in late:
-            scatter.step(g, nz - s)
-    if slots < nz:
-
-        @pl.when(z >= slots)
+    def keys_pass(place):
+        offset = order[place]
+
+        @pl.when(line.at(offset) <= z)
         def _():
             for b in range(2):
-                keys_down(b, slots).wait_send()
-
-    back_block(0, True)
+                for level in range(low_bit(offset)):
+                    keys_add(b, place, offset ^ (1 << level))
+                keys_hop(b, place).start()
+
+    def keys_sent(place):
+        @pl.when(line.at(order[place]) <= z)
+        def _():
+            for b in range(2):
+                keys_hop(b, place).wait_send()
+
+    dq[...] = jnp.zeros_like(dq)
+    final = nz - 1
+    load_start(0)
+    for place in range(final):
+        load_start(place + 1)
+        if place >= slots:
+            keys_sent(place - slots)
+
+        @pl.when(line.at(order[place]) <= z)
+        def _(place=place):
+            back_block(place, False)
+
+        if low_bit(order[place]) == 0 or slots < nz:
+            keys_pass(place)
+    scatter.step(0, 2)
+    scatter.relay(2)
+    if final >= slots:
+        keys_sent(final - slots)
+    back_block(final, True)
+    scatter.relay(0)
+    scatter.step(2, 1)
+    if slots == nz:
+        for place in range(final):
+            if low_bit(order[place]) > 0:
+                keys_pass(place)
+    second = TokenSum(lambda who, i: out_part[who, :, columns(i)], bufs, sems, 1)
+    second.start()
+    scatter.step(1, 0)
+    scatter.step(3, 0)
+    scatter.step(2, 2)
     for i in range(4):
         second.arrived(i)
         layer_out[:, columns(i)] = (residual[:, columns(i)] + second.total(i)).astype(BF16)
     second.drain()
+    for level in range(line.levels):
+
+        @pl.when(line.bits[level] == 0)
+        def _(level=level):
+            for b in range(2):
+                keys_add(b, final, 1 << level)
 
     def unrotated(field, b):
         turned = pltpu.roll(field, LANES // 2, 1)
@@ -1075,15 +965,7 @@
             jnp.concatenate(heads, axis=1), spread_mat[...], 1, 1
         ).astype(BF16)
     for b in range(2):
-
-        @pl.when(z < nz - 1)
-        def _(b=b):
-            keys_from(b, 0).wait_recv()
-            kv_send[0, b] = (
-                kv_send[0, b].astype(F32) + kv_land[z, b].astype(F32)
-            ).astype(BF16)
-
-        wide = dot(kv_send[0, b], spread_mat[...])
+        wide = dot(kv_send[final % slots, b], spread_mat[...])
         fields = [unrotated(wide[:, k * LANES : (k + 1) * LANES], b) for k in range(2)]
         fields += [wide[:, (2 + k) * LANES : (3 + k) * LANES].astype(BF16) for k in range(2)]
         qkv_rows[b, :, half:] = dot(
@@ -1094,6 +976,7 @@
             normed[span:, columns(i)], qkv_rows[1], 0, 0
         )
         qkv_part[i // 2, i % 2] = part.astype(BF16).reshape(qkv_part.shape[2:])
+    scatter.last(0)
     scatter.start(4)
 
     def back_in(who, i):
@@ -1101,11 +984,22 @@
         return dot(qkv_rows[who], weights, 1, 1)
 
     third = TokenSum(back_in, bufs, sems, 2)
+    scatter.step(1, 1)
+    scatter.relay(1)
+    scatter.step(3, 1)
+    scatter.step(1, 2)
+    scatter.step(4, 0)
+    scatter.step(3, 2)
+    scatter.step(4, 1)
+    for g in range(5):
+        for place in range(3, final):
+            scatter.step(g, place)
+    scatter.last(2)
     third.start()
     scatter.relay(3)
+    scatter.last(1)
+    scatter.last(3)
     scatter.relay(4)
-    for g in late:
-        scatter.last(g)
     squares = jnp.zeros((span, 1), F32)
     inner_sum = jnp.zeros((span, 1), F32)
     for i in range(4):
@@ -1147,9 +1041,7 @@
         def _(t=t):
             gain_to(t).start()
 
-    for place in range(nz):
-        scatter.step(3, place)
-        scatter.step(4, place)
+    scatter.step(4, 2)
     for t in range(nz):
 
         @pl.when(z != t)
@@ -1158,7 +1050,6 @@
 
     gain_line = remote(gains.at[y], gains.at[y], ts.at[0], tr.at[0], {"fy": 1 - y})
     gain_line.start()
-    scatter.last(3)
     scatter.last(4)
     remote(gains.at[1 - y], gains.at[1 - y], ts.at[0], tr.at[0], {"fy": 1 - y}).wait_recv()
     for g in range(5):
@@ -1172,12 +1063,8 @@
         def _(t=t):
             gain_to(t).wait_send()
 
-    for s in range(1, slots):
-
-        @pl.when(z >= s)
-        def _(s=s):
-            for b in range(2):
-                keys_down(b, s).wait_send()
+    for place in range(max(0, nz - slots), final):
+        keys_sent(place)
 
 
 def backward(parts, operands, ny, nz):
@@ -1207,8 +1094,7 @@
         out_specs=[vmem] * 2 + [anywhere] * 6,
         scratch_shapes=bufs((2, 2))[:OWN]
         + bufs((nz, 2))
-        + bufs((nz, 2))
-        + bufs((2,))
+        + bufs((nz - 1, 2))
         + bufs(())
         + bufs(())
         + bufs((2,), F32)
@@ -1234,7 +1120,7 @@
         + [dma((5, 5))]
         + [dma((5, nz + 1))] * 2
         + [dma((5,))] * 2
-        + [dma((5, 2, nz))] * 2
+        + [dma((5, nz))] * 2
         + [dma((5,))] * 2
         + [dma((3, 4))] * 4
         + [dma((1,))] * 2

time: 499 us -> 434 us (0.87)
  the two profiles are of different devices: /device:TPU:11 before, /device:TPU:25 now
where the time goes in v3:
time: 434 us; the launch traced here: 426 us
  Pallas kernels  365 us (84%)
  matrix products  27.1 us (6%)
  other arithmetic  18.8 us (4%)
  local copies, waits for them, and re-layouts  13.2 us (3%)
    pallas_call x1, Pallas kernels, forward(): pl.pallas_call(functools.partial(forward_kernel, nz, items, DH ** (-0.5))...  177 us
    pallas_call x1, Pallas kernels, backward(): pl.pallas_call(functools.partial(backward_kernel, nz, DH ** (-0.5)), out_...  174 us
    dot_general x6, matrix products, contract(): lax.dot_general(left, right, (((left_dim,), (right_dim,)), ((), ())), pre...  18.5 us
    pallas_call x1, Pallas kernels, pair_swap(): pl.pallas_call(functools.partial(pair_kernel, nz, ng), out_shape=shapes,...  14.5 us

profile of v3, /device:TPU:25, one launch (start us, length us, event | category | flops | bytes accessed | tf_op | source)
XLA Modules:
  0.0 425.6 jit_solution(898521071834403138)
XLA Ops:
  0.7 0.8 convert_element_type.57
  1.4 0.7 convert_element_type.58
  2.1 0.7 bitcast_convert_fusion
  2.8 0.6 concatenate.34.refs_5_
  3.4 0.9 slice_bitcast_fusion.23
  4.4 0.9 slice_bitcast_fusion.21
  5.3 0.7 pad_maximum_fusion.10.refs_1_
  6.0 1.0 slice_bitcast_fusion.25
  7.0 0.8 maximum_maximum_fusion.refs_0_
  7.8 0.9 fusion.4.refs_11_.refs_14_
  8.8 0.9 pad_maximum_fusion.2
  9.7 0.8 pad_maximum_fusion.4.refs_4_
  10.5 14.5 %pair_swap.1 = (bf16[2,96,768]{2,1,0:T(8,128)(2,1)}, bf16[2,96,384]{2,1,0:T(8,128)(2,1)}, bf16[2,96,1024]{2,1,0:T(8,128)(2,1)}, bf16[2,96,1024]{2,1,0:T(8,128)(2...) custom-call(bf16[2,96,768]{2,1,0:T(8,128)(2,1)} %maximum_maximum_fus, ...), custom_call_target="tpu_custom_call" | custom-call | tf_op jit(solution)/shard_map/pair_swap/pallas_call | solution.py:148
  25.1 1.9 multiply_reduce_fusion
  27.0 1.0 slice_reduce_fusion
  28.0 0.8 dynamic-slice_bitcast_fusion
  28.8 0.7 reshape_reshape_squeeze.2.refs_12_.refs_8_
  29.5 0.7 broadcast_in_dim_reshape_squeeze.3.refs_9_
  30.2 1.7 fusion.1.refs_5_.refs_23_
  31.9 1.1 tile.12.refs_9_.refs_12_
  33.1 1.0 fusion.7
  34.1 1.1 pad_maximum_fusion.5
  35.2 176.7 %forward.1 = (bf16[2,2,4,96,768]{4,3,2,1,0:T(8,128)(2,1)}, bf16[2,2,4,96,384]{4,3,2,1,0:T(8,128)(2,1)}, bf16[2,2,4,96,1024]{4,3,2,1,0:T(8,128)(2,1)}, bf16[2,2,4...) custom-call(bf16[2,96,768]{2,1,0:T(8,128)(2,1)} %get-tuple-element.4, ...), custom_call_target="tpu_custom_call" | custom-call | tf_op jit(solution)/shard_map/forward/pallas_call | solution.py:491
  211.9 4.3 %fusion.17 = f32[512,1024]{1,0:T(8,128)S(1)} fusion(bf16[512,1536]{1,0:T(8,128)(2,1)} %bitcast.154, bf16[1536,1024]{1,0:T(8,128)(2,1)} %bitcast.148), kind=kOutput, calls=%fused_computation.94 | convolution fusion | flops 1610612736 | bytes 6815744 | tf_op jit(solution)/shard_map/dot_general | solution.py:1230
  216.3 1.8 fusion.18
  218.2 0.5 copy-done.14
  218.6 2.5 multiply_convert_fusion
  221.2 3.0 convolution_convert_fusion.3
  224.2 1.8 fusion.19
  226.0 3.2 fusion.2
  229.2 3.5 convolution_convert_fusion.2
  232.7 3.6 convolution_convert_fusion
  236.2 3.5 convolution_convert_fusion.1
  239.7 173.8 %backward.1 = (bf16[256,1536]{1,0:T(8,128)(2,1)}, bf16[256,1536]{1,0:T(8,128)(2,1)}, f32[2,96,1024]{2,1,0:T(8,128)}, f32[2,96,1024]{2,1,0:T(8,128)}, f32[2,96,10...) custom-call(bf16[2,2,4,96,1024]{4,3,2,1,0:T(8,128)(2,1)} %bitcast.128, ...), custom_call_target="tpu_custom_call" | custom-call | tf_op jit(solution)/shard_map/backward/pallas_call | solution.py:1090
  413.5 1.1 reduce_sum.19
  414.7 0.5 slice_bitcast_fusion.28
  415.2 1.0 slice_bitcast_fusion.13
  416.2 0.7 maximum_bitcast_fusion.1
  416.9 1.0 slice_bitcast_fusion.15
  418.0 0.1 slice_bitcast_fusion.17
  418.1 0.8 pad_maximum_fusion.12
  418.8 0.7 pad_maximum_fusion.9
  419.6 0.8 pad_maximum_fusion.11
  420.4 0.9 pad_maximum_fusion
  421.4 0.9 pad_maximum_fusion.1
  422.4 0.9 maximum_bitcast_fusion
  423.4 0.9 copy.32
  424.3 0.9 copy.33
  (51 shorter events, 0.7 us)
Async XLA Ops:
  0.6 8.1 %copy-start.8 = (bf16[96,2048]{1,0:T(8,128)(2,1)S(1)}, bf16[96,2048]{1,0:T(8,128)(2,1)}, u32[]{:S(2)}) copy-start(bf16[96,2048]{1,0:T(8,128)(2,1)} %param.23) | copy-start | bytes 1179652
  0.7 8.0 %copy-start.7 = (bf16[96,2048]{1,0:T(8,128)(2,1)S(1)}, bf16[96,2048]{1,0:T(8,128)(2,1)}, u32[]{:S(2)}) copy-start(bf16[96,2048]{1,0:T(8,128)(2,1)} %param.22) | copy-start | bytes 1179652
  7.0 2.7 copy-start.9
  25.1 5.2 %copy-start = (bf16[2,256,1536]{2,1,0:T(8,128)(2,1)S(1)}, bf16[2,256,1536]{2,1,0:T(8,128)(2,1)}, u32[]{:S(2)}) copy-start(bf16[2,256,1536]{2,1,0:T(8,128)(2,1)} %get-tuple-element.46) | copy-start | bytes 4718596
  28.8 5.3 %copy-start.10 = (s32[2,4,2,128]{3,2,1,0:T(2,128)}, s32[2,4,2,128]{3,2,1,0:T(2,128)S(1)}, u32[]{:S(2)}) copy-start(s32[2,4,2,128]{3,2,1,0:T(2,128)S(1)} %get-tuple-element.105) | copy-start | bytes 24580
  211.9 4.3 %copy-start.11 = (bf16[2,2,4,96,1024]{4,3,2,1,0:T(8,128)(2,1)S(1)}, bf16[2,2,4,96,1024]{4,3,2,1,0:T(8,128)(2,1)}, u32[]{:S(2)}) copy-start(bf16[2,2,4,96,1024]{4,3,2,1,0:T(8,128)(2,1)} %get-tuple-element.50) | copy-start | bytes 9437188
  211.9 4.3 %copy-start.15 = (bf16[2,256,1536]{2,1,0:T(8,128)(2,1)S(1)}, bf16[2,256,1536]{2,1,0:T(8,128)(2,1)}, u32[]{:S(2)}) copy-start(bf16[2,256,1536]{2,1,0:T(8,128)(2,1)} %get-tuple-element.48) | copy-start | bytes 4718596
  216.3 1.9 copy-start.13
  216.3 2.3 copy-start.14
  221.2 3.0 copy-start.12
  413.5 4.5 %copy-start.1 = (f32[2,96,768]{2,1,0:T(8,128)S(1)}, f32[2,96,768]{2,1,0:T(8,128)}, u32[]{:S(2)}) copy-start(f32[2,96,768]{2,1,0:T(8,128)} %get-tuple-element.64) | copy-start | bytes 1769476
  413.5 6.8 %copy-start.6 = (f32[2,96,1024]{2,1,0:T(8,128)S(1)}, f32[2,96,1024]{2,1,0:T(8,128)}, u32[]{:S(2)}) copy-start(f32[2,96,1024]{2,1,0:T(8,128)} %get-tuple-element.66) | copy-start | bytes 2359300
  418.8 2.5 copy-start.5
  420.4 2.0 copy-start.4
  421.4 2.0 copy-start.3
  422.4 1.9 copy-start.2

commit v4 on v3

v4 whole, which is shorter than its diff:
```python
import functools

import jax
import jax.numpy as jnp
from jax import lax
from jax.experimental import pallas as pl
from jax.experimental.pallas import tpu as pltpu
from jax.sharding import Mesh, PartitionSpec as P

HQ = 16
HK = 8
DH = 96


EPS = 1e-05
THETA = 100000.0
NEGATIVE = -1e30


def contract(left, right, left_dim, right_dim):
    return lax.dot_general(
        left, right, (((left_dim,), (right_dim,)), ((), ())), preferred_element_type=jnp.float32
    )


MESH_ID = pl.DeviceIdType.MESH
BF16 = jnp.bfloat16
F32 = jnp.float32
GROUP = ("fy", "pr", "ctx")
VMEM_LIMIT = 62 * 1024 * 1024
LANES = 128


def remote(src, dst, send_sem, recv_sem, device):
    return pltpu.make_async_remote_copy(
        src_ref=src,
        dst_ref=dst,
        send_sem=send_sem,
        recv_sem=recv_sem,
        device_id=device,
        device_id_type=MESH_ID,
    )


def greet(devices_and_conditions, count):
    barrier = pltpu.get_barrier_semaphore()
    for device, condition in devices_and_conditions:
        if condition is None:
            pl.semaphore_signal(barrier, inc=1, device_id=device, device_id_type=MESH_ID)
        else:

            @pl.when(condition)
            def _(device=device):
                pl.semaphore_signal(barrier, inc=1, device_id=device, device_id_type=MESH_ID)

    pl.semaphore_wait(barrier, count)


def dot(left, right, left_dim=1, right_dim=0):
    return lax.dot_general(
        left, right, (((left_dim,), (right_dim,)), ((), ())), preferred_element_type=F32
    )


def low_bit(number):
    return (number & -number).bit_length() - 1


class Line:
    def __init__(self, nz):
        self.nz, self.levels = nz, nz.bit_length() - 1
        self.z = lax.axis_index("ctx")
        self.bits = [lax.rem(self.z // (1 << level), 2) for level in range(self.levels)]

    def at(self, offset):
        place = self.z
        for level in range(self.levels):
            if offset >> level & 1:
                place = place + (1 << level) - (2 << level) * self.bits[level]
        return place

    def partner(self, level):
        return self.at(1 << level)


class Gather:
    def __init__(self, line, outs, zs, zr, ys, yr):
        self.line, self.outs = line, outs
        self.zs, self.zr, self.ys, self.yr = zs, zr, ys, yr
        self.y = lax.axis_index("fy")
        offsets = range(1, line.nz)
        self.arrivals = sorted(offsets, key=lambda offset: (-low_bit(offset), offset))

    def hop(self, g, offset, level):
        piece = self.outs[g].at[self.y, :, self.line.at(offset)]
        slot = offset + (1 << level)
        return remote(
            piece, piece, self.zs.at[g, slot], self.zr.at[g, slot], {"ctx": self.line.partner(level)}
        )

    def hop_from(self, g, offset):
        piece = self.outs[g].at[self.y, :, self.line.at(offset)]
        partner = self.line.partner(low_bit(offset))
        return remote(piece, piece, self.zs.at[g, offset], self.zr.at[g, offset], {"ctx": partner})

    def across(self, g, offset, row):
        piece = self.outs[g].at[row, :, self.line.at(offset)]
        return remote(
            piece, piece, self.ys.at[g, offset], self.yr.at[g, offset], {"fy": 1 - self.y}
        )

    def hops(self, offset):
        last = low_bit(offset) if offset else self.line.levels
        return reversed(range(last))

    def own_z(self, g):
        for level in self.hops(0):
            self.hop(g, 0, level).start()

    def own_y(self, g):
        self.across(g, 0, self.y).start()

    def step(self, g, offset):
        self.hop_from(g, offset).wait_recv()
        for level in self.hops(offset):
            self.hop(g, offset, level).start()
        self.across(g, offset, self.y).start()

    def finish(self, g):
        for offset in (0, *self.arrivals):
            self.across(g, offset, 1 - self.y).wait_recv()

    def drain(self, g):
        for offset in (0, *self.arrivals):
            for level in self.hops(offset):
                self.hop(g, offset, level).wait_send()
            self.across(g, offset, self.y).wait_send()


class TokenSum:
    def __init__(self, part, bufs, sems, n):
        self.part, self.n = part, n
        self.core_send, self.core_land, self.x_send, self.x_land = bufs
        self.cs, self.cr, self.xs, self.xr = sems
        self.c = lax.axis_index("pr")
        self.x = lax.axis_index("tp")

    def core(self, i):
        return remote(
            self.core_send.at[i],
            self.core_land.at[self.n % 2, i],
            self.cs.at[self.n, i],
            self.cr.at[self.n, i],
            {"pr": 1 - self.c},
        )

    def sideways(self, i):
        return remote(
            self.x_send.at[i],
            self.x_land.at[self.n % 2, i],
            self.xs.at[self.n, i],
            self.xr.at[self.n, i],
            {"tp": 1 - self.x},
        )

    def start(self):
        def give(i, _):
            self.core_send[i] = self.part(1 - self.c, i).astype(BF16)
            self.core(i).start()
            return 0

        def add(i, _):
            mine = self.part(self.c, i).astype(F32)
            self.core(i).wait_recv()
            self.x_send[i] = (mine + self.core_land[self.n % 2, i].astype(F32)).astype(BF16)
            self.sideways(i).start()
            return 0

        lax.fori_loop(0, 4, give, 0)
        lax.fori_loop(0, 4, add, 0)

    def arrived(self, i):
        self.sideways(i).wait_recv()

    def total(self, i):
        return self.x_send[i].astype(F32) + self.x_land[self.n % 2, i].astype(F32)

    def drain(self):
        for i in range(4):
            self.core(i).wait_send()
            self.sideways(i).wait_send()


def weight_grad(into, left, right, stage, sems):
    _, span, width = left.shape
    chunk = width // 4

    def stored_part(i):
        slot = lax.rem(i, 2)
        return pltpu.make_async_copy(stage.at[slot], into.at[i // 2, slot], sems.at[slot])

    def one(i, _):
        here = pl.ds(pl.multiple_of(i * chunk, LANES), chunk)
        part = dot(left[0, :, here], right[:span], 0, 0) + dot(left[1, :, here], right[span:], 0, 0)

        @pl.when(i > 1)
        def _():
            stored_part(i - 2).wait()

        stage[lax.rem(i, 2)] = part.astype(BF16).reshape(stage.shape[1:])
        stored_part(i).start()
        return 0

    lax.fori_loop(0, 4, one, 0)
    for i in (2, 3):
        stored_part(i).wait()


def forward_kernel(nz, items, scale, *refs):
    weights = refs[:6]
    rows, upstream, small, info, freq, spread_mat = refs[6:12]
    stored = refs[12:26]
    down_grad = refs[26]
    cos, sin, q_seg, k_seg, gains = refs[27:32]
    made = refs[32:46]
    (
        w_qkv, w_out, q_out, kvu, mixed_out, mixed_low, lse_out, residual, normed, dx_part, out_part,
        normed_mlp, gate_grad, up_grad,
    ) = made
    (
        w_gate, w_up, w_down, acc, keys, values, top, core_send, core_land, x_send, x_land, smalls, info_both,
        rows_both, gate_pre, up_pre, upstream_both, hidden, stage,
    ) = refs[46:65]
    (
        loc, ps, pr, ws, wr, ts, tr, zs, zr, ys, yr, ks, kr, cs, cr, xs, xr, ns, nr, hs, gs,
    ) = refs[65:]

    def store(n):
        return pltpu.make_async_copy(made[n], stored[n], hs.at[n])

    outs = (w_qkv, w_out, w_gate, w_up, w_down)
    y = lax.axis_index("fy")
    c = lax.axis_index("pr")
    z = lax.axis_index("ctx")
    x = lax.axis_index("tp")
    span, width = rows.shape
    other_y, other_c, other_x = {"fy": 1 - y}, {"pr": 1 - c}, {"tp": 1 - x}
    line = Line(nz)
    gather = Gather(line, outs, zs, zr, ys, yr)
    chunk = width // 4
    half = w_out.shape[4]
    block = w_out.shape[3]
    late = (2, 3, 4)

    def columns(i):
        return pl.ds(pl.multiple_of(i * chunk, LANES), chunk)

    greet(
        [(other_y, None), (other_c, None), (other_x, None)]
        + [({"ctx": line.at(offset)}, None) for offset in range(1, nz)],
        2 + nz,
    )

    places = [(0, 0, half), (0, half, half), (1, 0, half)]
    places += [(g, 0, outs[g].shape[4]) for g in late]

    def half_of(n, which):
        size = places[n][2]
        return weights[n].at[:, pl.ds(pl.multiple_of(which * size, LANES), size)]

    def piece_of(n):
        g, first, size = places[n]
        return outs[g].at[y, c, z, :, pl.ds(first, size)]

    def other_piece(n):
        g, first, size = places[n]
        return outs[g].at[y, 1 - c, z, :, pl.ds(first, size)]

    moved = [(rows, rows_both), (upstream, upstream_both), (info, info_both)]
    local = [pltpu.make_async_copy(half_of(n, c), piece_of(n), loc.at[n]) for n in range(6)]
    local += [
        pltpu.make_async_copy(src, dst.at[c], loc.at[6 + n]) for n, (src, dst) in enumerate(moved)
    ]
    sent = [
        remote(half_of(n, 1 - c), piece_of(n), ps.at[n], pr.at[n], other_c) for n in range(6)
    ]
    sent += [
        remote(src, dst.at[c], ps.at[6 + n], pr.at[6 + n], other_c)
        for n, (src, dst) in enumerate(moved)
    ]
    landed = [
        remote(half_of(n, 1 - c), other_piece(n), ps.at[n], pr.at[n], other_c) for n in range(6)
    ]
    landed += [
        remote(src, dst.at[1 - c], ps.at[6 + n], pr.at[6 + n], other_c)
        for n, (src, dst) in enumerate(moved)
    ]

    def small_to(offset):
        return remote(
            small, smalls.at[y, c, z], ws.at[offset], wr.at[offset], {"ctx": line.at(offset)}
        )

    def small_from(offset):
        return remote(
            small, smalls.at[y, c, line.at(offset)], ws.at[offset], wr.at[offset],
            {"ctx": line.at(offset)},
        )

    small_here = pltpu.make_async_copy(small, smalls.at[y, c, z], loc.at[9])
    small_here.start()
    for n in range(3):
        local[n].start()
        sent[n].start()
    for offset in range(1, nz):
        small_to(offset).start()
    for n in (6, 8, 3, 4, 5, 7):
        local[n].start()
        sent[n].start()
    for n in range(2):
        local[n].wait()
        landed[n].wait_recv()
    gather.own_z(0)
    small_here.wait()
    for offset in range(1, nz):
        small_from(offset).wait_recv()
    small_line = remote(smalls.at[y, c], smalls.at[y, c], ts.at[0], tr.at[0], other_y)
    small_line.start()
    small_plane = remote(smalls.at[:, c], smalls.at[:, c], ts.at[1], tr.at[1], other_c)
    gather.own_y(0)
    for n in (5, 4, 2, 3):
        local[n].wait()
        landed[n].wait_recv()

    def prepare():
        remote(smalls.at[1 - y, c], smalls.at[1 - y, c], ts.at[0], tr.at[0], other_y).wait_recv()
        small_plane.start()
        for n in (6, 7, 8):
            local[n].wait()
            landed[n].wait_recv()
        factors = []
        for b in range(2):
            value = rows_both[b].astype(F32)
            factors.append(lax.rsqrt(jnp.sum(value * value, axis=1, keepdims=True) / width + EPS))
            angles = info_both[b, :, 0:1] * freq[...]
            lane = lax.broadcasted_iota(jnp.int32, (span, LANES), 1)
            used = lax.rem(lane, LANES // 2) < DH // 2
            here = pl.ds(b * span, span)
            cos[here] = jnp.where(used, jnp.cos(angles), 0.0)
            turn = jnp.where(used, jnp.sin(angles), 0.0)
            sin[here] = jnp.where(lane < LANES // 2, -turn, turn)
            for j in range(2):
                q_seg[b, pl.ds(j * span, span)] = info_both[b, :, 1:2]
        remote(smalls.at[:, 1 - c], smalls.at[:, 1 - c], ts.at[1], tr.at[1], other_c).wait_recv()
        per = span // LANES
        for b in range(2):
            for j in range(nz):
                for part in range(per):
                    k_seg[b, j, :, pl.ds(part * LANES, LANES)] = smalls[
                        y, b, j, pl.ds(2 + part, 1)
                    ]
        for which in range(2):
            gain_row = jnp.zeros((1, width), F32)
            blank = jnp.zeros((1, width - LANES), F32)
            for n in range(4 * nz):
                own = smalls[n // (2 * nz), n // nz % 2, n % nz, pl.ds(which, 1)]
                wide = jnp.concatenate([own, blank], axis=1)
                gain_row = gain_row + (pltpu.roll(wide, n * block, 1) if n else wide)
            gains[which] = gain_row
        for b in range(2):
            normed[b] = (rows_both[b].astype(F32) * factors[b] * gains[0]).astype(BF16)
        store(8).start()

    def head_fields():
        acc[...] = jnp.zeros_like(acc)

        def one(i, _):
            part = w_qkv[i // 2, lax.rem(i, 2)].reshape(chunk, 2 * half)
            wide = jnp.concatenate(
                [
                    dot(part[:, :half], spread_mat[...]).astype(BF16),
                    dot(part[:, half:], spread_mat[...]).astype(BF16),
                ],
                axis=1,
            )
            for b in range(2):
                acc[pl.ds(b * span, span)] += dot(normed[b, :, columns(i)], wide)
            return 0

        lax.fori_loop(0, 4, one, 0)

    def rotated(b, lane):
        here = pl.ds(b * span, span)
        field = acc[here, pl.ds(lane * LANES, LANES)]
        turned = pltpu.roll(field, LANES // 2, 1)
        return (field * cos[here] + turned * sin[here]).astype(BF16)

    def keys_hop(b, offset, level):
        piece = kvu.at[line.at(offset), b]
        slot = offset + (1 << level)
        return remote(
            piece, piece, ks.at[b, slot], kr.at[b, slot], {"ctx": line.partner(level)}
        )

    def keys_from(b, offset):
        piece = kvu.at[line.at(offset), b]
        partner = line.partner(low_bit(offset))
        return remote(piece, piece, ks.at[b, offset], kr.at[b, offset], {"ctx": partner})

    def each_hop(offset, act):
        for level in gather.hops(offset):

            @pl.when(line.at(offset) <= line.partner(level))
            def _(level=level):
                act(level)

    def project_heads():
        head_fields()
        for b in range(2):
            fields = []
            for k in range(2):
                keys[b * 2 + k] = rotated(b, 4 + k)
                fields.append(keys[b * 2 + k])
            for k in range(2):
                values[b * 2 + k] = acc[
                    pl.ds(b * span, span), pl.ds((6 + k) * LANES, LANES)
                ].astype(BF16)
                fields.append(values[b * 2 + k])
            kvu[z, b] = dot(jnp.concatenate(fields, axis=1), spread_mat[...], 1, 1).astype(BF16)
            each_hop(0, lambda level, b=b: keys_hop(b, 0, level).start())

        for b in range(2):
            for k in range(2):
                for j in range(2):
                    q_out[b * 2 + k, pl.ds(j * span, span)] = rotated(b, 2 * k + j)

    def attend(there, first):
        def one(n, _):
            i = n // 2
            b = i // 2
            here = pl.ds(pl.multiple_of(lax.rem(n, 2) * span, span), span)
            scores = dot(q_out[i, here], keys[i], 1, 1) * scale
            allowed = q_seg[b, :span] == k_seg[b, there]
            if first:
                row = lax.broadcasted_iota(jnp.int32, scores.shape, 0)
                column = lax.broadcasted_iota(jnp.int32, scores.shape, 1)
                allowed = allowed & (row >= column)
            scores = jnp.where(allowed, scores, NEGATIVE)
            peak = jnp.max(scores, axis=1, keepdims=True)
            if first:
                probs = jnp.exp(scores - peak)
                total = jnp.sum(probs, axis=1, keepdims=True)
                mixed_out[i, here] = dot(probs.astype(BF16), values[i])
            else:
                old = top[i, here][:, :1]
                peak = jnp.maximum(old, peak)
                keep = jnp.exp(old - peak)
                probs = jnp.exp(scores - peak)
                total = keep * lse_out[i, here][:, :1] + jnp.sum(probs, axis=1, keepdims=True)
                mixed_out[i, here] = keep * mixed_out[i, here] + dot(
                    probs.astype(BF16), values[i]
                )
            top[i, here] = jnp.broadcast_to(peak, (span, LANES))
            lse_out[i, here] = jnp.broadcast_to(total, (span, LANES))
            return 0

        lax.fori_loop(0, 2 * items, one, 0)

    def attend_own():
        attend(z, True)

    def keys_in(offset):
        @pl.when(line.at(offset) <= z)
        def _():
            for b in range(2):
                keys_from(b, offset).wait_recv()
                each_hop(offset, lambda level, b=b: keys_hop(b, offset, level).start())

    def attend_at(offset):
        there = line.at(offset)

        @pl.when(there <= z)
        def _():
            for b in range(2):
                wide = dot(kvu[there, b], spread_mat[...]).astype(BF16)
                for k in range(2):
                    keys[b * 2 + k] = wide[:, k * LANES : (k + 1) * LANES]
                    values[b * 2 + k] = wide[:, (2 + k) * LANES : (3 + k) * LANES]
            attend(there, False)

    def close():
        def divide(i, _):
            total = lse_out[i]
            mixed_out[i] = mixed_out[i] / total
            lse_out[i] = top[i] + jnp.log(total)
            return 0

        lax.fori_loop(0, items, divide, 0)
        for b in range(2):
            heads = [
                mixed_out[b * 2 + k, pl.ds(j * span, span)].astype(BF16)
                for k in range(2)
                for j in range(2)
            ]
            mixed_low[pl.ds(b * span, span)] = dot(
                jnp.concatenate(heads, axis=1), spread_mat[...], 1, 1
            ).astype(BF16)
        for n in (2, 3, 4, 5, 6):
            store(n).start()

    def projected(who, i):
        part = w_out[i // 2, lax.rem(i, 2)].reshape(chunk, half)
        return dot(mixed_low[pl.ds(pl.multiple_of(who * span, span), span)], part, 1, 1)

    token_sum = TokenSum(
        projected, (core_send, core_land, x_send, x_land), (cs, cr, xs, xr), 0
    )
    swap = remote(normed_mlp.at[c], normed_mlp.at[c], ns.at[0], nr.at[0], other_c)

    def add_residual():
        def one(i, _):
            token_sum.arrived(i)
            residual[:, columns(i)] = rows[:, columns(i)].astype(F32) + token_sum.total(i)
            return 0

        lax.fori_loop(0, 4, one, 0)
        store(7).start()

    def norm():
        def one(i, squares):
            total = residual[:, columns(i)]
            return squares + jnp.sum(total * total, axis=1, keepdims=True)

        squares = lax.fori_loop(0, 4, one, jnp.zeros((span, 1), F32))
        factor = lax.rsqrt(squares / width + EPS)

        def two(i, _):
            here = columns(i)
            normed_mlp[c, :, here] = (residual[:, here] * factor * gains[1, :, here]).astype(BF16)
            return 0

        lax.fori_loop(0, 4, two, 0)
        swap.start()

    def swapped():
        remote(normed_mlp.at[1 - c], normed_mlp.at[1 - c], ns.at[0], nr.at[0], other_c).wait_recv()

    size = 256
    blocks = w_gate.shape[4] // size

    def column_block(ref, n):
        part = ref[:, :, :, :, pl.ds(pl.multiple_of(n * size, size), size)]
        return part.reshape(width, size)

    def project(into, ref):
        def one(n, _):
            cols = pl.ds(pl.multiple_of(n * size, size), size)
            part = column_block(ref, n)
            for b in range(2):
                into[pl.ds(b * span, span), cols] = dot(normed_mlp[b], part)
            return 0

        lax.fori_loop(0, blocks, one, 0)

    def hidden_block(n, _):
        cols = pl.ds(pl.multiple_of(n * size, size), size)
        for b in range(2):
            here = pl.ds(b * span, span)
            gate = gate_pre[here, cols]
            hidden[here, cols] = (gate * jax.nn.sigmoid(gate) * up_pre[here, cols]).astype(BF16)
        return 0

    def grads_block(n, _):
        cols = pl.ds(pl.multiple_of(n * size, size), size)
        part = column_block(w_down, n)
        for b in range(2):
            here = pl.ds(b * span, span)
            back = dot(upstream_both[b], part)
            gate, up = gate_pre[here, cols], up_pre[here, cols]
            open_part = jax.nn.sigmoid(gate)
            gate_grad[here, cols] = (
                back * up * open_part * (1.0 + gate * (1.0 - open_part))
            ).astype(BF16)
            up_grad[here, cols] = (back * (gate * open_part)).astype(BF16)
        return 0

    def back_block(i, _):
        cols = pl.ds(pl.multiple_of(i * chunk, LANES), chunk)
        gate_part = w_gate[i // 2, lax.rem(i, 2)].reshape(chunk, blocks * size)
        up_part = w_up[i // 2, lax.rem(i, 2)].reshape(chunk, blocks * size)
        down_part = w_down[i // 2, lax.rem(i, 2)].reshape(chunk, blocks * size)
        for b in range(2):
            here = pl.ds(b * span, span)
            dx_part[b, :, cols] = (
                dot(gate_grad[here], gate_part, 1, 1) + dot(up_grad[here], up_part, 1, 1)
            ).astype(BF16)
            out_part[b, :, cols] = dot(hidden[here], down_part, 1, 1).astype(BF16)
        return 0

    own_z, own_y, step = gather.own_z, gather.own_y, gather.step

    def finish(g):
        gather.finish(g)
        if g < 2:
            store(g).start()

    start_sum = token_sum.start

    def gate():
        project(gate_pre, w_gate)

    def up():
        project(up_pre, w_up)

    def hide():
        lax.fori_loop(0, blocks, hidden_block, 0)
        weight_grad(down_grad, upstream_both, hidden, stage, gs)

    def grads():
        lax.fori_loop(0, blocks, grads_block, 0)
        for n in (11, 12, 13):
            store(n).start()

    def back_rows():
        lax.fori_loop(0, 4, back_block, 0)
        store(9).start()
        store(10).start()

    arrivals = gather.arrivals
    if nz == 4:
        plan = [
            (own_y, 4), (own_y, 3), (step, 0, 2), (own_y, 1), (own_z, 1), (prepare,), (own_z, 2),
            (step, 0, 1), (step, 0, 3), (step, 1, 2), (step, 1, 1), (own_z, 3), (step, 2, 2),
            (step, 2, 1), (finish, 0), (project_heads,), (step, 3, 1), (step, 1, 3),
            (step, 2, 3), (attend_own,), (keys_in, 2), (own_y, 2), (finish, 1), (own_z, 4),
            (attend_at, 2), (keys_in, 1), (step, 3, 2), (attend_at, 1), (keys_in, 3),
            (attend_at, 3), (close,), (step, 4, 2), (start_sum,), (step, 4, 1), (step, 3, 3),
            (add_residual,), (finish, 2), (norm,), (step, 4, 3), (finish, 3), (swapped,),
            (gate,), (up,), (hide,), (finish, 4), (grads,), (back_rows,),
        ]
    else:
        plan = [(own_z, 1), (own_y, 1), (prepare,)]
        plan += [(step, g, offset) for offset in arrivals for g in (0, 1)]
        plan += [(run, g) for g in late for run in (own_z, own_y)]
        plan += [(finish, 0), (project_heads,), (attend_own,)]
        plan += [(run, offset) for offset in arrivals for run in (keys_in, attend_at)]
        plan += [(close,), (finish, 1), (start_sum,)]
        plan += [(step, g, offset) for offset in arrivals for g in late]
        plan += [(add_residual,), (norm,), (swapped,), (finish, 2), (gate,), (finish, 3), (up,)]
        plan += [(hide,), (finish, 4), (grads,), (back_rows,)]
    for run, *which in plan:
        run(*which)

    for g in range(5):
        gather.drain(g)
    for b in range(2):
        each_hop(0, lambda level, b=b: keys_hop(b, 0, level).wait_send())
        for offset in gather.arrivals:

            @pl.when(line.at(offset) <= z)
            def _(b=b, offset=offset):
                each_hop(offset, lambda level: keys_hop(b, offset, level).wait_send())

    for n in range(14):
        store(n).wait()
    token_sum.drain()
    swap.wait_send()
    for copy in sent:
        copy.wait_send()
    small_line.wait_send()
    small_plane.wait_send()
    for offset in range(1, nz):
        small_to(offset).wait_send()


def forward(weights, rows, upstream, small, info, freq, spread_mat, ny, nz):
    dma = pltpu.SemaphoreType.DMA
    vmem = pl.BlockSpec(memory_space=pltpu.VMEM)
    span, width = rows.shape
    block, half, wide = weights[0].shape[0], weights[0].shape[1] // 2, weights[3].shape[1] // 2
    items, q_rows, both = 4, 2 * span, 2 * span
    shape = jax.ShapeDtypeStruct
    chunk = width // 4
    anywhere = pl.BlockSpec(memory_space=pl.ANY)
    weight = (ny, 2, nz, block)
    made = [
        (weight + (2 * half,), BF16),
        (weight + (half,), BF16),
        ((items, q_rows, LANES), BF16),
        ((nz, 2, span, half), BF16),
        ((items, q_rows, LANES), F32),
        ((both, half), BF16),
        ((items, q_rows, LANES), F32),
        ((span, width), F32),
        ((2, span, width), BF16),
        ((2, span, width), BF16),
        ((2, span, width), BF16),
        ((2, span, width), BF16),
        ((both, wide), BF16),
        ((both, wide), BF16),
    ]
    out_shape = [shape(*each) for each in made] + [shape(weight + (wide,), BF16)]
    out_shape += [
        shape((both, LANES), F32),
        shape((both, LANES), F32),
        shape((2, q_rows, 1), F32),
        shape((2, nz, 1, span), F32),
        shape((2, 1, width), F32),
    ]
    return pl.pallas_call(
        functools.partial(forward_kernel, nz, items, DH ** (-0.5)),
        out_shape=out_shape,
        in_specs=[vmem] * 12,
        out_specs=[anywhere] * 15 + [vmem] * 5,
        scratch_shapes=[pltpu.VMEM(*each) for each in made]
        + [pltpu.VMEM(weight + (wide,), BF16)] * 3
        + [
            pltpu.VMEM((both, 8 * LANES), F32),
            pltpu.VMEM((items, span, LANES), BF16),
            pltpu.VMEM((items, span, LANES), BF16),
            pltpu.VMEM((items, q_rows, LANES), F32),
            pltpu.VMEM((4, span, chunk), BF16),
            pltpu.VMEM((1, 4, span, chunk), BF16),
            pltpu.VMEM((4, span, chunk), BF16),
            pltpu.VMEM((1, 4, span, chunk), BF16),
            pltpu.VMEM((ny, 2, nz) + small.shape, F32),
            pltpu.VMEM((2, span, LANES), F32),
            pltpu.VMEM((2, span, width), BF16),
            pltpu.VMEM((both, wide), F32),
            pltpu.VMEM((both, wide), F32),
            pltpu.VMEM((2, span, width), BF16),
            pltpu.VMEM((both, wide), BF16),
            pltpu.VMEM((2, nz, block, wide), BF16),
        ]
        + [dma((10,)), dma((9,)), dma((9,)), dma((nz,)), dma((nz,)), dma((2,)), dma((2,))]
        + [dma((5, nz))] * 4
        + [dma((2, nz))] * 2
        + [dma((1, 4))] * 4
        + [dma((1,))] * 2
        + [dma((14,)), dma((2,))],
        name="forward",
        compiler_params=pltpu.CompilerParams(
            collective_id=1, has_side_effects=True, vmem_limit_bytes=VMEM_LIMIT
        ),
    )(*weights, rows, upstream, small, info, freq, spread_mat)


RELAYED = (0,)
LATER = (19, 21, 20, 17, 14, 13, 11, 15, 1, 18, 16, 3)


class Scatter:
    def __init__(self, line, sources, owns, lands, ins, mids, extras, totals, outs, sems):
        self.line, self.sources, self.owns, self.lands = line, sources, owns, lands
        self.ins, self.mids, self.extras = ins, mids, extras
        self.totals, self.outs, self.sems = totals, outs, sems
        self.y = lax.axis_index("fy")
        self.c = lax.axis_index("pr")
        nz = line.nz
        self.order = sorted(range(1, nz), key=lambda offset: (low_bit(offset), -offset)) + [0]

    def own_copy(self, g, place):
        return pltpu.make_async_copy(
            self.sources[g].at[self.y, :, self.line.at(self.order[place])],
            self.owns[g].at[place % 2],
            self.sems[0].at[g, 3 + place % 2],
        )

    def own(self, g, place, k, rows):
        if self.owns[g] is None:
            place_at = self.line.at(self.order[place])
            return self.sources[g][self.y, k, place_at, rows].astype(F32)
        return self.owns[g][place % 2, k, rows].astype(F32)

    def fetch(self, g, place):
        if self.owns[g] is not None and place < self.line.nz:
            self.own_copy(g, place).start()

    def fetched(self, g, place):
        if self.owns[g] is not None:
            self.own_copy(g, place).wait()

    def middle(self, g):
        return pltpu.make_async_copy(
            self.sources[g].at[1 - self.y, 1, self.line.z], self.mids[g], self.sems[0].at[g, 1]
        )

    def across(self, g, offset):
        ys, yr = self.sems[1], self.sems[2]
        src, dst, place = self.sources[g], self.lands[g], self.line.at(offset)
        if offset > 1 or g not in RELAYED:
            src, dst = src.at[1 - self.y, :, place], dst.at[offset]
        else:
            src, dst = src.at[1 - self.y, 0, place], dst.at[offset, 0]
        return remote(src, dst, ys.at[g, offset], yr.at[g, offset], {"fy": 1 - self.y})

    def relayed(self, g):
        ys, yr = self.sems[1], self.sems[2]
        slot = self.line.nz
        return remote(
            self.mids[g], self.lands[g].at[0, 1], ys.at[g, slot], yr.at[g, slot], {"fy": 1 - self.y}
        )

    def extra(self, g):
        es, er = self.sems[3], self.sems[4]
        src = self.sources[g].at[1 - self.y, 1, self.line.at(1)]
        return remote(src, self.extras[g], es.at[g], er.at[g], {"ctx": self.line.partner(0)})

    def hop(self, g, offset):
        zs, zr = self.sems[5], self.sems[6]
        return remote(
            self.lands[g].at[offset],
            self.ins[g].at[offset - 1],
            zs.at[g, offset],
            zr.at[g, offset],
            {"ctx": self.line.partner(low_bit(offset))},
        )

    def swap(self, g, slot):
        cs, cr = self.sems[7], self.sems[8]
        return remote(
            self.totals[g].at[1 - self.c], self.outs[g].at[slot], cs.at[g], cr.at[g], {"pr": 1 - self.c}
        )

    def keep(self, g):
        return pltpu.make_async_copy(
            self.totals[g].at[self.c], self.outs[g].at[self.c], self.sems[0].at[g, 2]
        )

    def each_tile(self, g, body):
        block = self.lands[g].shape[2]
        rows = 32 if block % 32 == 0 else block
        per = block // rows

        def step(i, _):
            body(i // per, pl.ds(pl.multiple_of(lax.rem(i, per) * rows, 8), rows))
            return 0

        lax.fori_loop(0, 2 * per, step, 0)

    def start(self, g):
        self.fetch(g, 0)
        self.fetch(g, 1)
        if g in RELAYED:
            self.middle(g).start()
            self.extra(g).start()
            self.lands[g][1, 1] = jnp.zeros(self.lands[g].shape[2:], BF16)
        for offset in self.order:
            self.across(g, offset).start()

    def relay(self, g):
        self.middle(g).wait()
        self.extra(g).wait_recv()
        self.mids[g][...] = (
            self.mids[g][...].astype(F32) + self.extras[g][...].astype(F32)
        ).astype(BF16)
        self.relayed(g).start()

    def step(self, g, place):
        offset = self.order[place]
        land, into = self.lands[g], self.ins[g]
        self.fetched(g, place)
        self.across(g, offset).wait_recv()
        arrived = [offset ^ (1 << level) for level in range(low_bit(offset))]
        for other in arrived:
            self.hop(g, other).wait_recv()

        def add(k, rows):
            total = self.own(g, place, k, rows) + land[offset, k, rows].astype(F32)
            for other in arrived:
                total = total + into[other - 1, k, rows].astype(F32)
            land[offset, k, rows] = total.astype(BF16)

        self.each_tile(g, add)
        self.hop(g, offset).start()
        self.fetch(g, place + 2)

    def last(self, g):
        place = self.line.nz - 1
        land, into = self.lands[g], self.ins[g]
        total = self.totals[g]
        self.fetched(g, place)
        self.across(g, 0).wait_recv()
        if g in RELAYED:
            self.relayed(g).wait_recv()
        arrived = [1 << level for level in range(self.line.levels)]
        for other in arrived:
            self.hop(g, other).wait_recv()

        def add(k, rows):
            value = self.own(g, place, k, rows) + land[0, k, rows].astype(F32)
            for other in arrived:
                value = value + into[other - 1, k, rows].astype(F32)
            total[k, rows] = value

        self.each_tile(g, add)
        self.swap(g, self.c).start()
        self.keep(g).start()

    def finish(self, g):
        self.swap(g, 1 - self.c).wait_recv()
        self.swap(g, self.c).wait_send()
        self.keep(g).wait()
        if g in RELAYED:
            self.extra(g).wait_send()
            self.relayed(g).wait_send()
        for offset in self.order:
            self.across(g, offset).wait_send()
            if offset:
                self.hop(g, offset).wait_send()


def backward_kernel(nz, scale, *refs):
    operands = list(refs[1:23])
    layer_out, input_grad = refs[23:25]
    outs = refs[25:30]
    gains = refs[30]
    sources = (refs[0], refs[31], refs[32])
    fetched, scratch = refs[33 : 33 + len(LATER)], refs[33 + len(LATER) : -3]
    stage, stage_sems = refs[-3], refs[-2]
    fetch = {}
    for n, which in enumerate(LATER):
        fetch[which] = pltpu.make_async_copy(operands[which], fetched[n], refs[-1].at[n])
        operands[which] = fetched[n]
    (
        dx_part, out_part, residual, rows, upstream, full_gains, cos, sin, q_seg, k_seg,
        spread_mat, q_items, kv_all, mixed_wide, mixed_low, lse, w_qkv, w_out, normed,
        normed_mlp, gate_grad, up_grad,
    ) = operands
    kept = 3
    owns = (*scratch[:kept], None, None)
    lands, ins, totals = (scratch[kept + 5 * i : kept + 5 * i + 5] for i in range(3))
    mids, extras = ({g: ref} for g, ref in zip(RELAYED * 2, scratch[kept + 15 : kept + 17]))
    (
        o_part, qkv_part, core_send, core_land, x_send, x_land, back_rows, low_rows, grad_items,
        delta, dq, kv_send, kv_land, qkv_rows, gain_rows, kv_here,
    ) = scratch[kept + 17 : kept + 33]
    (
        loc, ys, yr, es, er, zs, zr, ss, sr, cs, cr, xs, xr, ns, nr, ks, kr, gs, gr, ts, tr, bs,
    ) = scratch[kept + 33 :]
    y = lax.axis_index("fy")
    c = lax.axis_index("pr")
    z = lax.axis_index("ctx")
    span, width = rows.shape
    chunk = width // 4
    half = 4 * DH
    sources = (*sources, o_part, qkv_part)
    line = Line(nz)
    scatter = Scatter(
        line, sources, owns, lands, ins, mids, extras, totals, outs,
        (loc, ys, yr, es, er, zs, zr, ss, sr),
    )
    greet(
        [
            ({"fy": 1 - y}, None),
            ({"pr": 1 - c}, None),
            ({"tp": 1 - lax.axis_index("tp")}, None),
        ]
        + [({"ctx": t}, z != t) for t in range(nz)],
        2 + nz,
    )
    for which in LATER:
        fetch[which].start()
    bufs = (core_send, core_land, x_send, x_land)
    sems = (cs, cr, xs, xr)
    def columns(i):
        return pl.ds(pl.multiple_of(i * chunk, LANES), chunk)

    def back_in(who, i):
        weights = w_qkv[i // 2, lax.rem(i, 2)].reshape(chunk, 2 * half)
        return dot(qkv_rows[who], weights, 1, 1)

    first = TokenSum(lambda who, i: dx_part[who, :, columns(i)], bufs, sems, 0)
    second = TokenSum(lambda who, i: out_part[who, :, columns(i)], bufs, sems, 1)
    third = TokenSum(back_in, bufs, sems, 2)
    swap = remote(low_rows.at[c], low_rows.at[c], ns.at[0], nr.at[0], {"pr": 1 - c})

    def residual_back():
        def one(i, sums):
            here = columns(i)
            first.arrived(i)
            grad = first.total(i)
            back_rows[:, here] = grad
            value = residual[:, here]
            return (
                sums[0] + jnp.sum(value * value, axis=1, keepdims=True),
                sums[1] + jnp.sum(grad * full_gains[1, :, here] * value, axis=1, keepdims=True),
            )

        zero = jnp.zeros((span, 1), F32)
        squares, inner_sum = lax.fori_loop(0, 4, one, (zero, zero))
        factor = lax.rsqrt(squares / width + EPS)
        slope = factor * factor * factor * (inner_sum / width)

        def two(i, _):
            here = columns(i)
            grad = back_rows[:, here]
            value = residual[:, here]
            gain_rows[1:2, here] = jnp.sum(grad * value * factor, axis=0, keepdims=True)
            back = (
                upstream[:, here].astype(F32)
                + factor * (grad * full_gains[1, :, here])
                - value * slope
            )
            back_rows[:, here] = back
            low_rows[c, :, here] = back.astype(BF16)
            return 0

        lax.fori_loop(0, 4, two, 0)
        first.drain()
        swap.start()

    def low_rows_in():
        remote(low_rows.at[1 - c], low_rows.at[1 - c], ns.at[0], nr.at[0], {"pr": 1 - c}).wait_recv()

    def heads_back():
        fetch[17].wait()
        fetch[14].wait()
        for b in range(2):

            def add(i, total, b=b):
                weights = w_out[i // 2, lax.rem(i, 2)].reshape(chunk, half)
                return total + dot(low_rows[b, :, columns(i)], weights)

            grads = lax.fori_loop(0, 4, add, jnp.zeros((span, half), F32))
            wide = dot(grads.astype(BF16), spread_mat[...]).astype(BF16)
            for k in range(2):
                for j in range(2):
                    head = 2 * k + j
                    grad_items[b * 2 + k, pl.ds(j * span, span)] = wide[
                        :, head * LANES : (head + 1) * LANES
                    ]

        def one(i, _):
            part = dot(low_rows[0, :, columns(i)], mixed_low[:span], 0, 0) + dot(
                low_rows[1, :, columns(i)], mixed_low[span:], 0, 0
            )
            o_part[i // 2, lax.rem(i, 2)] = part.astype(BF16).reshape(o_part.shape[2:])
            return 0

        lax.fori_loop(0, 4, one, 0)

    def deltas():
        fetch[13].wait()
        for i in range(4):
            delta[i] = jnp.broadcast_to(
                jnp.sum(grad_items[i].astype(F32) * mixed_wide[i], axis=1, keepdims=True),
                delta.shape[1:],
            )
        dq[...] = jnp.zeros_like(dq)
        load_start(0)

    slots = kv_send.shape[0]
    order = scatter.order

    def keys_hop(b, place):
        offset = order[place]
        return remote(
            kv_send.at[place % slots, b],
            kv_land.at[offset, b],
            ks.at[b, offset],
            kr.at[b, offset],
            {"ctx": line.partner(low_bit(offset))},
        )

    def keys_add(b, place, offset):
        remote(
            kv_send.at[place % slots, b],
            kv_land.at[offset, b],
            ks.at[b, offset],
            kr.at[b, offset],
            {"ctx": line.partner(low_bit(offset))},
        ).wait_recv()
        kv_send[place % slots, b] = (
            kv_send[place % slots, b].astype(F32) + kv_land[offset, b].astype(F32)
        ).astype(BF16)

    def load(place):
        block = line.at(order[place])
        return pltpu.make_async_copy(kv_all.at[block], kv_here.at[place % 2], bs.at[place % 2])

    def load_start(place):
        @pl.when(line.at(order[place]) <= z)
        def _():
            load(place).start()

    def back_block(place, diagonal):
        block, slot = line.at(order[place]), place % 2
        load(place).wait()

        def one(b, _):
            key_grads, value_grads = [], []
            wide_kv = dot(kv_here[slot, b], spread_mat[...]).astype(BF16)
            for k in range(2):
                item = b * 2 + k
                keys = wide_kv[:, k * LANES : (k + 1) * LANES]
                values = wide_kv[:, (2 + k) * LANES : (3 + k) * LANES]
                scores = dot(q_items[item], keys, 1, 1) * scale
                allowed = q_seg[b] == k_seg[b, block]
                if diagonal:
                    row = lax.broadcasted_iota(jnp.int32, scores.shape, 0)
                    column = lax.broadcasted_iota(jnp.int32, scores.shape, 1)
                    allowed = allowed & (lax.rem(row, span) >= column)
                probs = jnp.where(allowed, jnp.exp(scores - lse[item][:, :1]), 0.0)
                prob_grad = dot(grad_items[item], values, 1, 1)
                score_grad = (probs * (prob_grad - delta[item][:, :1])).astype(BF16)
                value_grads.append(dot(probs.astype(BF16), grad_items[item], 0, 0))
                key_grads.append(dot(score_grad, q_items[item], 0, 0) * scale)
                dq[item] += dot(score_grad, keys) * scale
            wide = jnp.concatenate(key_grads + value_grads, axis=1).astype(BF16)
            kv_send[place % slots, b] = dot(wide, spread_mat[...], 1, 1).astype(BF16)
            return 0

        lax.fori_loop(0, 2, one, 0)

    def keys_pass(place):
        offset = order[place]

        @pl.when(line.at(offset) <= z)
        def _():
            for b in range(2):
                for level in range(low_bit(offset)):
                    keys_add(b, place, offset ^ (1 << level))
                keys_hop(b, place).start()

    def keys_sent(place):
        @pl.when(line.at(order[place]) <= z)
        def _():
            for b in range(2):
                keys_hop(b, place).wait_send()

    final = nz - 1

    def attend_back(place):
        if place == 0:
            fetch[11].wait()
            fetch[15].wait()
        if place < final:
            load_start(place + 1)
        if place >= slots:
            keys_sent(place - slots)
        if place == final:
            back_block(final, True)
            return

        @pl.when(line.at(order[place]) <= z)
        def _():
            back_block(place, False)

        if low_bit(order[place]) == 0 or slots < nz:
            keys_pass(place)

    def keys_final():
        for level in range(line.levels):

            @pl.when(line.bits[level] == 0)
            def _(level=level):
                for b in range(2):
                    keys_add(b, final, 1 << level)

    def layer_rows():
        def one(i, _):
            second.arrived(i)
            layer_out[:, columns(i)] = (residual[:, columns(i)] + second.total(i)).astype(BF16)
            return 0

        lax.fori_loop(0, 4, one, 0)
        second.drain()

    def unrotated(field, b):
        turned = pltpu.roll(field, LANES // 2, 1)
        here = pl.ds(b * span, span)
        return (field * cos[here] - turned * sin[here]).astype(BF16)

    def qkv_back():
        fetch[18].wait()
        for b in range(2):
            heads = [
                unrotated(dq[b * 2 + k, pl.ds(j * span, span)], b) for k in range(2) for j in range(2)
            ]
            qkv_rows[b, :, :half] = dot(
                jnp.concatenate(heads, axis=1), spread_mat[...], 1, 1
            ).astype(BF16)
        for b in range(2):
            wide = dot(kv_send[final % slots, b], spread_mat[...])
            fields = [unrotated(wide[:, k * LANES : (k + 1) * LANES], b) for k in range(2)]
            fields += [wide[:, (2 + k) * LANES : (3 + k) * LANES].astype(BF16) for k in range(2)]
            qkv_rows[b, :, half:] = dot(
                jnp.concatenate(fields, axis=1), spread_mat[...], 1, 1
            ).astype(BF16)

        def one(i, _):
            part = dot(normed[0, :, columns(i)], qkv_rows[0], 0, 0) + dot(
                normed[1, :, columns(i)], qkv_rows[1], 0, 0
            )
            qkv_part[i // 2, lax.rem(i, 2)] = part.astype(BF16).reshape(qkv_part.shape[2:])
            return 0

        lax.fori_loop(0, 4, one, 0)

    mine = pltpu.make_async_copy(gain_rows, gains.at[y, c, z], ts.at[2])
    core_gain = remote(gains.at[y, c, z], gains.at[y, c, z], ts.at[1], tr.at[1], {"pr": 1 - c})
    gain_line = remote(gains.at[y], gains.at[y], ts.at[0], tr.at[0], {"fy": 1 - y})

    def gain_to(t):
        return remote(gains.at[y, :, z], gains.at[y, :, z], gs.at[t], gr.at[z], {"ctx": t})

    def gain_from(t):
        return remote(gains.at[y, :, t], gains.at[y, :, t], gs.at[t], gr.at[t], {"ctx": t})

    def input_back():
        fetch[3].wait()
        def one(i, sums):
            here = columns(i)
            third.arrived(i)
            value = rows[:, here].astype(F32)
            weighed = third.total(i) * full_gains[0, :, here] * value
            return (
                sums[0] + jnp.sum(value * value, axis=1, keepdims=True),
                sums[1] + jnp.sum(weighed, axis=1, keepdims=True),
            )

        zero = jnp.zeros((span, 1), F32)
        squares, inner_sum = lax.fori_loop(0, 4, one, (zero, zero))
        factor = lax.rsqrt(squares / width + EPS)
        slope = factor * factor * factor * (inner_sum / width)

        def two(i, _):
            here = columns(i)
            value = rows[:, here].astype(F32)
            grad = third.total(i)
            gain_rows[0:1, here] = jnp.sum(grad * value * factor, axis=0, keepdims=True)
            input_grad[:, here] = (
                back_rows[:, here] + factor * (grad * full_gains[0, :, here]) - value * slope
            ).astype(BF16)
            return 0

        lax.fori_loop(0, 4, two, 0)
        third.drain()
        mine.start()
        mine.wait()
        core_gain.start()
        remote(
            gains.at[y, 1 - c, z], gains.at[y, 1 - c, z], ts.at[1], tr.at[1], {"pr": 1 - c}
        ).wait_recv()
        for t in range(nz):

            @pl.when(z != t)
            def _(t=t):
                gain_to(t).start()

    def gains_in():
        for t in range(nz):

            @pl.when(z != t)
            def _(t=t):
                gain_from(t).wait_recv()

        gain_line.start()

    start, relay, step, last = scatter.start, scatter.relay, scatter.step, scatter.last

    def grow(g):
        if g == 2:
            fetch[19].wait()
        which = 19 + g
        fetch[which].wait()
        weight_grad(sources[g], normed_mlp, operands[which], stage, stage_sems)

    def start_sum(n):
        if n:
            fetch[(None, 1, 16)[n]].wait()
        (first, second, third)[n].start()

    if nz == 4:
        plan = [
            (start, 0), (start_sum, 0), (grow, 2), (start, 2), (step, 0, 0), (grow, 1),
            (step, 0, 1), (residual_back,),
            (step, 0, 2), (low_rows_in,), (heads_back,), (start, 3), (start, 1), (deltas,),
            (step, 2, 0), (attend_back, 0), (start_sum, 1), (step, 2, 1), (attend_back, 1),
            (attend_back, 2), (step, 3, 0), (step, 3, 1), (keys_pass, 2), (step, 2, 2),
            (attend_back, 3), (keys_final,), (layer_rows,), (qkv_back,), (start, 4),
            (step, 1, 0), (step, 3, 2), (step, 1, 1), (relay, 0), (start_sum, 2), (step, 1, 2),
            (step, 4, 0), (step, 4, 1), (input_back,), (last, 2), (step, 4, 2), (last, 0),
            (last, 1), (last, 3), (gains_in,), (last, 4),
        ]
    else:
        plan = [(start, 0), (start_sum, 0), (grow, 2), (start, 2), (grow, 1), (start, 1)]
        plan += [(residual_back,)]
        plan += [(low_rows_in,), (heads_back,), (start, 3), (deltas,)]
        plan += [(attend_back, place) for place in range(nz)]
        plan += [(keys_pass, place) for place in range(nz // 2, nz - 1) if nz <= 4]
        plan += [(start_sum, 1), (keys_final,), (layer_rows,), (qkv_back,), (start, 4)]
        plan += [(relay, g) for g in RELAYED] + [(start_sum, 2)]
        plan += [(step, g, place) for g in range(4) for place in range(nz - 1)]
        plan += [(input_back,), (gains_in,)] + [(step, 4, place) for place in range(nz - 1)]
        plan += [(last, g) for g in range(5)]
    for run, *which in plan:
        run(*which)
    remote(gains.at[1 - y], gains.at[1 - y], ts.at[0], tr.at[0], {"fy": 1 - y}).wait_recv()
    for g in range(5):
        scatter.finish(g)
    core_gain.wait_send()
    gain_line.wait_send()
    swap.wait_send()
    for t in range(nz):

        @pl.when(z != t)
        def _(t=t):
            gain_to(t).wait_send()

    for place in range(max(0, nz - slots), final):
        keys_sent(place)


def backward(down_grad, operands, ny, nz):
    dma = pltpu.SemaphoreType.DMA
    anywhere = pl.BlockSpec(memory_space=pl.ANY)
    vmem = pl.BlockSpec(memory_space=pltpu.VMEM)
    residual = operands[2]
    span, width = residual.shape
    chunk = width // 4
    block = down_grad.shape[3]
    half = 4 * DH
    wide = [down_grad.shape[4]] * 3 + [half, 2 * half]
    shape = jax.ShapeDtypeStruct
    out_shape = (
        [shape((span, width), BF16)] * 2
        + [shape((2, block, w), F32) for w in wide]
        + [shape((ny, 2, nz, 2, width), F32)]
        + [shape(down_grad.shape, BF16)] * 2
    )

    def bufs(lead, dtype=BF16):
        return [pltpu.VMEM(lead + (block, w), dtype) for w in wide]

    return pl.pallas_call(
        functools.partial(backward_kernel, nz, DH ** (-0.5)),
        out_shape=out_shape,
        in_specs=[anywhere] + [anywhere if n in (12, *LATER) else vmem for n in range(22)],
        out_specs=[vmem] * 2 + [anywhere] * 8,
        scratch_shapes=[pltpu.VMEM(operands[n].shape, operands[n].dtype) for n in LATER]
        + bufs((2, 2))[:3]
        + bufs((nz, 2))
        + bufs((nz - 1, 2))
        + bufs((2,), F32)
        + [pltpu.VMEM((block, wide[g]), BF16) for g in RELAYED * 2]
        + [
            pltpu.VMEM((ny, 2, nz, block, half), BF16),
            pltpu.VMEM((ny, 2, nz, block, 2 * half), BF16),
            pltpu.VMEM((4, span, chunk), BF16),
            pltpu.VMEM((2, 4, span, chunk), BF16),
            pltpu.VMEM((4, span, chunk), BF16),
            pltpu.VMEM((2, 4, span, chunk), BF16),
            pltpu.VMEM((span, width), F32),
            pltpu.VMEM((2, span, width), BF16),
            pltpu.VMEM((4, 2 * span, LANES), BF16),
            pltpu.VMEM((4, 2 * span, LANES), F32),
            pltpu.VMEM((4, 2 * span, LANES), F32),
            pltpu.VMEM((min(nz, 4), 2, span, half), BF16),
            pltpu.VMEM((nz, 2, span, half), BF16),
            pltpu.VMEM((2, span, 2 * half), BF16),
            pltpu.VMEM((2, width), F32),
            pltpu.VMEM((2, 2, span, half), BF16),
        ]
        + [dma((5, 5))]
        + [dma((5, nz + 1))] * 2
        + [dma((5,))] * 2
        + [dma((5, nz))] * 2
        + [dma((5,))] * 2
        + [dma((3, 4))] * 4
        + [dma((1,))] * 2
        + [dma((2, nz))] * 2
        + [dma((nz,))] * 2
        + [dma((3,)), dma((2,)), dma((2,))]
        + [pltpu.VMEM((2,) + down_grad.shape[2:], BF16), dma((2,)), dma((len(LATER),))],
        name="backward",
        compiler_params=pltpu.CompilerParams(
            collective_id=2, has_side_effects=True, vmem_limit_bytes=VMEM_LIMIT
        ),
    )(down_grad, *operands)


def join(halved):
    return jnp.concatenate([halved[0], halved[1]], axis=1)


def on_device(
    ny,
    nz,
    layer_input,
    segments,
    positions,
    attn_gain,
    query_proj,
    key_proj,
    value_proj,
    out_proj,
    mlp_gain,
    gate_proj,
    up_proj,
    down_proj,
    out_grad,
):
    _, span, width = layer_input.shape
    block = query_proj.shape[0]
    rows_per = span // LANES
    small = jnp.concatenate(
        [
            jnp.pad(attn_gain.astype(F32), (0, LANES - block))[None],
            jnp.pad(mlp_gain.astype(F32), (0, LANES - block))[None],
            segments.astype(F32).reshape(rows_per, LANES),
            jnp.zeros((6 - rows_per, LANES), F32),
        ]
    )
    lane = jnp.arange(LANES)[None]
    info = jnp.where(
        lane == 0, positions.reshape(span, 1).astype(F32), segments.reshape(span, 1).astype(F32)
    )
    freq_index = (lane % (LANES // 2)).astype(F32)
    freq = THETA ** (-2.0 * freq_index / DH)
    kv_half = key_proj.shape[1] // 2
    kv_proj = jnp.concatenate(
        [
            key_proj[:, :kv_half],
            value_proj[:, :kv_half],
            key_proj[:, kv_half:],
            value_proj[:, kv_half:],
        ],
        axis=1,
    )
    lane_from = jnp.arange(4 * DH)
    lane_to = lane_from // DH * LANES + lane_from % DH
    lane_to = jnp.where(lane_from % DH < DH // 2, lane_to, lane_to + LANES // 2 - DH // 2)
    spread_mat = (lane_to[:, None] == jnp.arange(4 * LANES)[None]).astype(BF16)
    rows = layer_input.reshape(span, width)
    upstream = out_grad.reshape(span, width)
    (
        w_qkv, w_out, q_items, kv_all, mixed_wide, mixed_low, row_lse, residual, normed_attn, dx_part,
        out_part, normed_mlp, gate_grad, up_grad, down_grad, cos_wide, sin_wide, q_seg, k_seg, full_gains,
    ) = forward(
        (query_proj, kv_proj, out_proj.T, gate_proj, up_proj, down_proj.T),
        rows, upstream, small, info, freq, spread_mat, ny, nz,
    )
    operands = (
        dx_part, out_part, residual, rows, upstream, full_gains, cos_wide, sin_wide, q_seg, k_seg,
        spread_mat, q_items, kv_all, mixed_wide, mixed_low, row_lse, w_qkv, w_out,
        normed_attn, normed_mlp, gate_grad, up_grad,
    )
    layer_output, input_grad, down_g, gate_g, up_g, out_g, qkv_g, gains_all, *_ = backward(
        down_grad, operands, ny, nz
    )
    gain_sum = jnp.sum(gains_all, axis=(0, 1, 2))
    y = lax.axis_index("fy")
    c = lax.axis_index("pr")
    z = lax.axis_index("ctx")
    place = ((y * 2 + c) * nz + z) * block
    gain_own = lax.dynamic_slice_in_dim(gain_sum, place, block, 1)
    q_width, kv_width = 4 * DH, 2 * DH
    return (
        layer_output.reshape(1, span, width),
        input_grad.reshape(1, span, width),
        gain_own[0],
        join(qkv_g[:, :, :q_width]),
        join(qkv_g[:, :, q_width : q_width + kv_width]),
        join(qkv_g[:, :, q_width + kv_width :]),
        join(out_g).T,
        gain_own[1],
        join(gate_g),
        join(up_g),
        join(down_g).T,
    )


def solution(mesh):
    sizes = mesh.shape
    ny, nz = sizes["fsdp"] // 2, sizes["ctx"]
    inner = Mesh(
        mesh.devices.reshape(ny, 2, nz, sizes["tp"]), ("fy", "pr", "ctx", "tp")
    )
    seqs = ("fy", "pr")
    rows = P(seqs, "ctx", None)
    marks = P(seqs, "ctx")
    gain = P(GROUP)
    tall = P(GROUP, "tp")
    wide = P("tp", GROUP)
    return jax.shard_map(
        functools.partial(on_device, ny, nz),
        mesh=inner,
        in_specs=(
            rows, marks, marks, gain, tall, tall, tall, wide, gain, tall, tall, wide, rows,
        ),
        out_specs=(rows, rows, gain, tall, tall, tall, wide, gain, tall, tall, wide),
        check_vma=False,
    )
```

time: 434 us -> 343 us (0.79)
  the two profiles are of different devices: /device:TPU:25 before, /device:TPU:11 now
where the time goes in v4:
time: 343 us; the launch traced here: 337 us
  Pallas kernels  319 us (93%)
  other arithmetic  11.5 us (3%)
  local copies, waits for them, and re-layouts  5.31 us (2%)
    pallas_call x1, Pallas kernels, forward(): pl.pallas_call(functools.partial(forward_kernel, nz, items, DH ** (-0.5))...  161 us
    pallas_call x1, Pallas kernels, backward(): pl.pallas_call(functools.partial(backward_kernel, nz, DH ** (-0.5)), out_...  158 us

profile of v4, /device:TPU:11, one launch (start us, length us, event | category | flops | bytes accessed | tf_op | source)
XLA Modules:
  0.0 336.8 jit_solution(9440997353525327948)
XLA Ops:
  0.6 1.0 fusion.13
  1.6 0.8 pad_maximum_fusion.3.refs_1_
  2.4 0.7 bitcast_convert_fusion
  3.1 0.7 convert_element_type.44
  3.8 0.1 pad.28.clone
  3.8 0.7 maximum_maximum_fusion.refs_8_
  4.5 0.9 fusion.refs_11_
  5.4 0.7 convert_element_type.45
  6.1 0.8 broadcast_select_fusion.refs_9_
  6.9 0.5 fusion.12.refs_10_
  7.4 161.1 %forward.1 = (bf16[2,2,4,96,768]{4,3,2,1,0:T(8,128)(2,1)}, bf16[2,2,4,96,384]{4,3,2,1,0:T(8,128)(2,1)}, bf16[4,512,128]{2,1,0:T(8,128)(2,1)}, bf16[4,2,256,384]{...) custom-call(bf16[96,768]{1,0:T(8,128)(2,1)} %refs_0_.1, ...), custom_call_target="tpu_custom_call" | custom-call | tf_op jit(solution)/shard_map/forward/pallas_call | solution.py:710
  168.5 158.1 %backward.1 = (bf16[256,1536]{1,0:T(8,128)(2,1)}, bf16[256,1536]{1,0:T(8,128)(2,1)}, f32[2,96,1024]{2,1,0:T(8,128)}, f32[2,96,1024]{2,1,0:T(8,128)}, f32[2,96,10...) custom-call(bf16[2,2,4,96,1024]{4,3,2,1,0:T(8,128)(2,1)} %get-tuple-, ...), custom_call_target="tpu_custom_call" | custom-call | tf_op jit(solution)/shard_map/backward/pallas_call | solution.py:1337
  326.6 0.0 copy-start.4
  326.6 1.3 slice_bitcast_fusion.1
  327.8 0.9 maximum_bitcast_fusion
  328.8 0.0 copy-done.4
  328.8 0.0 copy-start.3
  328.8 0.1 slice_bitcast_fusion.3
  328.8 0.9 pad_maximum_fusion.1
  329.8 0.3 copy-done.3
  330.1 0.0 copy-start.5
  330.1 0.1 slice_bitcast_fusion.5
  330.2 0.0 copy-start
  330.2 0.9 pad_maximum_fusion
  331.1 0.0 copy-done.5
  331.2 0.0 copy-start.6
  331.2 0.7 maximum_bitcast_fusion.1
  331.9 0.0 copy-start.2
  331.9 0.0 copy-done
  331.9 0.1 slice_bitcast_fusion.11
  332.0 0.8 pad_maximum_fusion.5
  332.8 0.8 pad_maximum_fusion.4
  333.5 0.0 copy-start.1
  333.6 0.7 pad_maximum_fusion.2
  334.3 0.0 copy-done.6
  334.3 0.1 reduce_sum.9
  334.4 0.1 constant_dynamic-slice_fusion
  334.5 0.5 slice_bitcast_fusion.14
  335.0 0.0 copy-done.2
  335.0 0.9 copy.26
  335.9 0.0 copy-done.1
  335.9 0.9 copy.27
  (5 shorter events, 0.1 us)
Async XLA Ops:
  326.6 2.2 copy-start.4
  328.8 1.3 copy-start.3
  330.1 1.0 copy-start.5
  330.2 1.7 copy-start
  331.2 3.1 copy-start.6
  331.9 3.1 copy-start.2
  333.5 2.3 copy-start.1

commit v5 on v4

--- a/solution.py
+++ b/solution.py
@@ -2,6 +2,7 @@
 
 import jax
 import jax.numpy as jnp
+import numpy as np
 from jax import lax
 from jax.experimental import pallas as pl
 from jax.experimental.pallas import tpu as pltpu
@@ -218,22 +219,22 @@
 
 def forward_kernel(nz, items, scale, *refs):
     weights = refs[:6]
-    rows, upstream, small, info, freq, spread_mat = refs[6:12]
-    stored = refs[12:26]
-    down_grad = refs[26]
-    cos, sin, q_seg, k_seg, gains = refs[27:32]
-    made = refs[32:46]
+    rows, upstream, segments, positions, attn_gain, mlp_gain, freq = refs[6:13]
+    stored = refs[13:28]
+    down_grad = refs[28]
+    cos, sin, q_seg, k_seg, gains = refs[29:34]
+    made = refs[34:49]
     (
         w_qkv, w_out, q_out, kvu, mixed_out, mixed_low, lse_out, residual, normed, dx_part, out_part,
-        normed_mlp, gate_grad, up_grad,
+        normed_mlp, gate_grad, up_grad, spread_mat,
     ) = made
     (
         w_gate, w_up, w_down, acc, keys, values, top, core_send, core_land, x_send, x_land, smalls, info_both,
-        rows_both, gate_pre, up_pre, upstream_both, hidden, stage,
-    ) = refs[46:65]
+        rows_both, gate_pre, up_pre, upstream_both, hidden, stage, small, info,
+    ) = refs[49:70]
     (
         loc, ps, pr, ws, wr, ts, tr, zs, zr, ys, yr, ks, kr, cs, cr, xs, xr, ns, nr, hs, gs,
-    ) = refs[65:]
+    ) = refs[70:]
 
     def store(n):
         return pltpu.make_async_copy(made[n], stored[n], hs.at[n])
@@ -254,6 +255,22 @@
 
     def columns(i):
         return pl.ds(pl.multiple_of(i * chunk, LANES), chunk)
+
+    small[...] = jnp.zeros_like(small)
+    small[0:1, :block] = attn_gain[...].astype(F32)
+    small[1:2, :block] = mlp_gain[...].astype(F32)
+    square = (LANES, LANES)
+    for part in range(span // LANES):
+        here = pl.ds(part * LANES, LANES)
+        segment = segments[:, here].astype(F32)
+        position = positions[:, here].astype(F32)
+        small[2 + part : 3 + part] = segment
+        lane = lax.broadcasted_iota(jnp.int32, square, 1)
+        info[here] = jnp.where(
+            lane == 0,
+            jnp.transpose(jnp.broadcast_to(position, square)),
+            jnp.transpose(jnp.broadcast_to(segment, square)),
+        )
 
     greet(
         [(other_y, None), (other_c, None), (other_x, None)]
@@ -333,6 +350,13 @@
         landed[n].wait_recv()
 
     def prepare():
+        row = lax.broadcasted_iota(jnp.int32, spread_mat.shape, 0)
+        column = lax.broadcasted_iota(jnp.int32, spread_mat.shape, 1)
+        head = sum((row >= k * DH).astype(jnp.int32) for k in range(1, 4))
+        row = row - head * DH
+        row = row + head * LANES + jnp.where(row >= DH // 2, LANES // 2 - DH // 2, 0)
+        spread_mat[...] = jnp.where(row == column, 1.0, 0.0).astype(BF16)
+        store(14).start()
         remote(smalls.at[1 - y, c], smalls.at[1 - y, c], ts.at[0], tr.at[0], other_y).wait_recv()
         small_plane.start()
         for n in (6, 7, 8):
@@ -661,7 +685,7 @@
             def _(b=b, offset=offset):
                 each_hop(offset, lambda level: keys_hop(b, offset, level).wait_send())
 
-    for n in range(14):
+    for n in range(15):
         store(n).wait()
     token_sum.drain()
     swap.wait_send()
@@ -673,7 +697,7 @@
         small_to(offset).wait_send()
 
 
-def forward(weights, rows, upstream, small, info, freq, spread_mat, ny, nz):
+def forward(weights, rows, upstream, segments, positions, attn_gain, mlp_gain, freq, ny, nz):
     dma = pltpu.SemaphoreType.DMA
     vmem = pl.BlockSpec(memory_space=pltpu.VMEM)
     span, width = rows.shape
@@ -698,6 +722,7 @@
         ((2, span, width), BF16),
         ((both, wide), BF16),
         ((both, wide), BF16),
+        ((half, 4 * LANES), BF16),
     ]
     out_shape = [shape(*each) for each in made] + [shape(weight + (wide,), BF16)]
     out_shape += [
@@ -710,8 +735,8 @@
     return pl.pallas_call(
         functools.partial(forward_kernel, nz, items, DH ** (-0.5)),
         out_shape=out_shape,
-        in_specs=[vmem] * 12,
-        out_specs=[anywhere] * 15 + [vmem] * 5,
+        in_specs=[vmem] * 13,
+        out_specs=[anywhere] * 16 + [vmem] * 5,
         scratch_shapes=[pltpu.VMEM(*each) for each in made]
         + [pltpu.VMEM(weight + (wide,), BF16)] * 3
         + [
@@ -723,7 +748,7 @@
             pltpu.VMEM((1, 4, span, chunk), BF16),
             pltpu.VMEM((4, span, chunk), BF16),
             pltpu.VMEM((1, 4, span, chunk), BF16),
-            pltpu.VMEM((ny, 2, nz) + small.shape, F32),
+            pltpu.VMEM((ny, 2, nz, 8, LANES), F32),
             pltpu.VMEM((2, span, LANES), F32),
             pltpu.VMEM((2, span, width), BF16),
             pltpu.VMEM((both, wide), F32),
@@ -731,18 +756,20 @@
             pltpu.VMEM((2, span, width), BF16),
             pltpu.VMEM((both, wide), BF16),
             pltpu.VMEM((2, nz, block, wide), BF16),
+            pltpu.VMEM((8, LANES), F32),
+            pltpu.VMEM((span, LANES), F32),
         ]
         + [dma((10,)), dma((9,)), dma((9,)), dma((nz,)), dma((nz,)), dma((2,)), dma((2,))]
         + [dma((5, nz))] * 4
         + [dma((2, nz))] * 2
         + [dma((1, 4))] * 4
         + [dma((1,))] * 2
-        + [dma((14,)), dma((2,))],
+        + [dma((15,)), dma((2,))],
         name="forward",
         compiler_params=pltpu.CompilerParams(
             collective_id=1, has_side_effects=True, vmem_limit_bytes=VMEM_LIMIT
         ),
-    )(*weights, rows, upstream, small, info, freq, spread_mat)
+    )(*weights, rows, upstream, segments, positions, attn_gain, mlp_gain, freq)
 
 
 RELAYED = (0,)
@@ -1381,10 +1408,6 @@
     )(down_grad, *operands)
 
 
-def join(halved):
-    return jnp.concatenate([halved[0], halved[1]], axis=1)
-
-
 def on_device(
     ny,
     nz,
@@ -1404,21 +1427,8 @@
 ):
     _, span, width = layer_input.shape
     block = query_proj.shape[0]
-    rows_per = span // LANES
-    small = jnp.concatenate(
-        [
-            jnp.pad(attn_gain.astype(F32), (0, LANES - block))[None],
-            jnp.pad(mlp_gain.astype(F32), (0, LANES - block))[None],
-            segments.astype(F32).reshape(rows_per, LANES),
-            jnp.zeros((6 - rows_per, LANES), F32),
-        ]
-    )
-    lane = jnp.arange(LANES)[None]
-    info = jnp.where(
-        lane == 0, positions.reshape(span, 1).astype(F32), segments.reshape(span, 1).astype(F32)
-    )
-    freq_index = (lane % (LANES // 2)).astype(F32)
-    freq = THETA ** (-2.0 * freq_index / DH)
+    freq_index = np.arange(LANES) % (LANES // 2)
+    freq = jnp.asarray((THETA ** (-2.0 * freq_index / DH)).astype(np.float32)[None])
     kv_half = key_proj.shape[1] // 2
     kv_proj = jnp.concatenate(
         [
@@ -1429,18 +1439,15 @@
         ],
         axis=1,
     )
-    lane_from = jnp.arange(4 * DH)
-    lane_to = lane_from // DH * LANES + lane_from % DH
-    lane_to = jnp.where(lane_from % DH < DH // 2, lane_to, lane_to + LANES // 2 - DH // 2)
-    spread_mat = (lane_to[:, None] == jnp.arange(4 * LANES)[None]).astype(BF16)
     rows = layer_input.reshape(span, width)
     upstream = out_grad.reshape(span, width)
     (
         w_qkv, w_out, q_items, kv_all, mixed_wide, mixed_low, row_lse, residual, normed_attn, dx_part,
-        out_part, normed_mlp, gate_grad, up_grad, down_grad, cos_wide, sin_wide, q_seg, k_seg, full_gains,
+        out_part, normed_mlp, gate_grad, up_grad, spread_mat, down_grad, cos_wide, sin_wide, q_seg, k_seg, full_gains,
     ) = forward(
         (query_proj, kv_proj, out_proj.T, gate_proj, up_proj, down_proj.T),
-        rows, upstream, small, info, freq, spread_mat, ny, nz,
+        rows, upstream, segments, positions, attn_gain.reshape(1, block), mlp_gain.reshape(1, block),
+        freq, ny, nz,
     )
     operands = (
         dx_part, out_part, residual, rows, upstream, full_gains, cos_wide, sin_wide, q_seg, k_seg,
@@ -1450,26 +1457,64 @@
     layer_output, input_grad, down_g, gate_g, up_g, out_g, qkv_g, gains_all, *_ = backward(
         down_grad, operands, ny, nz
     )
-    gain_sum = jnp.sum(gains_all, axis=(0, 1, 2))
-    y = lax.axis_index("fy")
-    c = lax.axis_index("pr")
-    z = lax.axis_index("ctx")
-    place = ((y * 2 + c) * nz + z) * block
-    gain_own = lax.dynamic_slice_in_dim(gain_sum, place, block, 1)
-    q_width, kv_width = 4 * DH, 2 * DH
+    layer_output, input_grad, q_g, k_g, v_g, o_g, gate_g, up_g, down_g, attn_g, mlp_g = assemble(
+        down_g, gate_g, up_g, out_g, qkv_g, gains_all, layer_output, input_grad, nz
+    )
     return (
         layer_output.reshape(1, span, width),
         input_grad.reshape(1, span, width),
-        gain_own[0],
-        join(qkv_g[:, :, :q_width]),
-        join(qkv_g[:, :, q_width : q_width + kv_width]),
-        join(qkv_g[:, :, q_width + kv_width :]),
-        join(out_g).T,
-        gain_own[1],
-        join(gate_g),
-        join(up_g),
-        join(down_g).T,
+        attn_g.reshape(block),
+        q_g,
+        k_g,
+        v_g,
+        o_g.T,
+        mlp_g.reshape(block),
+        gate_g,
+        up_g,
+        down_g.T,
     )
+
+
+def assemble_kernel(nz, down, gate, up, out, qkv, gains, layer, back, *refs):
+    layer_out, back_out, q_out, k_out, v_out, o_out, gate_out, up_out, down_out, attn, mlp = refs
+    layer_out[...] = layer[...]
+    back_out[...] = back[...]
+    for halves, whole in ((gate, gate_out), (up, up_out), (down, down_out), (out, o_out)):
+        size = halves.shape[2]
+        whole[:, :size] = halves[0]
+        whole[:, size:] = halves[1]
+    size = q_out.shape[1] // 2
+    q_out[:, :size] = qkv[0, :, :size]
+    q_out[:, size:] = qkv[1, :, :size]
+    both = [qkv[which, :, size:] for which in range(2)]
+    k_out[...] = jnp.concatenate([part[:, : size // 2] for part in both], axis=1)
+    v_out[...] = jnp.concatenate([part[:, size // 2 :] for part in both], axis=1)
+    block, width = attn.shape[1], gains.shape[4]
+    total = gains[0, 0, 0]
+    for n in range(1, 4 * nz):
+        total = total + gains[n // (2 * nz), n // nz % 2, n % nz]
+    place = ((lax.axis_index("fy") * 2 + lax.axis_index("pr")) * nz + lax.axis_index("ctx")) * block
+    own = pltpu.roll(total, lax.rem(width - place, width), 1)
+    attn[...] = own[0:1, :block]
+    mlp[...] = own[1:2, :block]
+
+
+def assemble(down, gate, up, out, qkv, gains, layer, back, nz):
+    vmem = pl.BlockSpec(memory_space=pltpu.VMEM)
+    shape = jax.ShapeDtypeStruct
+    block = down.shape[1]
+    size = out.shape[2]
+    outs = [shape(layer.shape, BF16), shape(back.shape, BF16), shape((block, 2 * size), F32)]
+    outs += [shape((block, size), F32)] * 2 + [shape((block, 2 * size), F32)]
+    outs += [shape((block, 2 * down.shape[2]), F32)] * 3 + [shape((1, block), F32)] * 2
+    return pl.pallas_call(
+        functools.partial(assemble_kernel, nz),
+        out_shape=outs,
+        in_specs=[vmem] * 8,
+        out_specs=[vmem] * len(outs),
+        name="assemble",
+        compiler_params=pltpu.CompilerParams(vmem_limit_bytes=VMEM_LIMIT),
+    )(down, gate, up, out, qkv, gains, layer, back)
 
 
 def solution(mesh):

time: 343 us -> 332 us (0.968)
  other arithmetic: 11.5 us -> 0.77 us
  Pallas kernels: 319 us -> 324 us
  local copies, waits for them, and re-layouts: 5.31 us -> 0.97 us
    concatenate x6 -> x0, other arithmetic: 4.79 us -> none  [the longest x5 4.12 us: join(): return jnp.concatenate([halved[0], halved[1]], axis=1)]
    pallas_call x0 -> x1, Pallas kernels: none -> 4.77 us  [assemble(): pl.pallas_call(functools.partial(assemble_kernel, nz), out_shape=outs, in...]
where the time goes in v5:
time: 332 us; the launch traced here: 326 us
  Pallas kernels  324 us (98%)
    pallas_call x1, Pallas kernels, forward(): pl.pallas_call(functools.partial(forward_kernel, nz, items, DH ** (-0.5))...  161 us
    pallas_call x1, Pallas kernels, backward(): pl.pallas_call(functools.partial(backward_kernel, nz, DH ** (-0.5)), out_...  158 us

profile of v5, /device:TPU:11, one launch (start us, length us, event | category | flops | bytes accessed | tf_op | source)
XLA Modules:
  0.0 326.4 jit_solution(13200563308217129279)
XLA Ops:
  0.6 1.0 fusion
  1.6 0.8 pad_maximum_fusion.refs_1_
  2.4 161.1 %forward.1 = (bf16[2,2,4,96,768]{4,3,2,1,0:T(8,128)(2,1)}, bf16[2,2,4,96,384]{4,3,2,1,0:T(8,128)(2,1)}, bf16[4,512,128]{2,1,0:T(8,128)(2,1)}, bf16[4,2,256,384]{...) custom-call(bf16[96,768]{1,0:T(8,128)(2,1)} %refs_0_.1, ...), custom_call_target="tpu_custom_call" | custom-call | tf_op jit(solution)/shard_map/forward/pallas_call | solution.py:735
  163.5 158.1 %backward.1 = (bf16[256,1536]{1,0:T(8,128)(2,1)}, bf16[256,1536]{1,0:T(8,128)(2,1)}, f32[2,96,1024]{2,1,0:T(8,128)}, f32[2,96,1024]{2,1,0:T(8,128)}, f32[2,96,10...) custom-call(bf16[2,2,4,96,1024]{4,3,2,1,0:T(8,128)(2,1)} %get-tuple-, ...), custom_call_target="tpu_custom_call" | custom-call | tf_op jit(solution)/shard_map/backward/pallas_call | solution.py:1364
  321.7 4.8 %assemble.1 = (bf16[256,1536]{1,0:T(8,128)(2,1)}, bf16[256,1536]{1,0:T(8,128)(2,1)}, f32[96,768]{1,0:T(8,128)}, f32[96,384]{1,0:T(8,128)}, f32[96,384]{1,0:T(8,1...) custom-call(f32[2,96,1024]{2,1,0:T(8,128)} %get-tuple-element.72.dow, ...), custom_call_target="tpu_custom_call" | custom-call | tf_op jit(solution)/shard_map/assemble/pallas_call | solution.py:1510

commit v6 on v5

--- a/solution.py
+++ b/solution.py
@@ -218,23 +218,23 @@
 
 
 def forward_kernel(nz, items, scale, *refs):
-    weights = refs[:6]
-    rows, upstream, segments, positions, attn_gain, mlp_gain, freq = refs[6:13]
-    stored = refs[13:28]
-    down_grad = refs[28]
-    cos, sin, q_seg, k_seg, gains = refs[29:34]
-    made = refs[34:49]
+    query_w, key_w, value_w, *other_w = refs[:7]
+    rows, upstream, segments, positions, attn_gain, mlp_gain, freq = refs[7:14]
+    stored = refs[14:29]
+    down_grad = refs[29]
+    cos, sin, q_seg, k_seg, gains = refs[30:35]
+    made = refs[35:50]
     (
         w_qkv, w_out, q_out, kvu, mixed_out, mixed_low, lse_out, residual, normed, dx_part, out_part,
         normed_mlp, gate_grad, up_grad, spread_mat,
     ) = made
     (
         w_gate, w_up, w_down, acc, keys, values, top, core_send, core_land, x_send, x_land, smalls, info_both,
-        rows_both, gate_pre, up_pre, upstream_both, hidden, stage, small, info,
-    ) = refs[49:70]
+        rows_both, gate_pre, up_pre, upstream_both, hidden, stage, small, info, kv_w,
+    ) = refs[50:72]
     (
         loc, ps, pr, ws, wr, ts, tr, zs, zr, ys, yr, ks, kr, cs, cr, xs, xr, ns, nr, hs, gs,
-    ) = refs[70:]
+    ) = refs[72:]
 
     def store(n):
         return pltpu.make_async_copy(made[n], stored[n], hs.at[n])
@@ -255,6 +255,12 @@
 
     def columns(i):
         return pl.ds(pl.multiple_of(i * chunk, LANES), chunk)
+
+    weights = (query_w, kv_w, *other_w)
+    near = key_w.shape[1] // 2
+    kv_w[...] = jnp.concatenate(
+        [key_w[:, :near], value_w[:, :near], key_w[:, near:], value_w[:, near:]], axis=1
+    )
 
     small[...] = jnp.zeros_like(small)
     small[0:1, :block] = attn_gain[...].astype(F32)
@@ -653,14 +659,14 @@
     arrivals = gather.arrivals
     if nz == 4:
         plan = [
-            (own_y, 4), (own_y, 3), (step, 0, 2), (own_y, 1), (own_z, 1), (prepare,), (own_z, 2),
-            (step, 0, 1), (step, 0, 3), (step, 1, 2), (step, 1, 1), (own_z, 3), (step, 2, 2),
-            (step, 2, 1), (finish, 0), (project_heads,), (step, 3, 1), (step, 1, 3),
-            (step, 2, 3), (attend_own,), (keys_in, 2), (own_y, 2), (finish, 1), (own_z, 4),
-            (attend_at, 2), (keys_in, 1), (step, 3, 2), (attend_at, 1), (keys_in, 3),
-            (attend_at, 3), (close,), (step, 4, 2), (start_sum,), (step, 4, 1), (step, 3, 3),
-            (add_residual,), (finish, 2), (norm,), (step, 4, 3), (finish, 3), (swapped,),
-            (gate,), (up,), (hide,), (finish, 4), (grads,), (back_rows,),
+            (own_y, 3), (step, 0, 2), (step, 0, 1), (own_z, 1), (step, 0, 3), (step, 1, 2),
+            (own_z, 2), (own_y, 4), (prepare,), (own_y, 2), (finish, 0), (own_y, 1),
+            (project_heads,), (attend_own,), (step, 2, 1), (step, 1, 1), (step, 2, 2),
+            (keys_in, 2), (own_z, 3), (step, 1, 3), (keys_in, 1), (attend_at, 2), (attend_at, 1),
+            (step, 2, 3), (step, 3, 2), (keys_in, 3), (attend_at, 3), (step, 3, 1), (close,),
+            (finish, 1), (own_z, 4), (start_sum,), (finish, 2), (step, 3, 3), (step, 4, 2),
+            (add_residual,), (finish, 3), (step, 4, 1), (norm,), (swapped,), (gate,),
+            (step, 4, 3), (up,), (hide,), (finish, 4), (grads,), (back_rows,),
         ]
     else:
         plan = [(own_z, 1), (own_y, 1), (prepare,)]
@@ -701,7 +707,7 @@
     dma = pltpu.SemaphoreType.DMA
     vmem = pl.BlockSpec(memory_space=pltpu.VMEM)
     span, width = rows.shape
-    block, half, wide = weights[0].shape[0], weights[0].shape[1] // 2, weights[3].shape[1] // 2
+    block, half, wide = weights[0].shape[0], weights[0].shape[1] // 2, weights[4].shape[1] // 2
     items, q_rows, both = 4, 2 * span, 2 * span
     shape = jax.ShapeDtypeStruct
     chunk = width // 4
@@ -735,7 +741,7 @@
     return pl.pallas_call(
         functools.partial(forward_kernel, nz, items, DH ** (-0.5)),
         out_shape=out_shape,
-        in_specs=[vmem] * 13,
+        in_specs=[vmem] * 14,
         out_specs=[anywhere] * 16 + [vmem] * 5,
         scratch_shapes=[pltpu.VMEM(*each) for each in made]
         + [pltpu.VMEM(weight + (wide,), BF16)] * 3
@@ -758,6 +764,7 @@
             pltpu.VMEM((2, nz, block, wide), BF16),
             pltpu.VMEM((8, LANES), F32),
             pltpu.VMEM((span, LANES), F32),
+            pltpu.VMEM((block, 2 * half), BF16),
         ]
         + [dma((10,)), dma((9,)), dma((9,)), dma((nz,)), dma((nz,)), dma((2,)), dma((2,))]
         + [dma((5, nz))] * 4
@@ -1429,23 +1436,13 @@
     block = query_proj.shape[0]
     freq_index = np.arange(LANES) % (LANES // 2)
     freq = jnp.asarray((THETA ** (-2.0 * freq_index / DH)).astype(np.float32)[None])
-    kv_half = key_proj.shape[1] // 2
-    kv_proj = jnp.concatenate(
-        [
-            key_proj[:, :kv_half],
-            value_proj[:, :kv_half],
-            key_proj[:, kv_half:],
-            value_proj[:, kv_half:],
-        ],
-        axis=1,
-    )
     rows = layer_input.reshape(span, width)
     upstream = out_grad.reshape(span, width)
     (
         w_qkv, w_out, q_items, kv_all, mixed_wide, mixed_low, row_lse, residual, normed_attn, dx_part,
         out_part, normed_mlp, gate_grad, up_grad, spread_mat, down_grad, cos_wide, sin_wide, q_seg, k_seg, full_gains,
     ) = forward(
-        (query_proj, kv_proj, out_proj.T, gate_proj, up_proj, down_proj.T),
+        (query_proj, key_proj, value_proj, out_proj.T, gate_proj, up_proj, down_proj.T),
         rows, upstream, segments, positions, attn_gain.reshape(1, block), mlp_gain.reshape(1, block),
         freq, ny, nz,
     )

time: 332 us -> 329 us (level)
    pallas_call x1, Pallas kernels: 158 us -> 162 us  [backward(): pl.pallas_call(functools.partial(backward_kernel, nz, DH ** (-0.5)), out_...]
where the time goes in v6:
time: 329 us; the launch traced here: 326 us
  Pallas kernels  325 us (99%)
    pallas_call x1, Pallas kernels, backward(): pl.pallas_call(functools.partial(backward_kernel, nz, DH ** (-0.5)), out_...  162 us
    pallas_call x1, Pallas kernels, forward(): pl.pallas_call(functools.partial(forward_kernel, nz, items, DH ** (-0.5))...  159 us

profile of v6, /device:TPU:11, one launch (start us, length us, event | category | flops | bytes accessed | tf_op | source)
XLA Modules:
  0.0 326.1 jit_solution(15513634913689628077)
XLA Ops:
  0.6 158.8 %forward.1 = (bf16[2,2,4,96,768]{4,3,2,1,0:T(8,128)(2,1)}, bf16[2,2,4,96,384]{4,3,2,1,0:T(8,128)(2,1)}, bf16[4,512,128]{2,1,0:T(8,128)(2,1)}, bf16[4,2,256,384]{...) custom-call(bf16[96,768]{1,0:T(8,128)(2,1)} %refs_0_.1, ...), custom_call_target="tpu_custom_call" | custom-call | tf_op jit(solution)/shard_map/forward/pallas_call | solution.py:741
  159.4 161.9 %backward.1 = (bf16[256,1536]{1,0:T(8,128)(2,1)}, bf16[256,1536]{1,0:T(8,128)(2,1)}, f32[2,96,1024]{2,1,0:T(8,128)}, f32[2,96,1024]{2,1,0:T(8,128)}, f32[2,96,10...) custom-call(bf16[2,2,4,96,1024]{4,3,2,1,0:T(8,128)(2,1)} %get-tuple-, ...), custom_call_target="tpu_custom_call" | custom-call | tf_op jit(solution)/shard_map/backward/pallas_call | solution.py:1371
  321.4 4.8 %assemble.1 = (bf16[256,1536]{1,0:T(8,128)(2,1)}, bf16[256,1536]{1,0:T(8,128)(2,1)}, f32[96,768]{1,0:T(8,128)}, f32[96,384]{1,0:T(8,128)}, f32[96,384]{1,0:T(8,1...) custom-call(f32[2,96,1024]{2,1,0:T(8,128)} %get-tuple-element.72.dow, ...), custom_call_target="tpu_custom_call" | custom-call | tf_op jit(solution)/shard_map/assemble/pallas_call | solution.py:1507

commit v7 on v6

--- a/solution.py
+++ b/solution.py
@@ -331,18 +331,21 @@
         )
 
     small_here = pltpu.make_async_copy(small, smalls.at[y, c, z], loc.at[9])
+    for n in range(2):
+        sent[n].start()
+        local[n].start()
     small_here.start()
-    for n in range(3):
-        local[n].start()
-        sent[n].start()
     for offset in range(1, nz):
         small_to(offset).start()
+    local[2].start()
+    sent[2].start()
     for n in (6, 8, 3, 4, 5, 7):
         local[n].start()
         sent[n].start()
     for n in range(2):
         local[n].wait()
         landed[n].wait_recv()
+    gather.own_y(0)
     gather.own_z(0)
     small_here.wait()
     for offset in range(1, nz):
@@ -350,7 +353,6 @@
     small_line = remote(smalls.at[y, c], smalls.at[y, c], ts.at[0], tr.at[0], other_y)
     small_line.start()
     small_plane = remote(smalls.at[:, c], smalls.at[:, c], ts.at[1], tr.at[1], other_c)
-    gather.own_y(0)
     for n in (5, 4, 2, 3):
         local[n].wait()
         landed[n].wait_recv()
@@ -993,7 +995,7 @@
         + [({"ctx": t}, z != t) for t in range(nz)],
         2 + nz,
     )
-    for which in LATER:
+    for which in LATER[:3]:
         fetch[which].start()
     bufs = (core_send, core_land, x_send, x_land)
     sems = (cs, cr, xs, xr)
@@ -1329,7 +1331,10 @@
         plan += [(step, g, place) for g in range(4) for place in range(nz - 1)]
         plan += [(input_back,), (gains_in,)] + [(step, 4, place) for place in range(nz - 1)]
         plan += [(last, g) for g in range(5)]
-    for run, *which in plan:
+    plan[0][0](*plan[0][1:])
+    for which in LATER[3:]:
+        fetch[which].start()
+    for run, *which in plan[1:]:
         run(*which)
     remote(gains.at[1 - y], gains.at[1 - y], ts.at[0], tr.at[0], {"fy": 1 - y}).wait_recv()
     for g in range(5):

time: 329 us -> 329 us (level)
  no operation moved by 1% of the time
where the time goes in v7:
time: 329 us; the launch traced here: 326 us
  Pallas kernels  326 us (99%)
    pallas_call x1, Pallas kernels, backward(): pl.pallas_call(functools.partial(backward_kernel, nz, DH ** (-0.5)), out_...  164 us
    pallas_call x1, Pallas kernels, forward(): pl.pallas_call(functools.partial(forward_kernel, nz, items, DH ** (-0.5))...  157 us

profile of v7, /device:TPU:11, one launch (start us, length us, event | category | flops | bytes accessed | tf_op | source)
XLA Modules:
  0.0 326.2 jit_solution(14142106550242992854)
XLA Ops:
  0.6 156.9 %forward.1 = (bf16[2,2,4,96,768]{4,3,2,1,0:T(8,128)(2,1)}, bf16[2,2,4,96,384]{4,3,2,1,0:T(8,128)(2,1)}, bf16[4,512,128]{2,1,0:T(8,128)(2,1)}, bf16[4,2,256,384]{...) custom-call(bf16[96,768]{1,0:T(8,128)(2,1)} %refs_0_.1, ...), custom_call_target="tpu_custom_call" | custom-call | tf_op jit(solution)/shard_map/forward/pallas_call | solution.py:743
  157.6 163.9 %backward.1 = (bf16[256,1536]{1,0:T(8,128)(2,1)}, bf16[256,1536]{1,0:T(8,128)(2,1)}, f32[2,96,1024]{2,1,0:T(8,128)}, f32[2,96,1024]{2,1,0:T(8,128)}, f32[2,96,10...) custom-call(bf16[2,2,4,96,1024]{4,3,2,1,0:T(8,128)(2,1)} %get-tuple-, ...), custom_call_target="tpu_custom_call" | custom-call | tf_op jit(solution)/shard_map/backward/pallas_call | solution.py:1376
  321.4 4.8 %assemble.1 = (bf16[256,1536]{1,0:T(8,128)(2,1)}, bf16[256,1536]{1,0:T(8,128)(2,1)}, f32[96,768]{1,0:T(8,128)}, f32[96,384]{1,0:T(8,128)}, f32[96,384]{1,0:T(8,1...) custom-call(f32[2,96,1024]{2,1,0:T(8,128)} %get-tuple-element.72.dow, ...), custom_call_target="tpu_custom_call" | custom-call | tf_op jit(solution)/shard_map/assemble/pallas_call | solution.py:1512
